TPU v7x, 32 devices: a whole 2x2x4 slice. The times are simulated.
32 devices in a mesh: narrow: 4 (over z), wide: 8 (over y, x, core).
Axes of the slice: x: 2, y: 2, z: 4, core: 2. Of those that a mesh axis runs over, the one named last changes fastest.
Arguments:
- tokens: bfloat16 [12288, 640], P('wide'), may hold values from -6 to 6
- cotangent: bfloat16 [12288, 640], P('wide'), may hold values from -6 to 6
- seq_lens: int32 [8, 16], P('wide'), may hold values from 1 to 1024, 1536 in all within a row
- norm_gains: bfloat16 [2, 640], replicated, may hold values from 0.099609375 to 1.8984375
- norm_shifts: bfloat16 [2, 640], replicated, may hold values from -3 to 3
- w_qkv: bfloat16 [3, 640, 640], P(None, 'wide', 'narrow'), may hold values from -0.25 to 0.25
- w_attn_out: bfloat16 [640, 640], P('narrow', 'wide'), may hold values from -2 to 2
- w_ffn_in: bfloat16 [640, 5120], P('narrow', 'wide'), may hold values from -0.25 to 0.25
- w_ffn_down: bfloat16 [640, 5120], P('narrow', 'wide'), may hold values from -0.078125 to 0.078125
Outputs:
- layer_out: bfloat16 [12288, 640], P('wide')
- input_grad: bfloat16 [12288, 640], P('wide')
- grad_norm_gains: float32 [2, 640], P(None, 'wide')
- grad_norm_shifts: float32 [2, 640], P(None, 'wide')
- grad_qkv: float32 [3, 640, 640], P(None, 'wide', 'narrow')
- grad_attn_out: float32 [640, 640], P('narrow', 'wide')
- grad_ffn_in: float32 [640, 5120], P('narrow', 'wide')
- grad_ffn_down: float32 [640, 5120], P('narrow', 'wide')
Inputs may be any that keep to these rules, and one draw needn't show every extreme that they name: `seq_lens`: each row lists the lengths of the 16 sequences packed end to end in that index's 1536 slots; a row sums to 1536 and its largest entry is exactly 1024.
All inputs are finite; a program needn't handle non-finite values.
Results may differ from a plain program's by a relative error of at most 0.015.
Values may be sent and summed in bfloat16 or wider, within the bound.
No kernel may reach another device: no remote copies, remote signals or barrier semaphores. Data moves between devices by JAX's collectives and lax.ppermute only.
A program may use at most 128 MiB of HBM per device.

v0:
```python
from functools import partial

import jax
import jax.numpy as jnp
from jax import lax
from jax.sharding import PartitionSpec as P

HD = 32
QBLK = 512
FBLK = 128


EPS = 1e-05


def layer_norm(rows, gain, shift):
    center = rows - jnp.mean(rows, axis=-1, keepdims=True)
    spread = jnp.mean(center * center, axis=-1, keepdims=True)
    return center * lax.rsqrt(spread + EPS) * gain + shift


def segment_ids(lengths, count):
    ends = jnp.cumsum(lengths, dtype=jnp.int32)
    position = jnp.arange(count, dtype=jnp.int32)
    return jnp.sum((position[:, None] >= ends[None, :]).astype(jnp.int32), axis=1)


def block_scores(q_block, keys, seg_block, segment):
    scores = jnp.einsum("qd,kd->qk", q_block, keys, preferred_element_type=jnp.float32) * HD ** (
        -0.5
    )
    return jnp.where(seg_block[:, None] == segment[None, :], scores, -1e30)


def attend_forward(query, key, value, segment):
    count, width = query.shape
    starts = jnp.arange(count // QBLK, dtype=jnp.int32) * QBLK

    def one_head(head):
        q_head = lax.dynamic_slice_in_dim(query, head * HD, HD, 1)
        k_head = lax.dynamic_slice_in_dim(key, head * HD, HD, 1)
        v_head = lax.dynamic_slice_in_dim(value, head * HD, HD, 1)

        def one_block(start):
            q_block = lax.dynamic_slice_in_dim(q_head, start, QBLK, 0)
            seg_block = lax.dynamic_slice_in_dim(segment, start, QBLK, 0)
            scores = block_scores(q_block, k_head, seg_block, segment)
            top = jnp.max(scores, axis=1, keepdims=True)
            expd = jnp.exp(scores - top)
            total = jnp.sum(expd, axis=1, keepdims=True)
            weights = (expd / total).astype(jnp.bfloat16)
            result = jnp.dot(weights, v_head, preferred_element_type=jnp.float32)
            return (result, (top + jnp.log(total))[:, 0])

        results, logsum = lax.map(one_block, starts)
        return (results.reshape(count, HD), logsum.reshape(count))

    results, logsum = lax.map(one_head, jnp.arange(width // HD, dtype=jnp.int32))
    return (results.transpose(1, 0, 2).reshape(count, width), logsum)


def attend_backward(query, key, value, dattended, logsum, segment):
    count, width = query.shape
    starts = jnp.arange(count // QBLK, dtype=jnp.int32) * QBLK
    scale = HD ** (-0.5)

    def one_head(head):
        q_head = lax.dynamic_slice_in_dim(query, head * HD, HD, 1)
        k_head = lax.dynamic_slice_in_dim(key, head * HD, HD, 1)
        v_head = lax.dynamic_slice_in_dim(value, head * HD, HD, 1)
        d_head = lax.dynamic_slice_in_dim(dattended, head * HD, HD, 1)
        log_head = logsum[head]

        def one_block(carry, start):
            dkey, dvalue = carry
            q_block = lax.dynamic_slice_in_dim(q_head, start, QBLK, 0)
            d_block = lax.dynamic_slice_in_dim(d_head, start, QBLK, 0)
            seg_block = lax.dynamic_slice_in_dim(segment, start, QBLK, 0)
            log_block = lax.dynamic_slice_in_dim(log_head, start, QBLK, 0)
            scores = block_scores(q_block, k_head, seg_block, segment)
            prob = jnp.exp(scores - log_block[:, None])
            dprob = jnp.einsum("qd,kd->qk", d_block, v_head, preferred_element_type=jnp.float32)
            delta = jnp.sum(prob * dprob, axis=1, keepdims=True)
            dscore = (prob * (dprob - delta)).astype(jnp.bfloat16)
            dquery = jnp.dot(dscore, k_head, preferred_element_type=jnp.float32) * scale
            dkey = (
                dkey
                + jnp.einsum("qk,qd->kd", dscore, q_block, preferred_element_type=jnp.float32)
                * scale
            )
            dvalue = dvalue + jnp.einsum(
                "qk,qd->kd", prob.astype(jnp.bfloat16), d_block, preferred_element_type=jnp.float32
            )
            return ((dkey, dvalue), dquery)

        zeros = jnp.zeros((count, HD), jnp.float32)
        (dkey, dvalue), dquery = lax.scan(one_block, (zeros, zeros), starts)
        return (dquery.reshape(count, HD), dkey, dvalue)

    dquery, dkey, dvalue = lax.map(one_head, jnp.arange(width // HD, dtype=jnp.int32))

    def joined(arr):
        return arr.transpose(1, 0, 2).reshape(count, width)

    return (joined(dquery), joined(dkey), joined(dvalue))


def hidden_block(normed_mine, ffn_in_full, start):
    x_block = lax.dynamic_slice_in_dim(normed_mine, start, FBLK, 0)
    share = lax.psum_scatter(
        jnp.dot(x_block, ffn_in_full, preferred_element_type=jnp.float32),
        "narrow",
        scatter_dimension=0,
        tiled=True,
    )
    act_share = jax.nn.gelu(share, approximate=False).astype(jnp.bfloat16)
    act_rows = lax.all_gather(act_share, "narrow", axis=0, tiled=True)
    return (x_block, share, act_rows)


def local(
    tokens, cotangent, seq_lens, norm_gains, norm_shifts, w_qkv, w_attn_out, w_ffn_in, w_ffn_down
):
    count = tokens.shape[0]
    width = w_attn_out.shape[0]
    first_col = lax.axis_index("narrow") * width
    gains = norm_gains.astype(jnp.float32)
    shifts = norm_shifts.astype(jnp.float32)
    segment = segment_ids(seq_lens[0], count)
    resid = tokens.astype(jnp.float32)
    dy_full = cotangent.astype(jnp.float32)
    qkv_full, out_full = (
        lax.all_gather(w_qkv, "wide", axis=1, tiled=True),
        lax.all_gather(w_attn_out, "wide", axis=1, tiled=True),
    )
    normed_low = layer_norm(resid, gains[0], shifts[0]).astype(jnp.bfloat16)
    proj = jnp.einsum(
        "td,jde->jte", normed_low, qkv_full, preferred_element_type=jnp.float32
    ).astype(jnp.bfloat16)
    query, key, value = (proj[0], proj[1], proj[2])
    attended, logsum = attend_forward(query, key, value, segment)
    attended_low = attended.astype(jnp.bfloat16)
    mixed = jnp.dot(attended_low, out_full, preferred_element_type=jnp.float32)
    mixed_mine = lax.psum_scatter(mixed, "narrow", scatter_dimension=1, tiled=True)
    middle_mine = lax.dynamic_slice_in_dim(resid, first_col, width, 1) + mixed_mine
    middle = lax.all_gather(middle_mine, "narrow", axis=1, tiled=True)
    normed_two = layer_norm(middle, gains[1], shifts[1])
    ffn_in_part, ffn_down_part = (
        lax.all_gather(w_ffn_in, "wide", axis=1, tiled=True),
        lax.all_gather(w_ffn_down, "wide", axis=1, tiled=True),
    )
    dy_cols = lax.dynamic_slice_in_dim(cotangent, first_col, width, 1)
    normed_mine = lax.dynamic_slice_in_dim(normed_two, first_col, width, 1).astype(jnp.bfloat16)
    starts = jnp.arange(count // FBLK, dtype=jnp.int32) * FBLK

    def ffn_forward(carry, start):
        x_block, share, act_rows = hidden_block(normed_mine, ffn_in_part, start)
        result = lax.dot_general(
            act_rows, ffn_down_part, (((1,), (1,)), ((), ())), preferred_element_type=jnp.float32
        )
        return (carry, result)

    _, branch = lax.scan(ffn_forward, jnp.zeros((), jnp.float32), starts)
    branch_full = lax.all_gather(
        branch.reshape(count, width).astype(jnp.bfloat16), "narrow", axis=1, tiled=True
    ).astype(jnp.float32)
    layer_out = (middle + branch_full).astype(jnp.bfloat16)

    def ffn_backward(carry, start):
        grad_in, grad_down = carry
        x_block, share, act_rows = hidden_block(normed_mine, ffn_in_part, start)
        dy_block = lax.dynamic_slice_in_dim(dy_cols, start, FBLK, 0)
        dact = lax.psum_scatter(
            jnp.dot(dy_block, ffn_down_part, preferred_element_type=jnp.float32),
            "narrow",
            scatter_dimension=0,
            tiled=True,
        )
        _, gelu_back = jax.vjp(partial(jax.nn.gelu, approximate=False), share)
        dshare = gelu_back(dact)[0].astype(jnp.bfloat16)
        drows = lax.all_gather(dshare, "narrow", axis=0, tiled=True)
        grad_in = grad_in + lax.dot_general(
            x_block, drows, (((0,), (0,)), ((), ())), preferred_element_type=jnp.float32
        )
        grad_down = grad_down + lax.dot_general(
            dy_block, act_rows, (((0,), (0,)), ((), ())), preferred_element_type=jnp.float32
        )
        dnormed = lax.dot_general(
            drows, ffn_in_part, (((1,), (1,)), ((), ())), preferred_element_type=jnp.float32
        )
        return ((grad_in, grad_down), dnormed)

    empty = jnp.zeros(ffn_in_part.shape, jnp.float32)
    (grad_in, grad_down), dnormed = lax.scan(ffn_backward, (empty, empty), starts)
    dnormed_two = lax.all_gather(dnormed.reshape(count, width), "narrow", axis=1, tiled=True)
    grad_in_out, grad_down_out = (
        lax.psum_scatter(grad_in, "wide", scatter_dimension=1, tiled=True),
        lax.psum_scatter(grad_down, "wide", scatter_dimension=1, tiled=True),
    )
    _, norm_back_two = jax.vjp(layer_norm, middle, gains[1], shifts[1])
    dmiddle, dgain_two, dshift_two = norm_back_two(dnormed_two)
    dmiddle = dmiddle + dy_full
    dmixed_low = dmiddle.astype(jnp.bfloat16)
    grad_out = lax.dot_general(
        attended_low, dmixed_low, (((0,), (0,)), ((), ())), preferred_element_type=jnp.float32
    )
    dattended = lax.dot_general(
        dmixed_low, out_full, (((1,), (1,)), ((), ())), preferred_element_type=jnp.float32
    ).astype(jnp.bfloat16)
    dquery, dkey, dvalue = attend_backward(query, key, value, dattended, logsum, segment)
    dproj = jnp.stack([dquery, dkey, dvalue]).astype(jnp.bfloat16)
    grad_proj = jnp.einsum("td,jte->jde", normed_low, dproj, preferred_element_type=jnp.float32)
    dnormed_part = jnp.einsum("jte,jde->td", dproj, qkv_full, preferred_element_type=jnp.float32)
    dnormed_one = lax.psum(dnormed_part.astype(jnp.bfloat16), "narrow").astype(jnp.float32)
    _, norm_back_one = jax.vjp(layer_norm, resid, gains[0], shifts[0])
    dresid, dgain_one, dshift_one = norm_back_one(dnormed_one)
    input_grad = (dmiddle + dresid).astype(jnp.bfloat16)
    dgains = jnp.stack([dgain_one, dgain_two])
    dshifts = jnp.stack([dshift_one, dshift_two])
    gain_out, shift_out, proj_out, attn_out = (
        lax.psum_scatter(dgains, "wide", scatter_dimension=1, tiled=True),
        lax.psum_scatter(dshifts, "wide", scatter_dimension=1, tiled=True),
        lax.psum_scatter(grad_proj, "wide", scatter_dimension=1, tiled=True),
        lax.psum_scatter(grad_out, "wide", scatter_dimension=1, tiled=True),
    )
    return (
        layer_out,
        input_grad,
        gain_out,
        shift_out,
        proj_out,
        attn_out,
        grad_in_out,
        grad_down_out,
    )


def solution(mesh):
    placed = (
        P("wide", None),
        P("wide", None),
        P("wide", None),
        P(),
        P(),
        P(None, "wide", "narrow"),
        P("narrow", "wide"),
        P("narrow", "wide"),
        P("narrow", "wide"),
    )
    return jax.shard_map(
        local,
        mesh=mesh,
        in_specs=placed,
        out_specs=(
            P("wide", None),
            P("wide", None),
            P(None, "wide"),
            P(None, "wide"),
            P(None, "wide", "narrow"),
            P("narrow", "wide"),
            P("narrow", "wide"),
            P("narrow", "wide"),
        ),
        check_vma=False,
    )
```

profile of v0, /device:TPU:0, one launch (start us, length us, event | category | flops | bytes accessed | tf_op | source)
XLA Modules:
  0.0 4609.3 jit_solution(13928919483076880924)
XLA Ops:
  36.1 182.4 %while.84 = (s32[]{:T(128)}, bf16[5,1536,32]{1,2,0:T(8,128)(2,1)}, f32[5,1536]{1,0:T(8,128)}, s32[5]{0:T(128)}, bf16[1536,160]{1,0:T(8,128)(2,1)}, /*index=5*/bf...) while((s32[]{:T(128)}, bf16[5,1536,32]{1,2,0:T(8,128)(2,1)}, ...), condition=%wide.region_9.10_spmd.clone, body=%wide.region_4.9_spmd.clone.sunk | while | flops 107740680 | bytes 11363814 | solution.py:58
  236.6 69.2 %reduce-scatter.19.cloned.1.call-done = f32[1536,160]{0,1:T(8,128)} async-done(((f32[1536,640]{0,1:T(8,128)}), f32[1536,160]{0,1:T(8,128)}) %reduce-scatter.19.cloned.1.call-update) | async-done | bytes 983056 | tf_op jit(solution)/shard_map/reduce_scatter | solution.py:144
  312.1 73.2 %all-gather.9.cloned.1.call-done = f32[1536,640]{0,1:T(8,128)} async-done(((f32[1536,160]{0,1:T(8,128)}), f32[1536,640]{0,1:T(8,128)}) %all-gather.9.cloned.1.call-update) | async-done | bytes 3932176 | tf_op jit(solution)/shard_map/all_gather | solution.py:146
  439.6 2218.3 %while.87 = (s32[]{:T(128)}, f32[160,5120]{1,0:T(8,128)}, f32[160,5120]{1,0:T(8,128)}, f32[12,128,160]{1,0,2:T(8,128)}, s32[12]{0:T(128)S(1)}, /*index=5*/bf16[1...) while((s32[]{:T(128)}, f32[160,5120]{1,0:T(8,128)}, ...), condition=%wide.region_19.20_spmd.clone, body=%wide.region_16.19_spmd.clone.sunk | while | flops 1064796160 | bytes 83411448 | solution.py:194
  501.3 50.8 %reduce-scatter.35.cloned.1.call-done = f32[32,5120]{1,0:T(8,128)} async-done(((f32[128,5120]{1,0:T(8,128)}), f32[32,5120]{1,0:T(8,128)}) %reduce-scatter.35.cloned.1.call-update) | async-done | bytes 655376 | tf_op jit(solution)/shard_map/while/body/eval_jaxpr/reduce_scatter | solution.py:173
  685.1 50.8 %reduce-scatter.35.cloned.1.call-done = f32[32,5120]{1,0:T(8,128)} async-done(((f32[128,5120]{1,0:T(8,128)}), f32[32,5120]{1,0:T(8,128)}) %reduce-scatter.35.cloned.1.call-update) | async-done | bytes 655376 | tf_op jit(solution)/shard_map/while/body/eval_jaxpr/reduce_scatter | solution.py:173
  869.9 50.8 %reduce-scatter.35.cloned.1.call-done = f32[32,5120]{1,0:T(8,128)} async-done(((f32[128,5120]{1,0:T(8,128)}), f32[32,5120]{1,0:T(8,128)}) %reduce-scatter.35.cloned.1.call-update) | async-done | bytes 655376 | tf_op jit(solution)/shard_map/while/body/eval_jaxpr/reduce_scatter | solution.py:173
  1054.6 50.8 %reduce-scatter.35.cloned.1.call-done = f32[32,5120]{1,0:T(8,128)} async-done(((f32[128,5120]{1,0:T(8,128)}), f32[32,5120]{1,0:T(8,128)}) %reduce-scatter.35.cloned.1.call-update) | async-done | bytes 655376 | tf_op jit(solution)/shard_map/while/body/eval_jaxpr/reduce_scatter | solution.py:173
  1239.3 50.9 %reduce-scatter.35.cloned.1.call-done = f32[32,5120]{1,0:T(8,128)} async-done(((f32[128,5120]{1,0:T(8,128)}), f32[32,5120]{1,0:T(8,128)}) %reduce-scatter.35.cloned.1.call-update) | async-done | bytes 655376 | tf_op jit(solution)/shard_map/while/body/eval_jaxpr/reduce_scatter | solution.py:173
  1424.2 50.8 %reduce-scatter.35.cloned.1.call-done = f32[32,5120]{1,0:T(8,128)} async-done(((f32[128,5120]{1,0:T(8,128)}), f32[32,5120]{1,0:T(8,128)}) %reduce-scatter.35.cloned.1.call-update) | async-done | bytes 655376 | tf_op jit(solution)/shard_map/while/body/eval_jaxpr/reduce_scatter | solution.py:173
  1793.9 50.9 %reduce-scatter.35.cloned.1.call-done = f32[32,5120]{1,0:T(8,128)} async-done(((f32[128,5120]{1,0:T(8,128)}), f32[32,5120]{1,0:T(8,128)}) %reduce-scatter.35.cloned.1.call-update) | async-done | bytes 655376 | tf_op jit(solution)/shard_map/while/body/eval_jaxpr/reduce_scatter | solution.py:173
  1978.8 50.9 %reduce-scatter.35.cloned.1.call-done = f32[32,5120]{1,0:T(8,128)} async-done(((f32[128,5120]{1,0:T(8,128)}), f32[32,5120]{1,0:T(8,128)}) %reduce-scatter.35.cloned.1.call-update) | async-done | bytes 655376 | tf_op jit(solution)/shard_map/while/body/eval_jaxpr/reduce_scatter | solution.py:173
  2163.8 50.9 %reduce-scatter.35.cloned.1.call-done = f32[32,5120]{1,0:T(8,128)} async-done(((f32[128,5120]{1,0:T(8,128)}), f32[32,5120]{1,0:T(8,128)}) %reduce-scatter.35.cloned.1.call-update) | async-done | bytes 655376 | tf_op jit(solution)/shard_map/while/body/eval_jaxpr/reduce_scatter | solution.py:173
  2348.9 50.8 %reduce-scatter.35.cloned.1.call-done = f32[32,5120]{1,0:T(8,128)} async-done(((f32[128,5120]{1,0:T(8,128)}), f32[32,5120]{1,0:T(8,128)}) %reduce-scatter.35.cloned.1.call-update) | async-done | bytes 655376 | tf_op jit(solution)/shard_map/while/body/eval_jaxpr/reduce_scatter | solution.py:173
  2533.6 50.9 %reduce-scatter.35.cloned.1.call-done = f32[32,5120]{1,0:T(8,128)} async-done(((f32[128,5120]{1,0:T(8,128)}), f32[32,5120]{1,0:T(8,128)}) %reduce-scatter.35.cloned.1.call-update) | async-done | bytes 655376 | tf_op jit(solution)/shard_map/while/body/eval_jaxpr/reduce_scatter | solution.py:173
  2660.5 1148.4 %while.82 = (s32[]{:T(128)}, bf16[12,128,160]{1,2,0:T(8,128)(2,1)}, s32[12]{0:T(128)S(1)}, bf16[1536,160]{1,0:T(8,128)(2,1)}, bf16[160,5120]{1,0:T(8,128)(2,1)},...) while((s32[]{:T(128)}, bf16[12,128,160]{1,2,0:T(8,128)(2,1)}, s32[12]{0:T(128)S(1)}, ...), condition=%wide.region_15.16_spmd, body=%wide.region_13.15_spmd.sunk | while | flops 430080000 | bytes 29638920 | solution.py:163
  2666.7 51.2 %reduce-scatter.33.cloned.1.call-done = f32[32,5120]{1,0:T(8,128)} async-done(((f32[128,5120]{1,0:T(8,128)}), f32[32,5120]{1,0:T(8,128)}) %reduce-scatter.33.cloned.1.call-update) | async-done | bytes 655376 | tf_op jit(solution)/shard_map/while/body/eval_jaxpr/reduce_scatter | solution.py:110
  2762.4 51.2 %reduce-scatter.33.cloned.1.call-done = f32[32,5120]{1,0:T(8,128)} async-done(((f32[128,5120]{1,0:T(8,128)}), f32[32,5120]{1,0:T(8,128)}) %reduce-scatter.33.cloned.1.call-update) | async-done | bytes 655376 | tf_op jit(solution)/shard_map/while/body/eval_jaxpr/reduce_scatter | solution.py:110
  2858.2 51.2 %reduce-scatter.33.cloned.1.call-done = f32[32,5120]{1,0:T(8,128)} async-done(((f32[128,5120]{1,0:T(8,128)}), f32[32,5120]{1,0:T(8,128)}) %reduce-scatter.33.cloned.1.call-update) | async-done | bytes 655376 | tf_op jit(solution)/shard_map/while/body/eval_jaxpr/reduce_scatter | solution.py:110
  2953.9 51.2 %reduce-scatter.33.cloned.1.call-done = f32[32,5120]{1,0:T(8,128)} async-done(((f32[128,5120]{1,0:T(8,128)}), f32[32,5120]{1,0:T(8,128)}) %reduce-scatter.33.cloned.1.call-update) | async-done | bytes 655376 | tf_op jit(solution)/shard_map/while/body/eval_jaxpr/reduce_scatter | solution.py:110
  3049.6 51.2 %reduce-scatter.33.cloned.1.call-done = f32[32,5120]{1,0:T(8,128)} async-done(((f32[128,5120]{1,0:T(8,128)}), f32[32,5120]{1,0:T(8,128)}) %reduce-scatter.33.cloned.1.call-update) | async-done | bytes 655376 | tf_op jit(solution)/shard_map/while/body/eval_jaxpr/reduce_scatter | solution.py:110
  3145.3 51.2 %reduce-scatter.33.cloned.1.call-done = f32[32,5120]{1,0:T(8,128)} async-done(((f32[128,5120]{1,0:T(8,128)}), f32[32,5120]{1,0:T(8,128)}) %reduce-scatter.33.cloned.1.call-update) | async-done | bytes 655376 | tf_op jit(solution)/shard_map/while/body/eval_jaxpr/reduce_scatter | solution.py:110
  3241.0 51.2 %reduce-scatter.33.cloned.1.call-done = f32[32,5120]{1,0:T(8,128)} async-done(((f32[128,5120]{1,0:T(8,128)}), f32[32,5120]{1,0:T(8,128)}) %reduce-scatter.33.cloned.1.call-update) | async-done | bytes 655376 | tf_op jit(solution)/shard_map/while/body/eval_jaxpr/reduce_scatter | solution.py:110
  3336.7 51.2 %reduce-scatter.33.cloned.1.call-done = f32[32,5120]{1,0:T(8,128)} async-done(((f32[128,5120]{1,0:T(8,128)}), f32[32,5120]{1,0:T(8,128)}) %reduce-scatter.33.cloned.1.call-update) | async-done | bytes 655376 | tf_op jit(solution)/shard_map/while/body/eval_jaxpr/reduce_scatter | solution.py:110
  3432.4 51.2 %reduce-scatter.33.cloned.1.call-done = f32[32,5120]{1,0:T(8,128)} async-done(((f32[128,5120]{1,0:T(8,128)}), f32[32,5120]{1,0:T(8,128)}) %reduce-scatter.33.cloned.1.call-update) | async-done | bytes 655376 | tf_op jit(solution)/shard_map/while/body/eval_jaxpr/reduce_scatter | solution.py:110
  3528.1 51.2 %reduce-scatter.33.cloned.1.call-done = f32[32,5120]{1,0:T(8,128)} async-done(((f32[128,5120]{1,0:T(8,128)}), f32[32,5120]{1,0:T(8,128)}) %reduce-scatter.33.cloned.1.call-update) | async-done | bytes 655376 | tf_op jit(solution)/shard_map/while/body/eval_jaxpr/reduce_scatter | solution.py:110
  3623.8 51.2 %reduce-scatter.33.cloned.1.call-done = f32[32,5120]{1,0:T(8,128)} async-done(((f32[128,5120]{1,0:T(8,128)}), f32[32,5120]{1,0:T(8,128)}) %reduce-scatter.33.cloned.1.call-update) | async-done | bytes 655376 | tf_op jit(solution)/shard_map/while/body/eval_jaxpr/reduce_scatter | solution.py:110
  3719.5 51.2 %reduce-scatter.33.cloned.1.call-done = f32[32,5120]{1,0:T(8,128)} async-done(((f32[128,5120]{1,0:T(8,128)}), f32[32,5120]{1,0:T(8,128)}) %reduce-scatter.33.cloned.1.call-update) | async-done | bytes 655376 | tf_op jit(solution)/shard_map/while/body/eval_jaxpr/reduce_scatter | solution.py:110
  3814.6 72.2 %all-gather.17.cloned.1.call-done = f32[1536,640]{0,1:T(8,128)} async-done(((f32[1536,160]{0,1:T(8,128)}), f32[1536,640]{0,1:T(8,128)}) %all-gather.17.cloned.1.call-update) | async-done | bytes 3932176 | tf_op jit(solution)/shard_map/all_gather | solution.py:195
  3942.7 319.0 %while.86 = (s32[]{:T(128)}, bf16[5,1536,32]{2,1,0:T(8,128)(2,1)}, bf16[5,1536,32]{1,2,0:T(8,128)(2,1)}, bf16[5,1536,32]{1,2,0:T(8,128)(2,1)}, s32[5]{0:T(128)},...) while((s32[]{:T(128)}, bf16[5,1536,32]{2,1,0:T(8,128)(2,1)}, ...), condition=%wide.region_26.27_spmd.clone, body=%wide.region_22.26_spmd.clone.sunk | while | flops 259784208 | bytes 27660404 | solution.py:100
  4281.8 67.5 %all-reduce.2.cloned.1.call-done = bf16[1536,640]{0,1:T(8,128)(2,1)} async-done(((bf16[1536,640]{0,1:T(8,128)(2,1)}), bf16[1536,640]{0,1:T(8,128)(2,1)}) %all-reduce.2.cloned.1.call-update) | async-done | bytes 1966096 | tf_op jit(solution)/shard_map/psum | solution.py:214
  4551.5 50.9 %reduce-scatter.23.cloned.1.call-done = f32[160,640]{1,0:T(8,128)} async-done(((f32[160,5120]{1,0:T(8,128)}), f32[160,640]{1,0:T(8,128)}) %reduce-scatter.23.cloned.1.call-update) | async-done | bytes 409616 | tf_op jit(solution)/shard_map/reduce_scatter | solution.py:198
  (1040 shorter events, 3340.1 us)
Async XLA Ops:
  7.2 298.6 %reduce-scatter.19.cloned.1.call-start = ((), (), s32[]{:S(2)}) async-start(), calls=%async_computation.10 | async-start | bytes 4915200 | tf_op jit(solution)/shard_map/reduce_scatter | solution.py:144
  232.6 152.7 %all-gather.9.cloned.1.call-start = ((), (), s32[]{:S(2)}) async-start(), calls=%async_computation.11 | async-start | bytes 4915200 | tf_op jit(solution)/shard_map/all_gather | solution.py:146
  309.1 130.5 %all-gather.13.cloned.1.call-start = ((), (), s32[]{:S(2)}) async-start(), calls=%async_computation.13 | async-start | bytes 1843200 | tf_op jit(solution)/shard_map/all_gather | solution.py:150
  445.8 106.3 %reduce-scatter.35.cloned.1.call-start = ((), (), s32[]{:S(2)}) async-start(), calls=%async_computation.25 | async-start | bytes 3276800 | tf_op jit(solution)/shard_map/while/body/eval_jaxpr/reduce_scatter | solution.py:173
  447.9 139.0 %all-gather.21.cloned.1.call-start = ((), (), s32[]{:S(2)}) async-start(), calls=%async_computation.27 | async-start | bytes 1638400 | tf_op jit(solution)/shard_map/while/body/eval_jaxpr/all_gather | solution.py:181
  632.8 138.0 %all-gather.21.cloned.1.call-start = ((), (), s32[]{:S(2)}) async-start(), calls=%async_computation.27 | async-start | bytes 1638400 | tf_op jit(solution)/shard_map/while/body/eval_jaxpr/all_gather | solution.py:181
  815.4 105.2 %reduce-scatter.35.cloned.1.call-start = ((), (), s32[]{:S(2)}) async-start(), calls=%async_computation.25 | async-start | bytes 3276800 | tf_op jit(solution)/shard_map/while/body/eval_jaxpr/reduce_scatter | solution.py:173
  817.5 138.0 %all-gather.21.cloned.1.call-start = ((), (), s32[]{:S(2)}) async-start(), calls=%async_computation.27 | async-start | bytes 1638400 | tf_op jit(solution)/shard_map/while/body/eval_jaxpr/all_gather | solution.py:181
  1002.3 138.0 %all-gather.21.cloned.1.call-start = ((), (), s32[]{:S(2)}) async-start(), calls=%async_computation.27 | async-start | bytes 1638400 | tf_op jit(solution)/shard_map/while/body/eval_jaxpr/all_gather | solution.py:181
  1184.9 105.4 %reduce-scatter.35.cloned.1.call-start = ((), (), s32[]{:S(2)}) async-start(), calls=%async_computation.25 | async-start | bytes 3276800 | tf_op jit(solution)/shard_map/while/body/eval_jaxpr/reduce_scatter | solution.py:173
  1187.0 138.1 %all-gather.21.cloned.1.call-start = ((), (), s32[]{:S(2)}) async-start(), calls=%async_computation.27 | async-start | bytes 1638400 | tf_op jit(solution)/shard_map/while/body/eval_jaxpr/all_gather | solution.py:181
  1369.7 105.2 %reduce-scatter.35.cloned.1.call-start = ((), (), s32[]{:S(2)}) async-start(), calls=%async_computation.25 | async-start | bytes 3276800 | tf_op jit(solution)/shard_map/while/body/eval_jaxpr/reduce_scatter | solution.py:173
  1371.9 138.0 %all-gather.21.cloned.1.call-start = ((), (), s32[]{:S(2)}) async-start(), calls=%async_computation.27 | async-start | bytes 1638400 | tf_op jit(solution)/shard_map/while/body/eval_jaxpr/all_gather | solution.py:181
  1556.7 138.0 %all-gather.21.cloned.1.call-start = ((), (), s32[]{:S(2)}) async-start(), calls=%async_computation.27 | async-start | bytes 1638400 | tf_op jit(solution)/shard_map/while/body/eval_jaxpr/all_gather | solution.py:181
  1739.5 105.4 %reduce-scatter.35.cloned.1.call-start = ((), (), s32[]{:S(2)}) async-start(), calls=%async_computation.25 | async-start | bytes 3276800 | tf_op jit(solution)/shard_map/while/body/eval_jaxpr/reduce_scatter | solution.py:173
  1741.6 138.1 %all-gather.21.cloned.1.call-start = ((), (), s32[]{:S(2)}) async-start(), calls=%async_computation.27 | async-start | bytes 1638400 | tf_op jit(solution)/shard_map/while/body/eval_jaxpr/all_gather | solution.py:181
  1924.3 105.4 %reduce-scatter.35.cloned.1.call-start = ((), (), s32[]{:S(2)}) async-start(), calls=%async_computation.25 | async-start | bytes 3276800 | tf_op jit(solution)/shard_map/while/body/eval_jaxpr/reduce_scatter | solution.py:173
  1926.5 138.1 %all-gather.21.cloned.1.call-start = ((), (), s32[]{:S(2)}) async-start(), calls=%async_computation.27 | async-start | bytes 1638400 | tf_op jit(solution)/shard_map/while/body/eval_jaxpr/all_gather | solution.py:181
  2109.4 105.4 %reduce-scatter.35.cloned.1.call-start = ((), (), s32[]{:S(2)}) async-start(), calls=%async_computation.25 | async-start | bytes 3276800 | tf_op jit(solution)/shard_map/while/body/eval_jaxpr/reduce_scatter | solution.py:173
  2111.5 138.1 %all-gather.21.cloned.1.call-start = ((), (), s32[]{:S(2)}) async-start(), calls=%async_computation.27 | async-start | bytes 1638400 | tf_op jit(solution)/shard_map/while/body/eval_jaxpr/all_gather | solution.py:181
  2294.4 105.3 %reduce-scatter.35.cloned.1.call-start = ((), (), s32[]{:S(2)}) async-start(), calls=%async_computation.25 | async-start | bytes 3276800 | tf_op jit(solution)/shard_map/while/body/eval_jaxpr/reduce_scatter | solution.py:173
  2296.5 138.0 %all-gather.21.cloned.1.call-start = ((), (), s32[]{:S(2)}) async-start(), calls=%async_computation.27 | async-start | bytes 1638400 | tf_op jit(solution)/shard_map/while/body/eval_jaxpr/all_gather | solution.py:181
  2479.1 105.4 %reduce-scatter.35.cloned.1.call-start = ((), (), s32[]{:S(2)}) async-start(), calls=%async_computation.25 | async-start | bytes 3276800 | tf_op jit(solution)/shard_map/while/body/eval_jaxpr/reduce_scatter | solution.py:173
  2481.2 138.1 %all-gather.21.cloned.1.call-start = ((), (), s32[]{:S(2)}) async-start(), calls=%async_computation.27 | async-start | bytes 1638400 | tf_op jit(solution)/shard_map/while/body/eval_jaxpr/all_gather | solution.py:181
  3809.7 120.9 %all-gather.15.cloned.1.call-start = ((), (), s32[]{:S(2)}) async-start(), calls=%async_computation.14 | async-start | bytes 2457600 | tf_op jit(solution)/shard_map/all_gather | solution.py:164
  3811.6 537.6 %all-reduce.2.cloned.1.call-start = ((), (), s32[]{:S(2)}) async-start(), calls=%async_computation.16 | async-start | bytes 3932160 | tf_op jit(solution)/shard_map/psum | solution.py:214
  4268.3 117.7 %reduce-scatter.31.cloned.1.call-start = ((), (), s32[]{:S(2)}) async-start(), calls=%async_computation.22 | async-start | bytes 737280
  4271.6 155.6 %reduce-scatter.29.cloned.1.call-start = ((), (), s32[]{:S(2)}) async-start(), calls=%async_computation.21 | async-start | bytes 1474560
  4281.7 182.2 %reduce-scatter.27.cloned.1.call-start = ((), (), s32[]{:S(2)}) async-start(), calls=%async_computation.20 | async-start | bytes 368640
  4356.3 144.4 %reduce-scatter.25.cloned.1.call-start = ((), (), s32[]{:S(2)}) async-start(), calls=%async_computation.19 | async-start | bytes 368640
  4357.3 194.1 %reduce-scatter.21.cloned.1.call-start = ((), (), s32[]{:S(2)}) async-start(), calls=%async_computation.17 | async-start | bytes 3686400 | tf_op jit(solution)/shard_map/reduce_scatter | solution.py:197
  4357.9 244.4 %reduce-scatter.23.cloned.1.call-start = ((), (), s32[]{:S(2)}) async-start(), calls=%async_computation.18 | async-start | bytes 3686400 | tf_op jit(solution)/shard_map/reduce_scatter | solution.py:198
  (155 other events, 7448.4 us)
Sparse Core Ops, SparseCore 0:
  232.7 72.9 reduce-scatter.18
  308.5 76.8 all-gather.8
  445.9 52.0 reduce-scatter.36
  500.2 51.7 reduce-scatter.34
  630.8 51.0 reduce-scatter.36
  684.1 51.7 reduce-scatter.34
  815.5 51.0 reduce-scatter.36
  868.8 51.7 reduce-scatter.34
  1000.3 51.0 reduce-scatter.36
  1053.6 51.7 reduce-scatter.34
  1185.0 51.0 reduce-scatter.36
  1238.4 51.7 reduce-scatter.34
  1369.9 51.0 reduce-scatter.36
  1423.2 51.7 reduce-scatter.34
  1554.7 51.0 reduce-scatter.36
  1608.0 51.7 reduce-scatter.34
  1739.6 51.0 reduce-scatter.36
  1793.1 51.7 reduce-scatter.34
  1924.5 51.0 reduce-scatter.36
  1977.9 51.7 reduce-scatter.34
  2109.5 51.0 reduce-scatter.36
  2162.9 51.7 reduce-scatter.34
  2294.5 51.1 reduce-scatter.36
  2347.8 51.7 reduce-scatter.34
  2479.2 51.0 reduce-scatter.36
  2532.7 51.7 reduce-scatter.34
  2666.8 51.1 reduce-scatter.32
  2762.5 51.0 reduce-scatter.32
  2858.2 51.0 reduce-scatter.32
  3336.7 51.0 reduce-scatter.32
  3811.4 75.4 all-gather.16
  4268.5 80.7 all-reduce.1
  (53 shorter events, 1887.9 us)
where the time goes:
time: 4630 us; the launch traced here: 4610 us
  waiting for transfers between devices  3470 us (75%)
  matrix products  501 us (11%)
  local copies, waits for them, and re-layouts  284 us (6%)
  other arithmetic  192 us (4%)
  loops' own time  119 us (3%)
    reduce_scatter x24, waiting for transfers between devices, hidden_block(): lax.psum_scatter(jnp.dot(x_block, ffn_in_full, preferred_element_type=jnp...  1200 us
    all_gather x24, waiting for transfers between devices, hidden_block(): act_rows = lax.all_gather(act_share, 'narrow', axis=0, tiled=True)  675 us
    reduce_scatter x12, waiting for transfers between devices, ffn_backward(): lax.psum_scatter(jnp.dot(dy_block, ffn_down_part, preferred_element_type=...  610 us
    all_gather x12, waiting for transfers between devices, ffn_backward(): drows = lax.all_gather(dshare, 'narrow', axis=0, tiled=True)  382 us
    unnamed x17, waiting for transfers between devices  126 us
  transfers between devices with their start and end apart: 85, of which 85 were waited for; matrix products, arithmetic and copies ran while one was open for 5% of the time, Pallas kernels for 0%

commit v1 on v0

v1 whole, which is shorter than its diff:
```python
from functools import partial

import jax
import jax.numpy as jnp
from jax import lax
from jax.experimental import pallas as pl
from jax.experimental.pallas import tpu as pltpu
from jax.sharding import PartitionSpec as P

HD = 32
EPS = 1e-05
LOG2E = 1.4426950408889634
SCALE = HD ** (-0.5)
BQ = 256
BK = 256
BF16 = jnp.bfloat16
F32 = jnp.float32
VMEM_LIMIT = 56 * 1024 * 1024


def vmem(*shape):
    return pl.BlockSpec(shape, None) if shape else pl.BlockSpec(memory_space=pltpu.VMEM)


def dot(a, b):
    return jnp.dot(a, b, preferred_element_type=F32)


def dot_nt(a, b):
    return lax.dot_general(a, b, (((1,), (1,)), ((), ())), preferred_element_type=F32)


def normalized(rows):
    center = rows - jnp.mean(rows, axis=-1, keepdims=True)
    spread = jnp.mean(center * center, axis=-1, keepdims=True)
    inverse = lax.rsqrt(spread + EPS)
    return center * inverse, inverse


def norm_backward(rows, gain, grad):
    unit, inverse = normalized(rows)
    scaled = grad * gain
    inner = scaled - jnp.mean(scaled, axis=-1, keepdims=True)
    inner = inner - unit * jnp.mean(scaled * unit, axis=-1, keepdims=True)
    return inverse * inner, grad * unit


def project_kernel(
    lens, x_ref, gain_ref, shift_ref, w_ref,
    xn_ref, q_ref, k_ref, qt_ref, kt_ref, vt_ref, segc_ref, segr_ref, bounds_ref,
):
    block = pl.program_id(0)
    first = block * BQ
    last = first + BQ - 1
    heads = q_ref.shape[0]
    end = jnp.int32(0)
    low = jnp.int32(0)
    high = jnp.int32(pl.num_programs(0) * BQ)
    rows = first + lax.broadcasted_iota(jnp.int32, segc_ref.shape, 0)
    cols = first + lax.broadcasted_iota(jnp.int32, segr_ref.shape, 1)
    seg_rows = jnp.zeros(segc_ref.shape, jnp.int32)
    seg_cols = jnp.zeros(segr_ref.shape, jnp.int32)
    for item in range(lens.shape[1]):
        end = end + lens[0, item]
        low = jnp.where(end <= first, end, low)
        high = jnp.where((end > last) & (end < high), end, high)
        seg_rows = seg_rows + (rows >= end).astype(jnp.int32)
        seg_cols = seg_cols + (cols >= end).astype(jnp.int32)
    segc_ref[...] = seg_rows
    segr_ref[...] = seg_cols
    bounds_ref[block, 0] = lax.div(low, jnp.int32(BK))
    bounds_ref[block, 1] = lax.div(high + (BK - 1), jnp.int32(BK))
    unit, _ = normalized(x_ref[...].astype(F32))
    xn = (unit * gain_ref[0:1, :].astype(F32) + shift_ref[0:1, :].astype(F32)).astype(BF16)
    xn_ref[...] = xn
    for item, (rows_ref, cols_ref) in enumerate(((q_ref, qt_ref), (k_ref, kt_ref), (None, vt_ref))):
        full = dot(xn, w_ref[item])
        cols_ref[...] = full.T.astype(BF16)
        if rows_ref is not None:
            low_rows = full.astype(BF16)
            for head in range(heads):
                rows_ref[head] = low_rows[:, head * HD : (head + 1) * HD]


def project(lens, tokens, gains, shifts, weights):
    count, dim = tokens.shape
    width = weights.shape[2]
    heads = width // HD
    blocks = count // BQ
    per_head = pl.BlockSpec((heads, BQ, HD), lambda i: (0, i, 0))
    turned = pl.BlockSpec((width, BQ), lambda i: (0, i))
    fixed2 = pl.BlockSpec((2, dim), lambda i: (0, 0))
    return pl.pallas_call(
        project_kernel,
        grid=(blocks,),
        in_specs=[
            pl.BlockSpec(memory_space=pltpu.SMEM),
            pl.BlockSpec((BQ, dim), lambda i: (i, 0)),
            fixed2,
            fixed2,
            pl.BlockSpec((3, dim, width), lambda i: (0, 0, 0)),
        ],
        out_specs=[
            pl.BlockSpec((BQ, dim), lambda i: (i, 0)),
            per_head,
            per_head,
            turned,
            turned,
            turned,
            pl.BlockSpec((BQ, 128), lambda i: (i, 0)),
            pl.BlockSpec((8, BQ), lambda i: (0, i)),
            pl.BlockSpec(memory_space=pltpu.SMEM),
        ],
        out_shape=[
            jax.ShapeDtypeStruct((count, dim), BF16),
            jax.ShapeDtypeStruct((heads, count, HD), BF16),
            jax.ShapeDtypeStruct((heads, count, HD), BF16),
            jax.ShapeDtypeStruct((width, count), BF16),
            jax.ShapeDtypeStruct((width, count), BF16),
            jax.ShapeDtypeStruct((width, count), BF16),
            jax.ShapeDtypeStruct((count, 128), jnp.int32),
            jax.ShapeDtypeStruct((8, count), jnp.int32),
            jax.ShapeDtypeStruct((blocks, 2), jnp.int32),
        ],
        compiler_params=pltpu.CompilerParams(vmem_limit_bytes=VMEM_LIMIT),
        cost_estimate=pl.CostEstimate(
            flops=2 * count * dim * 3 * width, bytes_accessed=4 * count * dim, transcendentals=0
        ),
        name="project",
    )(lens, tokens, gains, shifts, weights)


def spread_lanes(column, width):
    return jnp.concatenate([column] * (width // 128), axis=1) if width > 128 else column


def attend_kernel(
    first, heads, bounds, segc_ref, segr_ref, k_ref, qt_ref, vt_ref, part_ref, ot_ref, lse_ref
):
    count = segc_ref.shape[0]
    factor = SCALE * LOG2E

    def q_block(block, _):
        start = pl.multiple_of(block * BQ, BQ)
        seg_q = segr_ref[0:1, pl.ds(start, BQ)]
        queries = [
            qt_ref[(first + h) * HD : (first + h + 1) * HD, pl.ds(start, BQ)] for h in range(heads)
        ]

        def k_block(item, carry):
            at = pl.multiple_of(item * BK, BK)
            allowed = spread_lanes(segc_ref[pl.ds(at, BK), :], BQ) == seg_q
            out = []
            scores = [dot(k_ref[first + h, pl.ds(at, BK), :], queries[h]) for h in range(heads)]
            scores = [jnp.where(allowed, value, -1e30) for value in scores]
            fresh = [
                jnp.maximum(carry[h][0], jnp.max(scores[h], axis=0, keepdims=True))
                for h in range(heads)
            ]
            expd = [jnp.exp2((scores[h] - fresh[h]) * factor) for h in range(heads)]
            for h in range(heads):
                top, total, acc = carry[h]
                fade = jnp.exp2((top - fresh[h]) * factor)
                total = total * fade + jnp.sum(expd[h], axis=0, keepdims=True)
                rows = vt_ref[(first + h) * HD : (first + h + 1) * HD, pl.ds(at, BK)]
                acc = acc * fade + dot(rows, expd[h].astype(BF16))
                out.append((fresh[h], total, acc))
            return tuple(out)

        empty = (
            jnp.full((1, BQ), -1e30, F32),
            jnp.zeros((1, BQ), F32),
            jnp.zeros((HD, BQ), F32),
        )
        done = lax.fori_loop(bounds[block, 0], bounds[block, 1], k_block, (empty,) * heads)
        for h in range(heads):
            top, total, acc = done[h]
            ot_ref[h * HD : (h + 1) * HD, pl.ds(start, BQ)] = acc / total
            lse_ref[h : h + 1, pl.ds(start, BQ)] = top * factor + jnp.log(total) * LOG2E
        return 0

    lax.fori_loop(0, count // BQ, q_block, 0)
    parts = part_ref.shape[0]
    size = count // parts
    for part in range(parts):
        part_ref[part] = ot_ref[:, part * size : (part + 1) * size].astype(BF16)


def attend(first, heads, parts, tables, k_rows, q_cols, v_cols):
    segc, segr, bounds = tables
    count = segc.shape[0]
    return pl.pallas_call(
        partial(attend_kernel, first, heads),
        in_specs=[pl.BlockSpec(memory_space=pltpu.SMEM)] + [vmem()] * 5,
        out_specs=[vmem()] * 3,
        out_shape=[
            jax.ShapeDtypeStruct((parts, heads * HD, count // parts), BF16),
            jax.ShapeDtypeStruct((heads * HD, count), F32),
            jax.ShapeDtypeStruct((8, count), F32),
        ],
        compiler_params=pltpu.CompilerParams(vmem_limit_bytes=VMEM_LIMIT),
        cost_estimate=pl.CostEstimate(
            flops=heads * count * count * 300, bytes_accessed=4 * count * 640, transcendentals=0
        ),
        name=f"attend_{first}",
    )(bounds, segc, segr, k_rows, q_cols, v_cols)


def attend_back_kernel(
    first, heads, bounds, segc_ref, segr_ref, q_ref, k_ref, qt_ref, kt_ref, vt_ref,
    part_ref, ot_ref, lse_ref, out_ref, flat_ref,
    dot_ref, do_ref, stat_ref, dq_ref, dqt_ref, dkt_ref, dvt_ref,
):
    count = segc_ref.shape[0]
    factor = SCALE * LOG2E
    parts = part_ref.shape[0]
    size = count // parts
    for part in range(parts):
        dot_ref[:, part * size : (part + 1) * size] = part_ref[part]
        for h in range(heads):
            do_ref[h, part * size : (part + 1) * size, :] = part_ref[
                part, h * HD : (h + 1) * HD, :
            ].T
    dkt_ref[...] = jnp.zeros_like(dkt_ref)
    dvt_ref[...] = jnp.zeros_like(dvt_ref)

    def q_block(block, _):
        start = pl.multiple_of(block * BQ, BQ)
        spot = pl.ds(start, BQ)
        stats = [lse_ref[0:heads, spot]]
        for h in range(heads):
            lane = slice(h * HD, (h + 1) * HD)
            stats.append(
                jnp.sum(dot_ref[lane, spot].astype(F32) * ot_ref[lane, spot], axis=0, keepdims=True)
            )
        stats.append(jnp.zeros((8 - 2 * heads, BQ), F32)) if heads < 4 else None
        turned = jnp.concatenate(stats, axis=0).T
        for h in range(2 * heads):
            stat_ref[h] = jnp.broadcast_to(turned[:, h : h + 1], (BQ, 128))
        dq_ref[...] = jnp.zeros_like(dq_ref)
        seg_q = spread_lanes(segc_ref[spot, :], BK)

        def k_block(item, _):
            at = pl.multiple_of(item * BK, BK)
            here = pl.ds(at, BK)
            allowed = seg_q == segr_ref[0:1, here]
            lanes = [slice(h * HD, (h + 1) * HD) for h in range(heads)]
            owns = [slice((first + h) * HD, (first + h + 1) * HD) for h in range(heads)]
            scores = [dot(q_ref[first + h, spot, :], kt_ref[owns[h], here]) for h in range(heads)]
            dprob = [dot(do_ref[h, spot, :], vt_ref[owns[h], here]) for h in range(heads)]
            prob = [
                jnp.where(
                    allowed, jnp.exp2(scores[h] * factor - spread_lanes(stat_ref[h], BK)), 0.0
                )
                for h in range(heads)
            ]
            dscore = [
                (prob[h] * (dprob[h] - spread_lanes(stat_ref[heads + h], BK))).astype(BF16)
                for h in range(heads)
            ]
            for h in range(heads):
                dvt_ref[lanes[h], here] += dot(dot_ref[lanes[h], spot], prob[h].astype(BF16))
                dkt_ref[lanes[h], here] += dot(qt_ref[owns[h], spot], dscore[h])
                dq_ref[h] += dot(dscore[h], k_ref[first + h, here, :])
            return 0

        lax.fori_loop(bounds[block, 0], bounds[block, 1], k_block, 0)
        for h in range(heads):
            dqt_ref[h * HD : (h + 1) * HD, spot] = dq_ref[h].T * SCALE
        return 0

    lax.fori_loop(0, count // BQ, q_block, 0)
    width = heads * HD
    for item, (source, scale) in enumerate(((dqt_ref, 1.0), (dkt_ref, SCALE), (dvt_ref, 1.0))):
        value = source[...] if scale == 1.0 else source[...] * scale
        value = value.astype(BF16)
        flat_ref[item * width : (item + 1) * width, :] = value
        for part in range(parts):
            out_ref[part, item * width : (item + 1) * width, :] = value[
                :, part * size : (part + 1) * size
            ]


def attend_back(first, heads, tables, q_rows, k_rows, q_cols, k_cols, v_cols, dout, out, lse):
    segc, segr, bounds = tables
    count = segc.shape[0]
    parts = dout.shape[0]
    width = heads * HD
    return pl.pallas_call(
        partial(attend_back_kernel, first, heads),
        in_specs=[pl.BlockSpec(memory_space=pltpu.SMEM)] + [vmem()] * 10,
        out_specs=[vmem()] * 2,
        out_shape=[
            jax.ShapeDtypeStruct((parts, 3 * width, count // parts), BF16),
            jax.ShapeDtypeStruct((3 * width, count), BF16),
        ],
        scratch_shapes=[
            pltpu.VMEM((width, count), BF16),
            pltpu.VMEM((heads, count, HD), BF16),
            pltpu.VMEM((2 * heads, BQ, 128), F32),
            pltpu.VMEM((heads, BQ, HD), F32),
            pltpu.VMEM((width, count), F32),
            pltpu.VMEM((width, count), F32),
            pltpu.VMEM((width, count), F32),
        ],
        compiler_params=pltpu.CompilerParams(vmem_limit_bytes=VMEM_LIMIT),
        cost_estimate=pl.CostEstimate(
            flops=heads * count * count * 900, bytes_accessed=4 * count * 640, transcendentals=0
        ),
        name=f"attend_back_{first}",
    )(bounds, segc, segr, q_rows, k_rows, q_cols, k_cols, v_cols, dout, out, lse)


def mix_kernel(ot_ref, w_ref, x_ref, gain_ref, shift_ref, x2_ref, xn_ref, full_ref):
    tall, across, height, narrow = w_ref.shape
    for i in range(tall):
        for j in range(across):
            full_ref[i * height : (i + 1) * height, j * narrow : (j + 1) * narrow] = w_ref[i, j]
    mixed = lax.dot_general(
        ot_ref[...], full_ref[...], (((0,), (0,)), ((), ())), preferred_element_type=F32
    )
    middle = x_ref[...].astype(F32) + mixed
    x2_ref[...] = middle
    unit, _ = normalized(middle)
    xn_ref[...] = (unit * gain_ref[1:2, :].astype(F32) + shift_ref[1:2, :].astype(F32)).astype(BF16)


def mix(ot, w_pieces, rows, gains, shifts):
    count, dim = rows.shape
    return pl.pallas_call(
        mix_kernel,
        in_specs=[vmem()] * 5,
        out_specs=[vmem()] * 3,
        out_shape=[
            jax.ShapeDtypeStruct((count, dim), F32),
            jax.ShapeDtypeStruct((count, dim), BF16),
            jax.ShapeDtypeStruct((dim, dim), BF16),
        ],
        compiler_params=pltpu.CompilerParams(vmem_limit_bytes=VMEM_LIMIT),
        cost_estimate=pl.CostEstimate(
            flops=2 * count * dim * dim, bytes_accessed=8 * count * dim, transcendentals=0
        ),
        name="mix",
    )(ot, w_pieces, rows, gains, shifts)


ROWS = 256


def ffn_kernel(blocks, start, stop, *refs):
    refs = list(refs)
    xn_parts = [refs.pop(0), refs.pop(0)]
    dy_parts = [refs.pop(0), refs.pop(0)]
    weights = [(refs.pop(0), refs.pop(0)) for _ in range(blocks)]
    old = None if start else (refs.pop(0), refs.pop(0))
    y_out, dx_out = refs.pop(0), refs.pop(0)
    far_out = refs.pop(0) if stop else None
    grads = [(refs.pop(0), refs.pop(0)) for _ in range(blocks)]
    if stop:
        y_ref, dx_ref = refs.pop(0), refs.pop(0)
    else:
        y_ref, dx_ref = y_out, dx_out
    xn_ref, dy_ref, g_ref, du_ref = refs
    mine = xn_parts[0].shape[0]
    count = xn_ref.shape[0]
    for item in range(2):
        xn_ref[item * mine : (item + 1) * mine, :] = xn_parts[item][...]
        dy_ref[item * mine : (item + 1) * mine, :] = dy_parts[item][...]
    for index, ((in_ref, down_ref), (gin_ref, gdown_ref)) in enumerate(zip(weights, grads)):
        for first in range(0, count, ROWS):
            rows = slice(first, first + ROWS)
            u = dot(xn_ref[rows, :], in_ref[...])
            dg = dot(dy_ref[rows, :], down_ref[...])
            half = 0.5 + 0.5 * lax.erf(u * 0.7071067811865476)
            slope = half + u * (jnp.exp2(u * u * (-0.5 * LOG2E)) * 0.3989422804014327)
            g = (u * half).astype(BF16)
            du = (dg * slope).astype(BF16)
            g_ref[rows, :] = g
            du_ref[rows, :] = du
            y = dot_nt(g, down_ref[...])
            dx = dot_nt(du, in_ref[...])
            if index > 0:
                y = y + y_ref[rows, :]
                dx = dx + dx_ref[rows, :]
            elif old is not None:
                y = y + old[0][rows, :]
                dx = dx + old[1][rows, :]
            y_ref[rows, :] = y
            dx_ref[rows, :] = dx
        gin_ref[...] = lax.dot_general(
            xn_ref[...], du_ref[...], (((0,), (0,)), ((), ())), preferred_element_type=F32
        ).astype(BF16)
        gdown_ref[...] = lax.dot_general(
            dy_ref[...], g_ref[...], (((0,), (0,)), ((), ())), preferred_element_type=F32
        ).astype(BF16)
    if stop:
        y_out[...] = y_ref[:mine, :]
        dx_out[...] = dx_ref[:mine, :]
        far_out[0] = y_ref[mine:, :].astype(BF16)
        far_out[1] = dx_ref[mine:, :].astype(BF16)


def ffn(xn, dy, weights, sums=None, stop=False):
    mine, dim = xn[0].shape
    count = 2 * mine
    blocks = len(weights)
    hidden = weights[0][0].shape[1]
    start = sums is None
    total = jax.ShapeDtypeStruct((mine if stop else count, dim), F32)
    grad = jax.ShapeDtypeStruct((dim, hidden), BF16)
    far = [jax.ShapeDtypeStruct((2, mine, dim), BF16)] if stop else []
    args = [*xn, *dy, *(part for pair in weights for part in pair)]
    args += [] if start else list(sums)
    out_shape = [total, total] + far + [grad] * (2 * blocks)
    scratch = [pltpu.VMEM((count, dim), F32)] * 2 if stop else []
    out = pl.pallas_call(
        partial(ffn_kernel, blocks, start, stop),
        in_specs=[vmem()] * len(args),
        out_specs=[vmem()] * len(out_shape),
        out_shape=out_shape,
        scratch_shapes=scratch
        + [pltpu.VMEM((count, dim), BF16)] * 2
        + [pltpu.VMEM((count, hidden), BF16)] * 2,
        compiler_params=pltpu.CompilerParams(vmem_limit_bytes=VMEM_LIMIT),
        cost_estimate=pl.CostEstimate(
            flops=12 * count * dim * hidden * blocks,
            bytes_accessed=8 * count * dim + 8 * blocks * dim * hidden,
            transcendentals=2 * count * hidden * blocks,
        ),
        name="ffn",
    )(*args)
    head = 3 if stop else 2
    return out[:head], [tuple(out[head + 2 * i : head + 2 * i + 2]) for i in range(blocks)]


def turn_kernel(
    x2_ref, y_ref, dx_ref, far_ref, dy_ref, w_ref, ot_ref, gain_ref,
    out_ref, dx2_ref, dot_ref, gout_ref, sums_ref,
):
    middle = x2_ref[...]
    out_ref[...] = (middle + y_ref[...] + far_ref[0].astype(F32)).astype(BF16)
    grad = dx_ref[...] + far_ref[1].astype(F32)
    back, prod = norm_backward(middle, gain_ref[1:2, :].astype(F32), grad)
    dx2 = dy_ref[...].astype(F32) + back
    dx2_ref[...] = dx2
    sums_ref[...] = jnp.concatenate(
        [
            jnp.sum(prod, axis=0, keepdims=True),
            jnp.sum(grad, axis=0, keepdims=True),
            jnp.zeros((6, grad.shape[1]), F32),
        ],
        axis=0,
    )
    low = dx2.astype(BF16)
    dot_ref[...] = dot_nt(w_ref[...], low).astype(BF16)
    gout_ref[...] = lax.dot_general(
        low, ot_ref[...], (((0,), (1,)), ((), ())), preferred_element_type=F32
    ).astype(BF16)


def turn(x2, y, dx, far, dy, w_out, ot, gains):
    count, dim = x2.shape
    return pl.pallas_call(
        turn_kernel,
        in_specs=[vmem()] * 8,
        out_specs=[vmem()] * 5,
        out_shape=[
            jax.ShapeDtypeStruct((count, dim), BF16),
            jax.ShapeDtypeStruct((count, dim), F32),
            jax.ShapeDtypeStruct((dim, count), BF16),
            jax.ShapeDtypeStruct((dim, dim), BF16),
            jax.ShapeDtypeStruct((8, dim), F32),
        ],
        compiler_params=pltpu.CompilerParams(vmem_limit_bytes=VMEM_LIMIT),
        cost_estimate=pl.CostEstimate(
            flops=4 * count * dim * dim, bytes_accessed=24 * count * dim, transcendentals=0
        ),
        name="turn",
    )(x2, y, dx, far, dy, w_out, ot, gains)


def finish_kernel(parts_ref, w_ref, x_ref, dx2_ref, gain_ref, out_ref, sums_ref):
    groups, _, _, width = w_ref.shape
    total = None
    for group in range(groups):
        for item in range(3):
            term = dot(w_ref[group, item], parts_ref[group, item * width : (item + 1) * width, :])
            total = term if total is None else total + term
    grad = total.T
    back, prod = norm_backward(x_ref[...].astype(F32), gain_ref[0:1, :].astype(F32), grad)
    out_ref[...] = (dx2_ref[...] + back).astype(BF16)
    sums_ref[...] = jnp.concatenate(
        [
            jnp.sum(prod, axis=0, keepdims=True),
            jnp.sum(grad, axis=0, keepdims=True),
            jnp.zeros((6, grad.shape[1]), F32),
        ],
        axis=0,
    )


def finish(parts, w_qkv, rows, dx2, gains):
    count, dim = rows.shape
    return pl.pallas_call(
        finish_kernel,
        in_specs=[vmem()] * 5,
        out_specs=[vmem()] * 2,
        out_shape=[
            jax.ShapeDtypeStruct((count, dim), BF16),
            jax.ShapeDtypeStruct((8, dim), F32),
        ],
        compiler_params=pltpu.CompilerParams(vmem_limit_bytes=VMEM_LIMIT),
        cost_estimate=pl.CostEstimate(
            flops=6 * count * dim * dim, bytes_accessed=16 * count * dim, transcendentals=0
        ),
        name="finish",
    )(parts, w_qkv, rows, dx2, gains)


def swap(value, bit, size):
    return lax.ppermute(value, "wide", [(i, i ^ bit) for i in range(size)])


def exchange(value, axis):
    return lax.all_to_all(value, axis, 0, 0, tiled=True)


def local(
    tokens, cotangent, seq_lens, norm_gains, norm_shifts, w_qkv, w_attn_out, w_ffn_in, w_ffn_down
):
    depth = lax.axis_size("narrow")
    across = lax.axis_size("wide")
    count, dim = tokens.shape
    mine = count // depth
    width = w_qkv.shape[2]
    cols = w_ffn_in.shape[1]
    layer = lax.axis_index("narrow")
    place = lax.axis_index("wide")
    close = across == 8

    qkv = lax.all_gather(w_qkv, "wide", axis=1, tiled=True)
    pieces = lax.all_to_all(
        jnp.broadcast_to(w_attn_out[None], (depth * across,) + w_attn_out.shape),
        ("narrow", "wide"), 0, 0, tiled=True,
    ).reshape((depth, across) + w_attn_out.shape)
    stacked = lax.all_gather(
        jnp.concatenate([w_ffn_in, w_ffn_down], axis=1), "narrow", axis=0, tiled=True
    )
    if close:
        block = (stacked[:, :cols], stacked[:, cols:])
        block_x = tuple(swap(part, 2, across) for part in block)
        block_y = tuple(swap(part, 4, across) for part in block)
        block_d = (swap(block_x[0], 4, across), swap(block_y[1], 2, across))
        weights = [block, block_x, block_y, block_d]
    else:
        every = lax.all_gather(stacked, "wide", axis=0)
        every = every.reshape(across // 2, 2, dim, 2 * cols)
        every = lax.dynamic_index_in_dim(every, place % 2, 1, keepdims=False)
        flat = [
            every[:, :, at : at + cols].transpose(1, 0, 2).reshape(dim, -1) for at in (0, cols)
        ]
        weights = [
            tuple(part[:, at : at + dim] for part in flat) for at in range(0, flat[0].shape[1], dim)
        ]

    rows = lax.dynamic_slice_in_dim(tokens, layer * mine, mine, 0)
    dy = lax.dynamic_slice_in_dim(cotangent, layer * mine, mine, 0)
    dy_pair = (dy, swap(dy, 1, across))

    xn, q_rows, k_rows, q_cols, k_cols, v_cols, *tables = project(
        seq_lens, tokens, norm_gains, norm_shifts, qkv
    )
    heads = width // HD
    part, out, lse = attend(0, heads, depth, tables, k_rows, q_cols, v_cols)
    ot = exchange(part, "narrow").reshape(dim, mine)
    x2, xn2, w_out = mix(ot, pieces, rows, norm_gains, norm_shifts)
    xn_pair = (xn2, swap(xn2, 1, across))

    sums, grads_a = ffn(xn_pair, dy_pair, weights[:1])
    sums, grads_b = ffn(xn_pair, dy_pair, weights[1:-1], sums)
    (y, dx, far), grads_c = ffn(xn_pair, dy_pair, weights[-1:], sums, stop=True)
    far = swap(far, 1, across)
    out_mine, dx2, dot_cols, grad_out, norm_two = turn(
        x2, y, dx, far, dy, w_out, ot, norm_gains
    )
    layer_out = lax.all_gather(out_mine, "narrow", axis=0, tiled=True)

    dout = exchange(dot_cols.reshape(depth, width, mine), "narrow")
    back, flat_back = attend_back(
        0, heads, tables, q_rows, k_rows, q_cols, k_cols, v_cols, dout, out, lse
    )
    qkv_all = lax.all_gather(qkv, "narrow", axis=0)
    back = exchange(back, "narrow")
    in_mine, norm_one = finish(back, qkv_all, rows, dx2, norm_gains)
    input_grad = lax.all_gather(in_mine, "narrow", axis=0, tiled=True)

    grads = grads_a + grads_b + grads_c
    if close:
        own, gx, gy, gd = grads
        add = lambda *parts: sum(part.astype(F32) for part in parts).astype(BF16)
        relay_in = swap(gd[0], 2, across)
        relay_down = swap(gd[1], 4, across)
        gy_in = add(gy[0], relay_in)
        gx_down = add(gx[1], relay_down)
        from_x = (swap(gx[0], 2, across), swap(gx_down, 2, across))
        from_y = (swap(gy_in, 4, across), swap(gy[1], 4, across))
        total = jnp.concatenate([add(own[i], from_x[i], from_y[i]) for i in range(2)], axis=1)
    else:
        both = [
            jnp.concatenate([pair[i] for pair in grads], axis=1)
            .reshape(dim, across // 2, cols)
            .transpose(1, 0, 2)
            for i in range(2)
        ]
        both = jnp.concatenate(both, axis=2)[:, None]
        core = jnp.arange(2).reshape(1, 2, 1, 1) == place % 2
        both = jnp.where(core, both, jnp.zeros((), BF16)).reshape(across, dim, 2 * cols)
        total = lax.psum_scatter(both, "wide", scatter_dimension=0, tiled=False)
    total = lax.psum_scatter(total, "narrow", scatter_dimension=0, tiled=True).astype(F32)

    gqkv = lax.dot_general(
        xn, flat_back, (((0,), (1,)), ((), ())), preferred_element_type=F32
    ).astype(BF16)
    gqkv = exchange(gqkv.reshape(across, dim // across, 3 * width), "wide")
    gqkv = jnp.sum(gqkv.astype(F32), axis=0)
    gqkv = gqkv.reshape(dim // across, 3, width).transpose(1, 0, 2)

    gout = exchange(grad_out.reshape(across, dim // across, dim), "wide")
    gout = jnp.sum(gout.astype(F32), axis=0).astype(BF16)
    gout = exchange(gout.reshape(dim // across, depth, width).transpose(1, 0, 2), "narrow")
    gout = jnp.sum(gout.astype(F32), axis=0).T

    norms = jnp.concatenate([norm_one[:2], norm_two[:2]], axis=0)
    norms = lax.psum(norms, ("narrow", "wide"))
    norms = lax.dynamic_slice_in_dim(norms, place * (dim // across), dim // across, 1)
    return (
        layer_out,
        input_grad,
        norms[0::2],
        norms[1::2],
        gqkv,
        gout,
        total[:, :cols],
        total[:, cols:],
    )


def solution(mesh):
    placed = (
        P("wide", None),
        P("wide", None),
        P("wide", None),
        P(),
        P(),
        P(None, "wide", "narrow"),
        P("narrow", "wide"),
        P("narrow", "wide"),
        P("narrow", "wide"),
    )
    return jax.shard_map(
        local,
        mesh=mesh,
        in_specs=placed,
        out_specs=(
            P("wide", None),
            P("wide", None),
            P(None, "wide"),
            P(None, "wide"),
            P(None, "wide", "narrow"),
            P("narrow", "wide"),
            P("narrow", "wide"),
            P("narrow", "wide"),
        ),
        check_vma=False,
    )
```

time: 4630 us -> 448 us (0.10)
  waiting for transfers between devices: 3470 us -> 142 us
  matrix products: 501 us -> 2.86 us
  local copies, waits for them, and re-layouts: 284 us -> 32.9 us
  other arithmetic: 192 us -> 9 us
  loops' own time: 119 us -> 0 us
  Pallas kernels: 0 us -> 116 us
  blocking collectives: 22.4 us -> 89.6 us
    reduce_scatter x39 -> x1, waiting for transfers between devices: 1980 us -> 0.01 us  [local(): lax.psum_scatter(total, 'narrow', scatter_dimension=0, tiled=True)]
    all_gather x41 -> x4, waiting for transfers between devices: 1290 us -> 0.02 us  [the longest x1 0.02 us: local(): qkv_all = lax.all_gather(qkv, 'narrow', axis=0)]
    dot_general x193 -> x1, matrix products: 495 us -> 2.86 us  [local(): lax.dot_general(xn, flat_back, (((0,), (1,)), ((), ())), preferred_elemen...]
    convert_element_type x58 -> x4, other arithmetic: 141 us -> 5.5 us  [local(): add = lambda *parts: sum((part.astype(F32) for part in parts)).astype(BF16)]
    unnamed x17 -> x5, waiting for transfers between devices: 126 us -> 0.08 us
    dynamic_slice x147 -> x3, local copies, waits for them, and re-layouts: 128 us -> 2.79 us  [the longest x1 1.88 us: local(): rows = lax.dynamic_slice_in_dim(tokens, layer * mine, mine, 0)]
    another operation x14 -> x0, loops' own time: 119 us -> none  [the longest x5 28.6 us: one_head(): (dkey, dvalue), dquery = lax.scan(one_block, (zeros, zeros), starts)]
    pallas_call x0 -> x9, Pallas kernels: none -> 116 us  [the longest x1 34.9 us: attend_back(): pl.pallas_call(partial(attend_back_kernel, first, heads), in_specs=[pl.Bl...]
  transfers between devices with their start and end apart: 85 -> 25, of which waited for: 85 -> 12; matrix products, arithmetic and copies ran while one was open for 5% -> 7% of each run, Pallas kernels for 0% -> 26%
where the time goes in v1:
time: 448 us; the launch traced here: 443 us
  waiting for transfers between devices  142 us (32%)
  Pallas kernels  116 us (26%)
  blocking collectives  89.6 us (20%)
  starting transfers between devices  36.8 us (8%)
  local copies, waits for them, and re-layouts  32.9 us (7%)
  between operations  14.4 us (3%)
  other arithmetic  9 us (2%)
    ppermute x15, waiting for transfers between devices, swap(): return lax.ppermute(value, 'wide', [(i, i ^ bit) for i in range(size)])  57.8 us
    all_to_all x1, waiting for transfers between devices, local(): lax.all_to_all(jnp.broadcast_to(w_attn_out[None], (depth * across,) + w_a...  46 us
    all_to_all x4, waiting for transfers between devices, exchange(): return lax.all_to_all(value, axis, 0, 0, tiled=True)  37.8 us
    all_to_all x2, blocking collectives, exchange(): return lax.all_to_all(value, axis, 0, 0, tiled=True)  37.8 us
    psum x1, blocking collectives, local(): norms = lax.psum(norms, ('narrow', 'wide'))  37.5 us
    pallas_call x1, Pallas kernels, attend_back(): pl.pallas_call(partial(attend_back_kernel, first, heads), in_specs=[pl.Bl...  34.9 us
    pallas_call x3, Pallas kernels, ffn(): pl.pallas_call(partial(ffn_kernel, blocks, start, stop), in_specs=[vmem()...  33.3 us
    pallas_call x1, Pallas kernels, attend(): pl.pallas_call(partial(attend_kernel, first, heads), in_specs=[pl.BlockSp...  22.5 us
  transfers between devices with their start and end apart: 25, of which 12 were waited for; matrix products, arithmetic and copies ran while one was open for 7% of the time, Pallas kernels for 26%

profile of v1, /device:TPU:0, one launch (start us, length us, event | category | flops | bytes accessed | tf_op | source)
XLA Modules:
  0.0 443.3 jit_solution(10708637900903097313)
XLA Ops:
  9.2 14.3 %all_gather.18.w_ref = bf16[3,640,160]{2,1,0:T(8,128)(2,1)} all-gather(bf16[3,80,160]{2,1,0:T(8,128)(2,1)} %param.14), channel_id=1, replica_groups=mesh['narrow'=4,'wide'=8] {'wide'}, dimensions={1}, use_global_device_ids=true | all-gather | bytes 691200 | tf_op jit(solution)/shard_map/all_gather | solution.py:541
  23.5 9.3 %project.1 = (bf16[1536,640]{1,0:T(8,128)(2,1)}, bf16[5,1536,32]{2,1,0:T(8,128)(2,1)}, bf16[5,1536,32]{2,1,0:T(8,128)(2,1)}, bf16[160,1536]{1,0:T(8,128)(2,1)}, ...) custom-call(s32[1,16]{1,0:T(1,128)} %lens.1, ...), custom_call_target="tpu_custom_call" | custom-call | flops 943718400 | bytes 3932160 | tf_op jit(solution)/shard_map/project/pallas_call | solution.py:93
  32.8 22.5 %attend_0.1 = (bf16[4,160,384]{2,1,0:T(8,128)(2,1)}, f32[160,1536]{1,0:T(8,128)}, f32[8,1536]{1,0:T(8,128)}) custom-call(s32[6,2]{1,0:T(8,128)} %get-tuple-element.47.bounds, s32[1536,128]{1,0:T(8,128)} %get-tuple-element.48.segc_ref, s32[8,1536]{1,0:T(8,128)} %get-tuple-element.49.segr_ref, bf16[5,1536,32]{2,1,0:T(8,128)(2,1)} %get-tuple-element.50.k_ref, ...), custom_call_target="tpu_custom_call" | custom-call | flops 3538944000 | bytes 3932160 | tf_op jit(solution)/shard_map/attend_0/pallas_call | solution.py:192
  55.2 14.9 %all_to_all.35 = bf16[4,160,384]{2,1,0:T(8,128)(2,1)} all-to-all(bf16[4,160,384]{2,1,0:T(8,128)(2,1)} %get-tuple-element.53), channel_id=1, replica_groups=mesh['narrow'=4,'wide'=8] {'narrow'}, dimensions={0} | all-to-all | bytes 983040 | tf_op jit(solution)/shard_map/all_to_all | solution.py:525
  71.5 7.1 %all-to-all-start.1 = ((bf16[32,160,80]{2,1,0:T(8,128)(2,1)}), bf16[32,160,80]{2,1,0:T(8,128)(2,1)S(1)}, u32[]{:S(2)}, u32[]{:S(2)}) async-start(bf16[32,160,80]{2,1,0:T(8,128)(2,1)} %broadcast_in_dim.2), calls=%async_computation.1 | async-start | bytes 2621440 | tf_op jit(solution)/shard_map/all_to_all | solution.py:542
  88.9 46.0 %all-to-all-done.1 = bf16[32,160,80]{2,1,0:T(8,128)(2,1)S(1)} async-done(((bf16[32,160,80]{2,1,0:T(8,128)(2,1)}), bf16[32,160,80]{2,1,0:T(8,128)(2,1)S(1)}, u32[]{:S(2)}, u32[]{:S(2)}) %all-to-all-start.1) | async-done | bytes 819232 | tf_op jit(solution)/shard_map/all_to_all | solution.py:542
  135.9 4.2 mix.1
  141.9 2.7 collective-permute-start.7
  146.1 8.3 %ffn.3 = (f32[768,640]{1,0:T(8,128)}, f32[768,640]{1,0:T(8,128)}, bf16[640,640]{1,0:T(8,128)(2,1)}, bf16[640,640]{1,0:T(8,128)(2,1)}) custom-call(bf16[384,640]{1,0:T(8,128)(2,1)} %get-tuple-element.55.refs_0_, bf16[384,640]{1,0:T(8,128)(2,1)} %copy-done.19, bf16[384,640]{1,0:T(8,128)(2,1)} %constant_dynamic-slice_fusion.1.refs_2_.dy_ref, ...), custom_call_target="tpu_custom_call" | custom-call | flops 3774873600 | bytes 7208960 | tf_op jit(solution)/shard_map/ffn/pallas_call | solution.py:416
  154.4 6.7 %collective-permute-done.6.refs_5_ = bf16[640,640]{1,0:T(8,128)(2,1)S(1)} collective-permute-done((bf16[640,640]{1,0:T(8,128)(2,1)S(1)}, bf16[640,640]{1,0:T(8,128)(2,1)S(1)}, u32[]{:S(2)}, u32[]{:S(2)}) %collective-permute-start.6) | collective-permute-done | bytes 819232 | tf_op jit(solution)/shard_map/ppermute | solution.py:521
  164.6 15.5 %ffn.4 = (f32[768,640]{1,0:T(8,128)}, f32[768,640]{1,0:T(8,128)}, bf16[640,640]{1,0:T(8,128)(2,1)}, bf16[640,640]{1,0:T(8,128)(2,1)}, bf16[640,640]{1,0:T(8,128)(2,1)}, /*index=5*/bf16[640,640]{1,0:T(8,128)(2,1)}) custom-call(bf16[384,640]{1,0:T(8,128)(2,1)} %get-tuple-element.55.refs_0_, bf16[384,640]{1,0:T(8,128)(2,1)} %copy-done.19, ...), custom_call_target="tpu_custom_call" | custom-call | flops 7549747200 | bytes 10485760 | tf_op jit(solution)/shard_map/ffn/pallas_call | solution.py:416
  181.9 9.5 %ffn.5 = (f32[384,640]{1,0:T(8,128)}, f32[384,640]{1,0:T(8,128)}, bf16[2,384,640]{2,1,0:T(8,128)(2,1)}, bf16[640,640]{1,0:T(8,128)(2,1)}, bf16[640,640]{1,0:T(8,128)(2,1)}) custom-call(bf16[384,640]{1,0:T(8,128)(2,1)} %get-tuple-element.55.refs_0_, bf16[384,640]{1,0:T(8,128)(2,1)} %copy-done.19, ...), custom_call_target="tpu_custom_call" | custom-call | flops 3774873600 | bytes 7208960 | tf_op jit(solution)/shard_map/ffn/pallas_call | solution.py:416
  191.4 2.8 collective-permute-done.8.far_ref
  195.2 5.5 %turn.1 = (bf16[384,640]{1,0:T(8,128)(2,1)}, f32[384,640]{1,0:T(8,128)}, bf16[640,384]{1,0:T(8,128)(2,1)}, bf16[640,640]{1,0:T(8,128)(2,1)}, f32[8,640]{1,0:T(8,128)}) custom-call(f32[384,640]{1,0:T(8,128)} %get-tuple-element.54.x2_ref, f32[384,640]{1,0:T(8,128)} %get-tuple-element.60.y_ref, f32[384,640]{1,0:T(8,128)} %get-tuple-element.61.dx_ref, ...), custom_call_target="tpu_custom_call" | custom-call | flops 629145600 | bytes 5898240 | tf_op jit(solution)/shard_map/turn/pallas_call | solution.py:463
  204.8 17.3 %collective-permute-done.10 = bf16[640,640]{1,0:T(8,128)(2,1)S(1)} collective-permute-done((bf16[640,640]{1,0:T(8,128)(2,1)}, bf16[640,640]{1,0:T(8,128)(2,1)S(1)}, u32[]{:S(2)}, u32[]{:S(2)}) %collective-permute-start.10) | collective-permute-done | bytes 819232 | tf_op jit(solution)/shard_map/ppermute | solution.py:521
  227.0 3.5 all-to-all-start.2
  230.5 9.1 %collective-permute-done.9 = bf16[640,640]{1,0:T(8,128)(2,1)S(1)} collective-permute-done((bf16[640,640]{1,0:T(8,128)(2,1)}, bf16[640,640]{1,0:T(8,128)(2,1)S(1)}, u32[]{:S(2)}, u32[]{:S(2)}) %collective-permute-start.9) | collective-permute-done | bytes 819232 | tf_op jit(solution)/shard_map/ppermute | solution.py:521
  239.6 5.1 %collective-permute-done.11 = bf16[640,640]{1,0:T(8,128)(2,1)} collective-permute-done((bf16[640,640]{1,0:T(8,128)(2,1)}, bf16[640,640]{1,0:T(8,128)(2,1)}, u32[]{:S(2)}, u32[]{:S(2)}) %collective-permute-start.11) | collective-permute-done | bytes 819232 | tf_op jit(solution)/shard_map/ppermute | solution.py:521
  246.2 13.6 %collective-permute-done.14 = bf16[640,640]{1,0:T(8,128)(2,1)} collective-permute-done((bf16[640,640]{1,0:T(8,128)(2,1)}, bf16[640,640]{1,0:T(8,128)(2,1)}, u32[]{:S(2)}, u32[]{:S(2)}) %collective-permute-start.14) | collective-permute-done | bytes 819232 | tf_op jit(solution)/shard_map/ppermute | solution.py:521
  263.7 34.9 %attend_back_0.1 = (bf16[4,480,384]{2,1,0:T(8,128)(2,1)}, bf16[480,1536]{1,0:T(8,128)(2,1)}) custom-call(s32[6,2]{1,0:T(8,128)} %get-tuple-element.47.bounds, s32[1536,128]{1,0:T(8,128)} %get-tuple-element.48.segc_ref, s32[8,1536]{1,0:T(8,128)} %get-tuple-element.49.segr_ref, bf16[5,1536,32]{2,1,0:T(8,128)(2,1)} %get-tuple-element.65.q_ref, ...), custom_call_target="tpu_custom_call" | custom-call | flops 10616832000 | bytes 3932160 | tf_op jit(solution)/shard_map/attend_back_0/pallas_call | solution.py:289
  298.6 3.6 all-to-all-start.3
  302.2 5.5 %copy.31 = bf16[12,640,160]{2,1,0:T(8,128)(2,1)} copy(bf16[12,640,160]{1,2,0:T(8,128)(2,1)} %all-gather.12.cloned.1.call-done) | data formatting | bytes 4915200 | tf_op jit(solution)/shard_map/all_gather | solution.py:592
  307.7 20.3 %all-to-all-done.3.parts_ref = bf16[4,480,384]{2,1,0:T(8,128)(2,1)S(1)} async-done(((bf16[4,480,384]{2,1,0:T(8,128)(2,1)}), bf16[4,480,384]{2,1,0:T(8,128)(2,1)S(1)}, u32[]{:S(2)}, u32[]{:S(2)}) %all-to-all-start.3) | async-done | bytes 1474592 | tf_op jit(solution)/shard_map/all_to_all | solution.py:525
  329.1 6.5 %finish.1 = (bf16[384,640]{1,0:T(8,128)(2,1)}, f32[8,640]{1,0:T(8,128)}) custom-call(bf16[4,480,384]{2,1,0:T(8,128)(2,1)} %copy-done.2, bf16[4,3,640,160]{3,2,1,0:T(8,128)(2,1)} %bitcast.13, bf16[384,640]{1,0:T(8,128)(2,1)} %constant_dynamic-slice_fusion.2.x_ref, f32[384,640]{1,0:T(8,128)} %get-tuple-element.71.dx2_ref, bf16[2,640]{1,0:T(2,128)(2,1)} %gain_ref.7), custom_call_target="tpu_custom_call" | custom-call | flops 943718400 | bytes 3932160 | tf_op jit(solution)/shard_map/finish/pallas_call | solution.py:504
  335.6 22.8 %all_to_all.36 = bf16[8,80,640]{2,1,0:T(8,128)(2,1)S(1)} all-to-all(bf16[8,80,640]{2,1,0:T(8,128)(2,1)S(1)} %bitcast.18), channel_id=1, replica_groups=mesh['narrow'=4,'wide'=8] {'wide'}, dimensions={0} | all-to-all | bytes 1638400 | tf_op jit(solution)/shard_map/all_to_all | solution.py:525
  359.4 3.3 all-to-all-start.6
  362.8 2.9 convolution_convert_fusion
  366.7 8.0 %all-to-all-done.6 = bf16[4,80,160]{2,1,0:T(8,128)(2,1)S(1)} async-done(((bf16[4,80,160]{2,1,0:T(8,128)(2,1)}), bf16[4,80,160]{2,1,0:T(8,128)(2,1)S(1)}, u32[]{:S(2)}, u32[]{:S(2)}) %all-to-all-start.6) | async-done | bytes 102432 | tf_op jit(solution)/shard_map/all_to_all | solution.py:525
  374.7 3.5 all-to-all-start.4
  379.7 9.6 %all-to-all-done.4 = bf16[8,80,480]{2,1,0:T(8,128)(2,1)S(1)} async-done(((bf16[8,80,480]{2,1,0:T(8,128)(2,1)}), bf16[8,80,480]{2,1,0:T(8,128)(2,1)S(1)}, u32[]{:S(2)}, u32[]{:S(2)}) %all-to-all-start.4) | async-done | bytes 614432 | tf_op jit(solution)/shard_map/all_to_all | solution.py:525
  391.1 37.5 %psum.7 = f32[4,640]{1,0:T(4,128)S(1)} all-reduce(f32[4,640]{1,0:T(4,128)S(1)} %pad_maximum_fusion.2), channel_id=1, replica_groups=mesh['narrow'=4,'wide'=8] {'narrow','wide'}, use_global_device_ids=true, to_apply=%region_0.0 | all-reduce | flops 2560 | bytes 20480 | tf_op jit(solution)/shard_map/psum | solution.py:634
  431.9 3.1 copy.39
  (109 shorter events, 49.7 us)
Async XLA Ops:
  7.2 74.0 %copy-start = (bf16[1536,640]{1,0:T(8,128)(2,1)S(1)}, bf16[1536,640]{1,0:T(8,128)(2,1)}, u32[]{:S(2)}) copy-start(bf16[1536,640]{1,0:T(8,128)(2,1)} %param.10) | copy-start | bytes 5898244
  7.2 75.1 %all-gather.6.cloned.1.call-start = ((), (), s32[]{:S(2)}) async-start(), calls=%async_computation.8 | async-start | bytes 2048000 | tf_op jit(solution)/shard_map/all_gather | solution.py:546
  32.8 37.4 %copy-start.14 = (bf16[160,80]{1,0:T(8,128)(2,1)S(1)}, bf16[160,80]{1,0:T(8,128)(2,1)}, u32[]{:S(2)}) copy-start(bf16[160,80]{1,0:T(8,128)(2,1)} %param.15) | copy-start | bytes 76804
  71.5 63.4 %all-to-all-start.1 = ((bf16[32,160,80]{2,1,0:T(8,128)(2,1)}), bf16[32,160,80]{2,1,0:T(8,128)(2,1)S(1)}, u32[]{:S(2)}, u32[]{:S(2)}) async-start(bf16[32,160,80]{2,1,0:T(8,128)(2,1)} %broadcast_in_dim.2), calls=%async_computation.1 | async-start | bytes 2621440 | tf_op jit(solution)/shard_map/all_to_all | solution.py:542
  78.5 223.7 %all-gather.12.cloned.1.call-start = ((), (), s32[]{:S(2)}) async-start(), calls=%async_computation.12 | async-start | bytes 3072000 | tf_op jit(solution)/shard_map/all_gather | solution.py:592
  80.9 349.0 %all-gather.8.cloned.1.call-start = ((), (), s32[]{:S(2)}) async-start(), calls=%async_computation.9 | async-start | bytes 2457600 | tf_op jit(solution)/shard_map/all_gather | solution.py:586
  82.0 59.9 %collective-permute-start.1 = (bf16[384,640]{1,0:T(8,128)(2,1)}, bf16[384,640]{1,0:T(8,128)(2,1)}, u32[]{:S(2)}, u32[]{:S(2)}) collective-permute-start(bf16[384,640]{1,0:T(8,128)(2,1)} %constant_dynamic-slice_fusion.1.refs_2_.dy_ref), channel_id=1, source_target_pairs={{0,1},{1,0},{2,3},{3,2},{4,5},{5,4},{6,7},{7,6},{8,9},{9,8},{10,11... | collective-permute-start | bytes 1474568 | tf_op jit(solution)/shard_map/ppermute | solution.py:521
  83.8 58.1 %copy-start.11 = (bf16[640,640]{1,0:T(8,128)(2,1)}, bf16[640,640]{1,0:T(8,128)(2,1)S(1)}, u32[]{:S(2)}) copy-start(bf16[640,640]{1,0:T(8,128)(2,1)S(1)} %get-tuple-element.119.refs_4_) | copy-start | bytes 2457604
  83.8 61.5 %copy-start.12 = (bf16[640,640]{1,0:T(8,128)(2,1)}, bf16[640,640]{1,0:T(8,128)(2,1)S(1)}, u32[]{:S(2)}) copy-start(bf16[640,640]{1,0:T(8,128)(2,1)S(1)} %get-tuple-element.118.refs_5_) | copy-start | bytes 2457604
  83.8 60.8 %collective-permute-start.2 = (bf16[640,640]{1,0:T(8,128)(2,1)S(1)}, bf16[640,640]{1,0:T(8,128)(2,1)}, u32[]{:S(2)}, u32[]{:S(2)}) collective-permute-start(bf16[640,640]{1,0:T(8,128)(2,1)S(1)} %get-tuple-element.119.refs_4_), channel_id=1, source_target_pairs={{0,2},{1,3},{2,0},{3,1},{4,6},{5,7},{6,4},{7,5},{8,10},{9,11},{10,... | collective-permute-start | bytes 2457608 | tf_op jit(solution)/shard_map/ppermute | solution.py:521
  85.5 59.1 %collective-permute-start.4 = (bf16[640,640]{1,0:T(8,128)(2,1)S(1)}, bf16[640,640]{1,0:T(8,128)(2,1)}, u32[]{:S(2)}, u32[]{:S(2)}) collective-permute-start(bf16[640,640]{1,0:T(8,128)(2,1)S(1)} %get-tuple-element.118.refs_5_), channel_id=1, source_target_pairs={{0,4},{1,5},{2,6},{3,7},{4,0},{5,1},{6,2},{7,3},{8,12},{9,13},{10,... | collective-permute-start | bytes 2457608 | tf_op jit(solution)/shard_map/ppermute | solution.py:521
  140.1 5.2 %collective-permute-start = (bf16[384,640]{1,0:T(8,128)(2,1)}, bf16[384,640]{1,0:T(8,128)(2,1)S(1)}, u32[]{:S(2)}, u32[]{:S(2)}) collective-permute-start(bf16[384,640]{1,0:T(8,128)(2,1)} %get-tuple-element.55.refs_0_), channel_id=1, source_target_pairs={{0,1},{1,0},{2,3},{3,2},{4,5},{5,4},{6,7},{7,6},{8,9},{9,8},{10,11... | collective-permute-start | bytes 1474568 | tf_op jit(solution)/shard_map/ppermute | solution.py:521
  140.1 21.0 %collective-permute-start.6 = (bf16[640,640]{1,0:T(8,128)(2,1)S(1)}, bf16[640,640]{1,0:T(8,128)(2,1)S(1)}, u32[]{:S(2)}, u32[]{:S(2)}) collective-permute-start(bf16[640,640]{1,0:T(8,128)(2,1)S(1)} %get-tuple-element.118.refs_5_), channel_id=1, source_target_pairs={{0,2},{1,3},{2,0},{3,1},{4,6},{5,7},{6,4},{7,5},{8,10},{9,11},{10,... | collective-permute-start | bytes 2457608 | tf_op jit(solution)/shard_map/ppermute | solution.py:521
  141.9 21.7 %collective-permute-start.7 = (bf16[640,640]{1,0:T(8,128)(2,1)S(1)}, bf16[640,640]{1,0:T(8,128)(2,1)S(1)}, u32[]{:S(2)}, u32[]{:S(2)}) collective-permute-start(bf16[640,640]{1,0:T(8,128)(2,1)S(1)} %get-tuple-element.119.refs_4_), channel_id=1, source_target_pairs={{0,4},{1,5},{2,6},{3,7},{4,0},{5,1},{6,2},{7,3},{8,12},{9,13},{10,... | collective-permute-start | bytes 2457608 | tf_op jit(solution)/shard_map/ppermute | solution.py:521
  144.6 36.2 %collective-permute-start.3 = (bf16[640,640]{1,0:T(8,128)(2,1)}, bf16[640,640]{1,0:T(8,128)(2,1)S(1)}, u32[]{:S(2)}, u32[]{:S(2)}) collective-permute-start(bf16[640,640]{1,0:T(8,128)(2,1)} %collective-permute-done.2.refs_4_), channel_id=1, source_target_pairs={{0,4},{1,5},{2,6},{3,7},{4,0},{5,1},{6,2},{7,3},{8,12},{9,13},{10,... | collective-permute-start | bytes 2457608 | tf_op jit(solution)/shard_map/ppermute | solution.py:521
  144.7 36.1 %collective-permute-start.5 = (bf16[640,640]{1,0:T(8,128)(2,1)}, bf16[640,640]{1,0:T(8,128)(2,1)S(1)}, u32[]{:S(2)}, u32[]{:S(2)}) collective-permute-start(bf16[640,640]{1,0:T(8,128)(2,1)} %collective-permute-done.4.refs_7_), channel_id=1, source_target_pairs={{0,2},{1,3},{2,0},{3,1},{4,6},{5,7},{6,4},{7,5},{8,10},{9,11},{10,... | collective-permute-start | bytes 2457608 | tf_op jit(solution)/shard_map/ppermute | solution.py:521
  191.4 2.8 collective-permute-start.8
  195.2 26.9 %copy-start.10 = (bf16[640,640]{1,0:T(8,128)(2,1)S(1)}, bf16[640,640]{1,0:T(8,128)(2,1)}, u32[]{:S(2)}) copy-start(bf16[640,640]{1,0:T(8,128)(2,1)} %get-tuple-element.80) | copy-start | bytes 2457604
  200.7 24.6 %copy-start.9 = (bf16[640,640]{1,0:T(8,128)(2,1)S(1)}, bf16[640,640]{1,0:T(8,128)(2,1)}, u32[]{:S(2)}) copy-start(bf16[640,640]{1,0:T(8,128)(2,1)} %get-tuple-element.83) | copy-start | bytes 2457604
  200.7 21.4 %collective-permute-start.10 = (bf16[640,640]{1,0:T(8,128)(2,1)}, bf16[640,640]{1,0:T(8,128)(2,1)S(1)}, u32[]{:S(2)}, u32[]{:S(2)}) collective-permute-start(bf16[640,640]{1,0:T(8,128)(2,1)} %get-tuple-element.81), channel_id=1, source_target_pairs={{0,2},{1,3},{2,0},{3,1},{4,6},{5,7},{6,4},{7,5},{8,10},{9,11},{10,... | collective-permute-start | bytes 2457608 | tf_op jit(solution)/shard_map/ppermute | solution.py:521
  201.4 23.8 %collective-permute-start.12 = (bf16[640,640]{1,0:T(8,128)(2,1)}, bf16[640,640]{1,0:T(8,128)(2,1)S(1)}, u32[]{:S(2)}, u32[]{:S(2)}) collective-permute-start(bf16[640,640]{1,0:T(8,128)(2,1)} %get-tuple-element.84), channel_id=1, source_target_pairs={{0,4},{1,5},{2,6},{3,7},{4,0},{5,1},{6,2},{7,3},{8,12},{9,13},{10,... | collective-permute-start | bytes 2457608 | tf_op jit(solution)/shard_map/ppermute | solution.py:521
  203.2 36.5 %collective-permute-start.9 = (bf16[640,640]{1,0:T(8,128)(2,1)}, bf16[640,640]{1,0:T(8,128)(2,1)S(1)}, u32[]{:S(2)}, u32[]{:S(2)}) collective-permute-start(bf16[640,640]{1,0:T(8,128)(2,1)} %get-tuple-element.79), channel_id=1, source_target_pairs={{0,2},{1,3},{2,0},{3,1},{4,6},{5,7},{6,4},{7,5},{8,10},{9,11},{10,... | collective-permute-start | bytes 2457608 | tf_op jit(solution)/shard_map/ppermute | solution.py:521
  223.2 21.5 %collective-permute-start.11 = (bf16[640,640]{1,0:T(8,128)(2,1)}, bf16[640,640]{1,0:T(8,128)(2,1)}, u32[]{:S(2)}, u32[]{:S(2)}) collective-permute-start(bf16[640,640]{1,0:T(8,128)(2,1)} %add_convert_fusion.3), channel_id=1, source_target_pairs={{0,4},{1,5},{2,6},{3,7},{4,0},{5,1},{6,2},{7,3},{8,12},{9,13},{10,... | collective-permute-start | bytes 2457608 | tf_op jit(solution)/shard_map/ppermute | solution.py:521
  225.0 34.9 %collective-permute-start.14 = (bf16[640,640]{1,0:T(8,128)(2,1)}, bf16[640,640]{1,0:T(8,128)(2,1)}, u32[]{:S(2)}, u32[]{:S(2)}) collective-permute-start(bf16[640,640]{1,0:T(8,128)(2,1)} %get-tuple-element.85), channel_id=1, source_target_pairs={{0,4},{1,5},{2,6},{3,7},{4,0},{5,1},{6,2},{7,3},{8,12},{9,13},{10,... | collective-permute-start | bytes 2457608 | tf_op jit(solution)/shard_map/ppermute | solution.py:521
  225.2 19.5 %copy-start.8 = (bf16[640,640]{1,0:T(8,128)(2,1)S(1)}, bf16[640,640]{1,0:T(8,128)(2,1)}, u32[]{:S(2)}) copy-start(bf16[640,640]{1,0:T(8,128)(2,1)} %get-tuple-element.78) | copy-start | bytes 2457604
  226.4 33.5 %collective-permute-start.13 = (bf16[640,640]{1,0:T(8,128)(2,1)}, bf16[640,640]{1,0:T(8,128)(2,1)}, u32[]{:S(2)}, u32[]{:S(2)}) collective-permute-start(bf16[640,640]{1,0:T(8,128)(2,1)} %add_convert_fusion.1), channel_id=1, source_target_pairs={{0,2},{1,3},{2,0},{3,1},{4,6},{5,7},{6,4},{7,5},{8,10},{9,11},{10,... | collective-permute-start | bytes 2457608 | tf_op jit(solution)/shard_map/ppermute | solution.py:521
  227.0 35.9 %all-to-all-start.2 = ((bf16[4,160,384]{2,1,0:T(8,128)(2,1)}), bf16[4,160,384]{2,1,0:T(8,128)(2,1)S(1)}, u32[]{:S(2)}, u32[]{:S(2)}) async-start(bf16[4,160,384]{2,1,0:T(8,128)(2,1)} %bitcast.2), calls=%async_computation.2 | async-start | bytes 983040 | tf_op jit(solution)/shard_map/all_to_all | solution.py:525
  230.5 199.5 %reduce-scatter.2.cloned.1.call-start = ((), (), s32[]{:S(2)}) async-start(), calls=%async_computation.11 | async-start | bytes 2048000 | tf_op jit(solution)/shard_map/reduce_scatter | solution.py:619
  298.6 29.4 %all-to-all-start.3 = ((bf16[4,480,384]{2,1,0:T(8,128)(2,1)}), bf16[4,480,384]{2,1,0:T(8,128)(2,1)S(1)}, u32[]{:S(2)}, u32[]{:S(2)}) async-start(bf16[4,480,384]{2,1,0:T(8,128)(2,1)} %get-tuple-element.70), calls=%async_computation.3 | async-start | bytes 2949120 | tf_op jit(solution)/shard_map/all_to_all | solution.py:525
  302.1 129.8 %all-gather.10.cloned.1.call-start = ((), (), s32[]{:S(2)}) async-start(), calls=%async_computation.10 | async-start | bytes 2457600 | tf_op jit(solution)/shard_map/all_gather | solution.py:595
  359.4 15.3 %all-to-all-start.6 = ((bf16[4,80,160]{2,1,0:T(8,128)(2,1)}), bf16[4,80,160]{2,1,0:T(8,128)(2,1)S(1)}, u32[]{:S(2)}, u32[]{:S(2)}) async-start(bf16[4,80,160]{2,1,0:T(8,128)(2,1)} %copy.34), calls=%async_computation.6 | async-start | bytes 327680 | tf_op jit(solution)/shard_map/all_to_all | solution.py:525
  374.7 14.6 %all-to-all-start.4 = ((bf16[8,80,480]{2,1,0:T(8,128)(2,1)}), bf16[8,80,480]{2,1,0:T(8,128)(2,1)S(1)}, u32[]{:S(2)}, u32[]{:S(2)}) async-start(bf16[8,80,480]{2,1,0:T(8,128)(2,1)} %bitcast.4), calls=%async_computation.4 | async-start | bytes 1310720 | tf_op jit(solution)/shard_map/all_to_all | solution.py:525
  (14 other events, 43.8 us)
Sparse Core Ops, SparseCore 0:
  10.2 40.8 all-gather.5
  81.0 69.2 all-gather.11
  200.8 51.0 all-gather.7
  263.0 34.0 reduce-scatter.1
  335.7 52.5 all-gather.9

commit v2 on v1

v2 whole, which is shorter than its diff:
```python
from functools import partial

import jax
import jax.numpy as jnp
from jax import lax
from jax.experimental import pallas as pl
from jax.experimental.pallas import tpu as pltpu
from jax.sharding import PartitionSpec as P

HD = 32
EPS = 1e-05
LOG2E = 1.4426950408889634
SCALE = HD ** (-0.5)
BQ = 256
BK = 256
STEP = 256
BF16 = jnp.bfloat16
F32 = jnp.float32
VMEM_LIMIT = 56 * 1024 * 1024
COST = pl.CostEstimate(flops=1000000, bytes_accessed=100000, transcendentals=0)


def vmem(*shape):
    return pl.BlockSpec(shape, None) if shape else pl.BlockSpec(memory_space=pltpu.VMEM)


def dot(a, b):
    return jnp.dot(a, b, preferred_element_type=F32)


def dot_nt(a, b):
    return lax.dot_general(a, b, (((1,), (1,)), ((), ())), preferred_element_type=F32)


def normalized(rows):
    center = rows - jnp.mean(rows, axis=-1, keepdims=True)
    spread = jnp.mean(center * center, axis=-1, keepdims=True)
    inverse = lax.rsqrt(spread + EPS)
    return center * inverse, inverse


def norm_backward(rows, gain, grad):
    unit, inverse = normalized(rows)
    scaled = grad * gain
    inner = scaled - jnp.mean(scaled, axis=-1, keepdims=True)
    inner = inner - unit * jnp.mean(scaled * unit, axis=-1, keepdims=True)
    return inverse * inner, grad * unit


def project_kernel(
    lens, x_ref, gain_ref, shift_ref, w_ref,
    unit_ref, q_ref, k_ref, qt_ref, kt_ref, vt_ref, segc_ref, segr_ref, bounds_ref, full_ref, out_ref,
):
    across, kinds, _, narrow = w_ref.shape

    @pl.when(pl.program_id(0) == 0)
    def _():
        for part in range(across):
            spot = slice(part * narrow, (part + 1) * narrow)
            for item in range(kinds - 1):
                full_ref[item, :, spot] = w_ref[part, item]
            for copy in range(out_ref.shape[0]):
                out_ref[copy, :, spot] = w_ref[part, kinds - 1]

    block = pl.program_id(0)
    first = block * BQ
    last = first + BQ - 1
    heads = q_ref.shape[0]
    end = jnp.int32(0)
    low = jnp.int32(0)
    high = jnp.int32(pl.num_programs(0) * BQ)
    rows = first + lax.broadcasted_iota(jnp.int32, segc_ref.shape, 0)
    cols = first + lax.broadcasted_iota(jnp.int32, segr_ref.shape, 1)
    seg_rows = jnp.zeros(segc_ref.shape, jnp.int32)
    seg_cols = jnp.zeros(segr_ref.shape, jnp.int32)
    for item in range(lens.shape[1]):
        end = end + lens[0, item]
        low = jnp.where(end <= first, end, low)
        high = jnp.where((end > last) & (end < high), end, high)
        seg_rows = seg_rows + (rows >= end).astype(jnp.int32)
        seg_cols = seg_cols + (cols >= end).astype(jnp.int32)
    segc_ref[...] = seg_rows
    segr_ref[...] = seg_cols
    low = lax.div(low, jnp.int32(STEP))
    high = lax.div(high + (STEP - 1), jnp.int32(STEP))
    steps = lax.div((high - low) * STEP + (BK - 1), jnp.int32(BK))
    room = pl.num_programs(0) * (BQ // STEP) - steps * (BK // STEP)
    bounds_ref[block, 0] = jnp.minimum(low, room)
    bounds_ref[block, 1] = steps
    unit, _ = normalized(x_ref[...].astype(F32))
    xn = (unit * gain_ref[0:1, :].astype(F32) + shift_ref[0:1, :].astype(F32)).astype(BF16)
    unit_ref[...] = unit.astype(BF16)
    for item, (rows_ref, cols_ref) in enumerate(((q_ref, qt_ref), (k_ref, kt_ref), (None, vt_ref))):
        cols_ref[...] = dot_nt(full_ref[item], xn).astype(BF16)
        if rows_ref is not None:
            full = dot_nt(xn, full_ref[item]).astype(BF16)
            for head in range(heads):
                rows_ref[head] = full[:, head * HD : (head + 1) * HD]


def project(lens, tokens, gains, shifts, weights, depth):
    count, dim = tokens.shape
    width = weights.shape[2]
    heads = width // HD
    blocks = count // BQ
    per_head = pl.BlockSpec((heads, BQ, HD), lambda i: (0, i, 0))
    turned = pl.BlockSpec((width, BQ), lambda i: (0, i))
    fixed2 = pl.BlockSpec((2, dim), lambda i: (0, 0))
    return pl.pallas_call(
        project_kernel,
        grid=(blocks,),
        in_specs=[
            pl.BlockSpec(memory_space=pltpu.SMEM),
            pl.BlockSpec((BQ, dim), lambda i: (i, 0)),
            fixed2,
            fixed2,
            pl.BlockSpec(weights.shape, lambda i: (0, 0, 0, 0)),
        ],
        out_specs=[
            pl.BlockSpec((BQ, dim), lambda i: (i, 0)),
            per_head,
            per_head,
            turned,
            turned,
            turned,
            pl.BlockSpec((BQ, 128), lambda i: (i, 0)),
            pl.BlockSpec((8, BQ), lambda i: (0, i)),
            pl.BlockSpec(memory_space=pltpu.SMEM),
            pl.BlockSpec((3, width, dim), lambda i: (0, 0, 0)),
            pl.BlockSpec((depth, width, dim), lambda i: (0, 0, 0)),
        ],
        out_shape=[
            jax.ShapeDtypeStruct((count, dim), BF16),
            jax.ShapeDtypeStruct((heads, count, HD), BF16),
            jax.ShapeDtypeStruct((heads, count, HD), BF16),
            jax.ShapeDtypeStruct((width, count), BF16),
            jax.ShapeDtypeStruct((width, count), BF16),
            jax.ShapeDtypeStruct((width, count), BF16),
            jax.ShapeDtypeStruct((count, 128), jnp.int32),
            jax.ShapeDtypeStruct((8, count), jnp.int32),
            jax.ShapeDtypeStruct((blocks, 2), jnp.int32),
            jax.ShapeDtypeStruct((3, width, dim), BF16),
            jax.ShapeDtypeStruct((depth, width, dim), BF16),
        ],
        compiler_params=pltpu.CompilerParams(vmem_limit_bytes=VMEM_LIMIT),
        cost_estimate=COST,
        name="project",
    )(lens, tokens, gains, shifts, weights)


def spread_lanes(column, width):
    return jnp.concatenate([column] * (width // 128), axis=1) if width > 128 else column


def spot_of(layer, item, size):
    return pl.ds(pl.multiple_of((layer[0] ^ item) * size, 128), size)


def attend_kernel(
    first, heads, parts, layer, bounds, segc_ref, segr_ref, k_ref, qt_ref, vt_ref, *refs
):
    part_refs, (ot_ref, lse_ref) = refs[:parts], refs[parts:]
    count = segc_ref.shape[0]
    factor = SCALE * LOG2E

    def q_block(block, _):
        start = pl.multiple_of(block * BQ, BQ)
        seg_q = segr_ref[0:1, pl.ds(start, BQ)]
        queries = [
            qt_ref[(first + h) * HD : (first + h + 1) * HD, pl.ds(start, BQ)] for h in range(heads)
        ]

        def k_block(item, carry):
            at = pl.multiple_of(bounds[block, 0] * STEP + item * BK, STEP)
            allowed = spread_lanes(segc_ref[pl.ds(at, BK), :], BQ) == seg_q
            out = []
            scores = [dot(k_ref[first + h, pl.ds(at, BK), :], queries[h]) for h in range(heads)]
            scores = [jnp.where(allowed, value, -1e30) for value in scores]
            fresh = [
                jnp.maximum(carry[h][0], jnp.max(scores[h], axis=0, keepdims=True))
                for h in range(heads)
            ]
            expd = [jnp.exp2((scores[h] - fresh[h]) * factor) for h in range(heads)]
            for h in range(heads):
                top, total, acc = carry[h]
                fade = jnp.exp2((top - fresh[h]) * factor)
                total = total * fade + jnp.sum(expd[h], axis=0, keepdims=True)
                rows = vt_ref[(first + h) * HD : (first + h + 1) * HD, pl.ds(at, BK)]
                acc = acc * fade + dot(rows, expd[h].astype(BF16))
                out.append((fresh[h], total, acc))
            return tuple(out)

        empty = (
            jnp.full((1, BQ), -1e30, F32),
            jnp.zeros((1, BQ), F32),
            jnp.zeros((HD, BQ), F32),
        )
        done = lax.fori_loop(0, bounds[block, 1], k_block, (empty,) * heads)
        for h in range(heads):
            top, total, acc = done[h]
            ot_ref[h * HD : (h + 1) * HD, pl.ds(start, BQ)] = acc / total
            lse_ref[h : h + 1, pl.ds(start, BQ)] = top * factor + jnp.log(total) * LOG2E
        return 0

    lax.fori_loop(0, count // BQ, q_block, 0)
    size = count // parts
    for part in range(parts):
        part_refs[part][...] = ot_ref[:, spot_of(layer, part, size)].astype(BF16)


def attend(first, heads, parts, layer, tables, k_rows, q_cols, v_cols):
    segc, segr, bounds = tables
    count = segc.shape[0]
    out = pl.pallas_call(
        partial(attend_kernel, first, heads, parts),
        in_specs=[pl.BlockSpec(memory_space=pltpu.SMEM)] * 2 + [vmem()] * 5,
        out_specs=[vmem()] * (parts + 2),
        out_shape=[jax.ShapeDtypeStruct((heads * HD, count // parts), BF16)] * parts
        + [
            jax.ShapeDtypeStruct((heads * HD, count), F32),
            jax.ShapeDtypeStruct((8, count), F32),
        ],
        compiler_params=pltpu.CompilerParams(vmem_limit_bytes=VMEM_LIMIT),
        cost_estimate=COST,
        name=f"attend_{first}",
    )(layer, bounds, segc, segr, k_rows, q_cols, v_cols)
    return out[:parts], out[parts], out[parts + 1]


def attend_back_kernel(
    first, heads, parts, layer, bounds, segc_ref, segr_ref,
    q_ref, k_ref, qt_ref, kt_ref, vt_ref, ot_ref, lse_ref, *refs,
):
    part_refs, out_refs, refs = refs[:parts], refs[parts : 2 * parts], refs[2 * parts :]
    flat_ref, dot_ref, do_ref, stat_ref, dq_ref, dqt_ref, dkt_ref, dvt_ref = refs
    count = segc_ref.shape[0]
    factor = SCALE * LOG2E
    size = count // parts
    for part in range(parts):
        value = part_refs[part][first * HD : (first + heads) * HD, :]
        dot_ref[:, spot_of(layer, part, size)] = value
        for h in range(heads):
            do_ref[h, spot_of(layer, part, size), :] = value[h * HD : (h + 1) * HD, :].T
    dkt_ref[...] = jnp.zeros_like(dkt_ref)
    dvt_ref[...] = jnp.zeros_like(dvt_ref)

    def q_block(block, _):
        start = pl.multiple_of(block * BQ, BQ)
        spot = pl.ds(start, BQ)
        stats = [lse_ref[0:heads, spot]]
        for h in range(heads):
            lane = slice(h * HD, (h + 1) * HD)
            stats.append(
                jnp.sum(dot_ref[lane, spot].astype(F32) * ot_ref[lane, spot], axis=0, keepdims=True)
            )
        stats.append(jnp.zeros((8 - 2 * heads, BQ), F32)) if heads < 4 else None
        turned = jnp.concatenate(stats, axis=0).T
        for h in range(2 * heads):
            stat_ref[h] = jnp.broadcast_to(turned[:, h : h + 1], (BQ, 128))
        dq_ref[...] = jnp.zeros_like(dq_ref)
        seg_q = spread_lanes(segc_ref[spot, :], BK)

        def k_block(item, _):
            at = pl.multiple_of(bounds[block, 0] * STEP + item * BK, STEP)
            here = pl.ds(at, BK)
            allowed = seg_q == segr_ref[0:1, here]
            lanes = [slice(h * HD, (h + 1) * HD) for h in range(heads)]
            owns = [slice((first + h) * HD, (first + h + 1) * HD) for h in range(heads)]
            scores = [dot(q_ref[first + h, spot, :], kt_ref[owns[h], here]) for h in range(heads)]
            dprob = [dot(do_ref[h, spot, :], vt_ref[owns[h], here]) for h in range(heads)]
            prob = [
                jnp.where(
                    allowed, jnp.exp2(scores[h] * factor - spread_lanes(stat_ref[h], BK)), 0.0
                )
                for h in range(heads)
            ]
            dscore = [
                (prob[h] * (dprob[h] - spread_lanes(stat_ref[heads + h], BK))).astype(BF16)
                for h in range(heads)
            ]
            for h in range(heads):
                dvt_ref[lanes[h], here] += dot(dot_ref[lanes[h], spot], prob[h].astype(BF16))
                dkt_ref[lanes[h], here] += dot(qt_ref[owns[h], spot], dscore[h])
                dq_ref[h] += dot(dscore[h], k_ref[first + h, here, :])
            return 0

        lax.fori_loop(0, bounds[block, 1], k_block, 0)
        for h in range(heads):
            dqt_ref[h * HD : (h + 1) * HD, spot] = dq_ref[h].T * SCALE
        return 0

    lax.fori_loop(0, count // BQ, q_block, 0)
    width = heads * HD
    for item, (source, scale) in enumerate(((dqt_ref, 1.0), (dkt_ref, SCALE), (dvt_ref, 1.0))):
        value = source[...] if scale == 1.0 else source[...] * scale
        value = value.astype(BF16)
        flat_ref[item * width : (item + 1) * width, :] = value
    for part in range(parts):
        out_refs[part][...] = flat_ref[:, spot_of(layer, part, size)]


def attend_back(first, heads, layer, tables, q_rows, k_rows, q_cols, k_cols, v_cols, out, lse, dout):
    segc, segr, bounds = tables
    count = segc.shape[0]
    parts = len(dout)
    width = heads * HD
    result = pl.pallas_call(
        partial(attend_back_kernel, first, heads, parts),
        in_specs=[pl.BlockSpec(memory_space=pltpu.SMEM)] * 2 + [vmem()] * (9 + parts),
        out_specs=[vmem()] * (parts + 1),
        out_shape=[jax.ShapeDtypeStruct((3 * width, count // parts), BF16)] * parts
        + [jax.ShapeDtypeStruct((3 * width, count), BF16)],
        scratch_shapes=[
            pltpu.VMEM((width, count), BF16),
            pltpu.VMEM((heads, count, HD), BF16),
            pltpu.VMEM((2 * heads, BQ, 128), F32),
            pltpu.VMEM((heads, BQ, HD), F32),
            pltpu.VMEM((width, count), F32),
            pltpu.VMEM((width, count), F32),
            pltpu.VMEM((width, count), F32),
        ],
        compiler_params=pltpu.CompilerParams(vmem_limit_bytes=VMEM_LIMIT),
        cost_estimate=COST,
        name=f"attend_back_{first}",
    )(layer, bounds, segc, segr, q_rows, k_rows, q_cols, k_cols, v_cols, out, lse, *dout)
    return result[:parts], result[parts]


def mix_kernel(parts, layer, *refs):
    ot_refs, w_ref, refs = refs[:parts], refs[parts], refs[parts + 1 :]
    x_ref, gain_ref, shift_ref, x2_ref, xn_ref, ot_ref = refs
    middle = x_ref[...].astype(F32)
    for part in range(parts):
        value = ot_refs[part][...]
        ot_ref[layer[0] ^ part] = value
        middle = middle + dot(value.T, w_ref[layer[0] ^ part])
    x2_ref[...] = middle
    unit, _ = normalized(middle)
    xn_ref[...] = (unit * gain_ref[1:2, :].astype(F32) + shift_ref[1:2, :].astype(F32)).astype(BF16)


def mix(layer, ot, w_out, rows, gains, shifts):
    count, dim = rows.shape
    parts = len(ot)
    return pl.pallas_call(
        partial(mix_kernel, parts),
        in_specs=[pl.BlockSpec(memory_space=pltpu.SMEM)] + [vmem()] * (parts + 4),
        out_specs=[vmem()] * 3,
        out_shape=[
            jax.ShapeDtypeStruct((count, dim), F32),
            jax.ShapeDtypeStruct((count, dim), BF16),
            jax.ShapeDtypeStruct((parts,) + ot[0].shape, BF16),
        ],
        compiler_params=pltpu.CompilerParams(vmem_limit_bytes=VMEM_LIMIT),
        cost_estimate=COST,
        name="mix",
    )(layer, *ot, w_out, rows, gains, shifts)


ROWS = 256


def ffn_kernel(*refs):
    xn_parts, dy_parts, w_ref = refs[:2], refs[2:4], refs[4]
    y_out, dx_out, y_far, dx_far, g_ref, du_ref = refs[5:11]
    y_ref, dx_ref, xn_ref, dy_ref = refs[11:]
    item = pl.program_id(0)
    mine = xn_parts[0].shape[0]
    count, hidden = g_ref.shape

    @pl.when(item == 0)
    def _():
        for part in range(2):
            xn_ref[part * mine : (part + 1) * mine, :] = xn_parts[part][...]
            dy_ref[part * mine : (part + 1) * mine, :] = dy_parts[part][...]
        y_ref[...] = jnp.zeros_like(y_ref)
        dx_ref[...] = jnp.zeros_like(dx_ref)

    w_in = w_ref.at[:, :hidden]
    w_down = w_ref.at[:, hidden:]
    for first in range(0, count, ROWS):
        rows = slice(first, first + ROWS)
        u = dot(xn_ref[rows, :], w_in[...])
        dg = dot(dy_ref[rows, :], w_down[...])
        half = 0.5 + 0.5 * lax.erf(u * 0.7071067811865476)
        slope = half + u * (jnp.exp2(u * u * (-0.5 * LOG2E)) * 0.3989422804014327)
        g = (u * half).astype(BF16)
        du = (dg * slope).astype(BF16)
        g_ref[rows, :] = g
        du_ref[rows, :] = du
        y_ref[rows, :] += dot_nt(g, w_down[...])
        dx_ref[rows, :] += dot_nt(du, w_in[...])

    @pl.when(item == pl.num_programs(0) - 1)
    def _():
        y_out[...] = y_ref[:mine, :]
        dx_out[...] = dx_ref[:mine, :]
        y_far[...] = y_ref[mine:, :].astype(BF16)
        dx_far[...] = dx_ref[mine:, :].astype(BF16)


def ffn(xn, dy, weights):
    mine, dim = xn[0].shape
    count = 2 * mine
    blocks = weights.shape[0] // dim
    hidden = weights.shape[1] // 2
    whole = pl.BlockSpec((mine, dim), lambda i: (0, 0))
    act = pl.BlockSpec((count, hidden), lambda i: (0, i))
    return pl.pallas_call(
        ffn_kernel,
        grid=(blocks,),
        in_specs=[whole] * 4 + [pl.BlockSpec((dim, 2 * hidden), lambda i: (i, 0))],
        out_specs=[whole] * 4 + [act] * 2,
        out_shape=[jax.ShapeDtypeStruct((mine, dim), F32)] * 2
        + [jax.ShapeDtypeStruct((mine, dim), BF16)] * 2
        + [jax.ShapeDtypeStruct((count, blocks * hidden), BF16)] * 2,
        scratch_shapes=[pltpu.VMEM((count, dim), F32)] * 2 + [pltpu.VMEM((count, dim), BF16)] * 2,
        compiler_params=pltpu.CompilerParams(vmem_limit_bytes=VMEM_LIMIT),
        cost_estimate=COST,
        name="ffn",
    )(*xn, *dy, weights)


def outer_kernel(sides, _, *refs):
    xn_parts, dy_parts = refs[: 2 * sides], refs[2 * sides : 4 * sides]
    g_refs, du_refs = refs[4 * sides : 5 * sides], refs[5 * sides : 6 * sides]
    grad_ref, xnt_ref, dyt_ref = refs[6 * sides :]
    mine = xn_parts[0].shape[0]
    hidden = g_refs[0].shape[1]

    @pl.when(pl.program_id(0) == 0)
    def _():
        for part in range(2 * sides):
            xnt_ref[:, part * mine : (part + 1) * mine] = xn_parts[part][...].T
            dyt_ref[:, part * mine : (part + 1) * mine] = dy_parts[part][...].T

    for at, turned, sources in ((0, xnt_ref, du_refs), (hidden, dyt_ref, g_refs)):
        total = None
        for side in range(sides):
            cut = slice(2 * side * mine, 2 * (side + 1) * mine)
            term = dot(turned[:, cut], sources[side][...])
            total = term if total is None else total + term
        grad_ref[0, :, at : at + hidden] = total.astype(BF16)


def outer(base, xn, dy, g, du, hidden):
    sides = len(g)
    mine, dim = xn[0].shape
    count = 2 * mine
    blocks = g[0].shape[1] // hidden
    whole = pl.BlockSpec((mine, dim), lambda i, base: (0, 0))
    act = pl.BlockSpec((count, hidden), lambda i, base: (0, i ^ base[0]))
    return pl.pallas_call(
        partial(outer_kernel, sides),
        grid_spec=pltpu.PrefetchScalarGridSpec(
            num_scalar_prefetch=1,
            grid=(blocks,),
            in_specs=[whole] * (4 * sides) + [act] * (2 * sides),
            out_specs=pl.BlockSpec((1, dim, 2 * hidden), lambda i, base: (i, 0, 0)),
            scratch_shapes=[pltpu.VMEM((dim, sides * count), BF16)] * 2,
        ),
        out_shape=jax.ShapeDtypeStruct((blocks, dim, 2 * hidden), BF16),
        compiler_params=pltpu.CompilerParams(vmem_limit_bytes=VMEM_LIMIT),
        cost_estimate=COST,
        name="outer",
    )(base, *xn, *dy, *g, *du)


def turn_kernel(layer, w_ref, *refs):
    x2_ref, dx_ref, core_ref, near_ref, dy_ref, ot_ref, gain_ref = refs[:7]
    dx2_ref, gout_ref, sums_ref = refs[7:10]
    dot_refs = refs[10:]
    middle = x2_ref[...]
    grad = dx_ref[...] + core_ref[...].astype(F32) + near_ref[...].astype(F32)
    back, prod = norm_backward(middle, gain_ref[1:2, :].astype(F32), grad)
    dx2 = dy_ref[...].astype(F32) + back
    dx2_ref[...] = dx2
    sums_ref[...] = jnp.concatenate(
        [
            jnp.sum(prod, axis=0, keepdims=True),
            jnp.sum(grad, axis=0, keepdims=True),
            jnp.zeros((6, grad.shape[1]), F32),
        ],
        axis=0,
    )
    low = dx2.astype(BF16)
    across = low.T
    width = ot_ref.shape[1]
    for part in range(w_ref.shape[0]):
        dot_refs[part][...] = dot(w_ref[layer[0] ^ part], across).astype(BF16)
        gout_ref[:, part * width : (part + 1) * width] = dot_nt(across, ot_ref[part]).astype(BF16)


def turn(layer, w_out, x2, dx, core, near, dy, ot, gains):
    count, dim = x2.shape
    parts = w_out.shape[0]
    out = pl.pallas_call(
        turn_kernel,
        in_specs=[pl.BlockSpec(memory_space=pltpu.SMEM)] + [vmem()] * 8,
        out_specs=[vmem()] * (parts + 3),
        out_shape=[
            jax.ShapeDtypeStruct((count, dim), F32),
            jax.ShapeDtypeStruct((dim, dim), BF16),
            jax.ShapeDtypeStruct((8, dim), F32),
        ]
        + [jax.ShapeDtypeStruct(ot.shape[1:], BF16)] * parts,
        compiler_params=pltpu.CompilerParams(vmem_limit_bytes=VMEM_LIMIT),
        cost_estimate=COST,
        name="turn",
    )(layer, w_out, x2, dx, core, near, dy, ot, gains)
    return *out[:3], out[3:]


def finish_kernel(parts, layer, *refs):
    part_refs, refs = refs[:parts], refs[parts:]
    w_ref, x_ref, dx2_ref, gain_ref, out_ref = refs
    width = w_ref.shape[2]
    grad = None
    for part in range(parts):
        for item in range(3):
            value = part_refs[part][item * width : (item + 1) * width, :]
            term = dot(value.T, w_ref[layer[0] ^ part, item])
            grad = term if grad is None else grad + term
    back, _ = norm_backward(x_ref[...].astype(F32), gain_ref[0:1, :].astype(F32), grad)
    out_ref[...] = (dx2_ref[...] + back).astype(BF16)


def finish(layer, parts, w_qkv, rows, dx2, gains):
    count, dim = rows.shape
    return pl.pallas_call(
        partial(finish_kernel, len(parts)),
        in_specs=[pl.BlockSpec(memory_space=pltpu.SMEM)] + [vmem()] * (len(parts) + 4),
        out_specs=vmem(),
        out_shape=jax.ShapeDtypeStruct((count, dim), BF16),
        compiler_params=pltpu.CompilerParams(vmem_limit_bytes=VMEM_LIMIT),
        cost_estimate=COST,
        name="finish",
    )(layer, *parts, w_qkv, rows, dx2, gains)


def small_kernel(flat_ref, unit_ref, w_ref, gain_ref, shift_ref, gout_ref, sums_ref, out_ref):
    dim = unit_ref.shape[1]
    inner = dot(flat_ref[...], unit_ref[...])
    sums = jnp.sum(flat_ref[...].astype(F32), axis=1, keepdims=True)
    grad = inner * gain_ref[0:1, :].astype(F32) + sums * shift_ref[0:1, :].astype(F32)
    width = w_ref.shape[1]
    gain = jnp.zeros((1, dim), F32)
    shift = jnp.zeros((1, dim), F32)
    for item in range(3):
        rows = slice(item * width, (item + 1) * width)
        w = w_ref[item].astype(F32)
        gain = gain + jnp.sum(w * inner[rows, :], axis=0, keepdims=True)
        shift = shift + jnp.sum(w * sums[rows, :], axis=0, keepdims=True)
    side = 3 * width
    out_ref[:, :dim] = gout_ref[...]
    out_ref[:, dim : dim + side] = grad.T.astype(BF16)
    sums = jnp.concatenate([gain, sums_ref[0:1, :], shift, sums_ref[1:2, :]], axis=0)
    sums = jnp.concatenate([sums, jnp.zeros((out_ref.shape[1] - dim - side - 4, dim), F32)], axis=0)
    out_ref[:, dim + side :] = sums.T.astype(BF16)


def small(flat, unit, w_qkv, gains, shifts, grad_out, sums):
    side, dim = flat.shape[0], unit.shape[1]
    total = -(-(dim + side + 8) // 128) * 128
    return pl.pallas_call(
        small_kernel,
        in_specs=[vmem()] * 7,
        out_specs=vmem(),
        out_shape=jax.ShapeDtypeStruct((dim, total), BF16),
        compiler_params=pltpu.CompilerParams(vmem_limit_bytes=VMEM_LIMIT),
        cost_estimate=COST,
        name="small",
    )(flat, unit, w_qkv, gains, shifts, grad_out, sums)


def collect_kernel(layer, *refs):
    parts, out_ref = refs[:-1], refs[-1]
    size = parts[0].shape[0]
    for item, part in enumerate(parts):
        out_ref[pl.ds(pl.multiple_of((layer[0] ^ item) * size, 128), size), :] = part[...]


def collect(layer, parts):
    size, dim = parts[0].shape
    return pl.pallas_call(
        collect_kernel,
        in_specs=[pl.BlockSpec(memory_space=pltpu.SMEM)] + [vmem()] * len(parts),
        out_specs=vmem(),
        out_shape=jax.ShapeDtypeStruct((size * len(parts), dim), parts[0].dtype),
        compiler_params=pltpu.CompilerParams(vmem_limit_bytes=VMEM_LIMIT),
        cost_estimate=COST,
        name="collect",
    )(layer, *parts)


WIDE = ("far", "near", "core")


def swap(value, axis):
    return lax.ppermute(value, axis, [(0, 1), (1, 0)])


def spread(parts):
    size = len(parts)
    return [parts[0]] + [
        lax.ppermute(parts[bit], "narrow", [(i, i ^ bit) for i in range(size)])
        for bit in range(1, size)
    ]


def exchange(value, axis):
    return lax.all_to_all(value, axis, 0, 0, tiled=True)


def after(value, *others):
    return lax.optimization_barrier((value,) + others)[0]


def add(*parts):
    return sum(part.astype(F32) for part in parts).astype(BF16)


def local(
    tokens, cotangent, seq_lens, norm_gains, norm_shifts, w_qkv, w_attn_out, w_ffn_in, w_ffn_down
):
    depth = lax.axis_size("narrow")
    across = lax.axis_size(WIDE)
    count, dim = tokens.shape
    mine = count // depth
    width = w_qkv.shape[2]
    cols = w_ffn_in.shape[1]
    heads = width // HD
    layer = lax.axis_index("narrow")
    layers = layer.astype(jnp.int32).reshape(1)

    pieces = lax.all_gather(
        jnp.concatenate([jnp.swapaxes(w_qkv, 1, 2), w_attn_out[None]], axis=0), WIDE, axis=0
    )
    weights = lax.all_gather(
        jnp.concatenate([w_ffn_in, w_ffn_down], axis=1), ("far", "narrow"), axis=0, tiled=True
    )
    group = max(1, dim // cols)
    shape = (-1, group, dim, 2, cols)
    if group > 1:
        weights = weights.reshape(shape).transpose(0, 2, 3, 1, 4).reshape(-1, 2 * group * cols)
    rows = lax.dynamic_slice_in_dim(tokens, layer * mine, mine, 0)
    dy = lax.dynamic_slice_in_dim(cotangent, layer * mine, mine, 0)
    dy_near = swap(dy, "near")
    dy_own = (dy, swap(dy, "core"))
    dy_far = (dy_near, swap(dy_near, "core"))

    unit, q_rows, k_rows, q_cols, k_cols, v_cols, *tables, w_proj, w_out = project(
        seq_lens, tokens, norm_gains, norm_shifts, pieces, depth
    )
    w_out = exchange(w_out, "narrow")
    parts, out, lse = attend(0, heads, depth, layers, tables, k_rows, q_cols, v_cols)
    x2, xn2, ot = mix(layers, spread(parts), w_out, rows, norm_gains, norm_shifts)
    xn_near = swap(xn2, "near")
    xn_own = (xn2, swap(xn2, "core"))
    w_proj_all = lax.all_gather(w_proj, "narrow", axis=0)

    y_a, dx_a, y_core, dx_core, g_a, du_a = ffn(xn_own, dy_own, weights)
    xn_near = after(xn_near, y_a)
    xn_far = (xn_near, swap(xn_near, "core"))
    y_b, dx_b, y_far, dx_far, g_b, du_b = ffn(xn_far, dy_far, weights)
    dx_core = swap(dx_core, "core")
    dx_near = swap(add(dx_b, swap(dx_far, "core")), "near")
    pair = lax.axis_size("far") == 2
    base = lax.axis_index("far") if pair else jnp.zeros((), jnp.int32)
    base = base.astype(jnp.int32).reshape(1)
    grads = outer(base, xn_own + xn_far, dy_own + dy_far, (g_a, g_b), (du_a, du_b), group * cols)
    dx2, grad_out, norm_two, dout = turn(
        layers, w_out, after(x2, grads), dx_a, dx_core, dx_near, dy, ot, norm_gains
    )
    dout = spread(dout)
    y_core, y_far = (swap(part, "core") for part in (y_core, y_far))
    y_near = swap(add(y_b, y_far), "near")
    out_mine = (x2 + y_a + y_core.astype(F32) + y_near.astype(F32)).astype(BF16)
    dout, out_mine = lax.optimization_barrier((dout, out_mine))
    layer_out = lax.all_gather(out_mine, "narrow", axis=0, tiled=True)
    back, flat_back = attend_back(
        0, heads, layers, tables, q_rows, k_rows, q_cols, k_cols, v_cols, out, lse, dout
    )
    if pair:
        back, far_grads = lax.optimization_barrier((back, swap(grads[1], "far")))
        total = add(after(grads[0], flat_back), far_grads)
    else:
        grads = grads.reshape(-1, dim, 2, group, cols).transpose(0, 3, 1, 2, 4)
        grads = grads.reshape(-1, dim, 2 * cols)
        total = lax.psum_scatter(grads, "far", scatter_dimension=0, tiled=False)
    total = lax.psum_scatter(total, "narrow", scatter_dimension=0, tiled=True).astype(F32)

    back = spread(back)
    in_mine = finish(layers, back, w_proj_all, rows, dx2, norm_gains)
    input_grad = lax.all_gather(in_mine, "narrow", axis=0, tiled=True)

    side = 3 * width
    part = dim // across
    rest = small(
        after(flat_back, in_mine), unit, w_proj, norm_gains, norm_shifts, grad_out, norm_two
    )
    rest = exchange(rest.reshape(across, part, -1), WIDE)
    rest = jnp.sum(rest.astype(F32), axis=0)
    gqkv = rest[:, dim : dim + side].reshape(part, 3, width).transpose(1, 0, 2)
    gout = rest[:, :dim].astype(BF16).reshape(part, depth, width).transpose(1, 0, 2)
    norms = rest[:, dim + side : dim + side + 4].astype(BF16)
    gout = jnp.concatenate([gout, jnp.broadcast_to(norms, (depth, part, 4))], axis=2)
    gout = jnp.sum(exchange(gout, "narrow").astype(F32), axis=0).T
    gout, norms = gout[:width], gout[width:]
    return (
        layer_out,
        input_grad,
        norms[:2],
        norms[2:],
        gqkv,
        gout,
        total[:, :cols],
        total[:, cols:],
    )


def solution(mesh):
    depth, across = mesh.shape["narrow"], mesh.shape["wide"]
    fine = jax.sharding.Mesh(
        mesh.devices.reshape(depth, across // 4, 2, 2), ("narrow", "far", "near", "core")
    )
    return jax.shard_map(
        local,
        mesh=fine,
        in_specs=(
            P(WIDE, None),
            P(WIDE, None),
            P(WIDE, None),
            P(),
            P(),
            P(None, WIDE, "narrow"),
            P("narrow", WIDE),
            P("narrow", WIDE),
            P("narrow", WIDE),
        ),
        out_specs=(
            P(WIDE, None),
            P(WIDE, None),
            P(None, WIDE),
            P(None, WIDE),
            P(None, WIDE, "narrow"),
            P("narrow", WIDE),
            P("narrow", WIDE),
            P("narrow", WIDE),
        ),
        check_vma=False,
    )
```

time: 448 us -> 341 us (0.76)
  waiting for transfers between devices: 142 us -> 83.2 us
  blocking collectives: 89.6 us -> 37.8 us
  local copies, waits for them, and re-layouts: 32.9 us -> 18.7 us
  starting transfers between devices: 36.8 us -> 50.4 us
  Pallas kernels: 116 us -> 126 us
    all_to_all x1 -> x0, waiting for transfers between devices: 46 us -> none  [local(): lax.all_to_all(jnp.broadcast_to(w_attn_out[None], (depth * across,) + w_a...]
    psum x1 -> x0, blocking collectives: 37.5 us -> none  [local(): norms = lax.psum(norms, ('narrow', 'wide'))]
    all_to_all x4 -> x2, waiting for transfers between devices: 37.8 us -> 11 us  [exchange(): return lax.all_to_all(value, axis, 0, 0, tiled=True)]
    all_to_all x2 -> x1, blocking collectives: 37.8 us -> 23.4 us  [exchange(): return lax.all_to_all(value, axis, 0, 0, tiled=True)]
    ppermute x15 -> x22, waiting for transfers between devices: 57.8 us -> 71.4 us  [the longest x9 67.7 us: spread(): lax.ppermute(parts[bit], 'narrow', [(i, i ^ bit) for i in range(size)])]
    all_to_all x4 -> x2, starting transfers between devices: 13.9 us -> 25.5 us  [exchange(): return lax.all_to_all(value, axis, 0, 0, tiled=True)]
    ppermute x15 -> x22, starting transfers between devices: 15.4 us -> 24.2 us  [the longest x9 17 us: spread(): lax.ppermute(parts[bit], 'narrow', [(i, i ^ bit) for i in range(size)])]
    pallas_call x8 -> x9, Pallas kernels: 107 us -> 115 us  [the longest x1 34.8 us: attend_back(): pl.pallas_call(partial(attend_back_kernel, first, heads, parts), in_specs...]
  transfers between devices with their start and end apart: 25 -> 29, of which waited for: 12 -> 9; matrix products, arithmetic and copies ran while one was open for 7% -> 5% of each run, Pallas kernels for 26% -> 37%
where the time goes in v2:
time: 341 us; the launch traced here: 340 us
  Pallas kernels  126 us (37%)
  waiting for transfers between devices  83.2 us (24%)
  starting transfers between devices  50.4 us (15%)
  blocking collectives  37.8 us (11%)
  local copies, waits for them, and re-layouts  18.7 us (5%)
  between operations  14.1 us (4%)
  other arithmetic  9.69 us (3%)
    ppermute x9, waiting for transfers between devices, spread(): lax.ppermute(parts[bit], 'narrow', [(i, i ^ bit) for i in range(size)])  67.7 us
    pallas_call x1, Pallas kernels, attend_back(): pl.pallas_call(partial(attend_back_kernel, first, heads, parts), in_specs...  34.8 us
    all_to_all x2, starting transfers between devices, exchange(): return lax.all_to_all(value, axis, 0, 0, tiled=True)  25.5 us
    pallas_call x2, Pallas kernels, ffn(): pl.pallas_call(ffn_kernel, grid=(blocks,), in_specs=[whole] * 4 + [pl.Blo...  25.3 us
    all_to_all x1, blocking collectives, exchange(): return lax.all_to_all(value, axis, 0, 0, tiled=True)  23.4 us
    pallas_call x1, Pallas kernels, attend(): pl.pallas_call(partial(attend_kernel, first, heads, parts), in_specs=[pl....  22.4 us
    ppermute x9, starting transfers between devices, spread(): lax.ppermute(parts[bit], 'narrow', [(i, i ^ bit) for i in range(size)])  17 us
    all_gather x1, blocking collectives, local(): lax.all_gather(jnp.concatenate([jnp.swapaxes(w_qkv, 1, 2), w_attn_out[Non...  14.4 us
  transfers between devices with their start and end apart: 29, of which 9 were waited for; matrix products, arithmetic and copies ran while one was open for 5% of the time, Pallas kernels for 37%

profile of v2, /device:TPU:0, one launch (start us, length us, event | category | flops | bytes accessed | tf_op | source)
XLA Modules:
  0.0 340.2 jit_solution(9916721884065065051)
XLA Ops:
  7.2 1.9 pad_maximum_fusion
  11.1 14.4 %all-gather = bf16[32,160,80]{2,1,0:T(8,128)(2,1)} all-gather(bf16[4,160,80]{2,1,0:T(8,128)(2,1)S(1)} %pad_maximum_fusion.1), channel_id=2, replica_groups=mesh['narrow'=4,'far'=2,'near'=2,'core'=2] {'far','near','core'}, dimensions={0}, use_global_device_ids=true | all-gather | bytes 921600 | tf_op jit(solution)/shard_map/all_gather | solution.py:636
  25.5 11.3 %project.1 = (bf16[1536,640]{1,0:T(8,128)(2,1)}, bf16[5,1536,32]{2,1,0:T(8,128)(2,1)}, bf16[5,1536,32]{2,1,0:T(8,128)(2,1)}, bf16[160,1536]{1,0:T(8,128)(2,1)}, ...) custom-call(s32[1,16]{1,0:T(1,128)} %lens.1, ...), custom_call_target="tpu_custom_call" | custom-call | flops 1000000 | bytes 100000 | tf_op jit(solution)/shard_map/project/pallas_call | solution.py:109
  36.8 5.2 %all-to-all-start = ((bf16[4,160,640]{2,1,0:T(8,128)(2,1)}), bf16[4,160,640]{2,1,0:T(8,128)(2,1)S(1)}, u32[]{:S(2)}, u32[]{:S(2)}) async-start(bf16[4,160,640]{2,1,0:T(8,128)(2,1)} %get-tuple-element.66), calls=%async_computation | async-start | bytes 1638400 | tf_op jit(solution)/shard_map/all_to_all | solution.py:612
  43.9 22.4 %attend_0.1 = (bf16[160,384]{1,0:T(8,128)(2,1)}, bf16[160,384]{1,0:T(8,128)(2,1)}, bf16[160,384]{1,0:T(8,128)(2,1)}, bf16[160,384]{1,0:T(8,128)(2,1)}, f32[160,1536]{1,0:T(8,128)}, /*index=5*/f32[8,1536]{1,0:T(8,128)}) custom-call(s32[1]{0:T(128)} %bitcast.layer, s32[6,2]{1,0:T(8,128)} %get-tuple-element.67.bounds, s32[1536,128]{1,0:T(8,128)} %get-tuple-element.68.segc_ref, ...), custom_call_target="tpu_custom_call" | custom-call | flops 1000000 | bytes 100000 | tf_op jit(solution)/shard_map/attend_0/pallas_call | solution.py:214
  66.3 2.0 collective-permute-start
  68.3 2.4 collective-permute-start.1
  70.7 1.9 constant_dynamic-slice_fusion.1.refs_5_
  72.6 5.7 %collective-permute-done.refs_1_ = bf16[160,384]{1,0:T(8,128)(2,1)S(1)} collective-permute-done((bf16[160,384]{1,0:T(8,128)(2,1)}, bf16[160,384]{1,0:T(8,128)(2,1)S(1)}, u32[]{:S(2)}, u32[]{:S(2)}) %collective-permute-start) | collective-permute-done | bytes 122912 | tf_op jit(solution)/shard_map/ppermute | solution.py:606
  78.4 18.0 %collective-permute-done.1.refs_2_ = bf16[160,384]{1,0:T(8,128)(2,1)S(1)} collective-permute-done((bf16[160,384]{1,0:T(8,128)(2,1)}, bf16[160,384]{1,0:T(8,128)(2,1)S(1)}, u32[]{:S(2)}, u32[]{:S(2)}) %collective-permute-start.1) | collective-permute-done | bytes 122912 | tf_op jit(solution)/shard_map/ppermute | solution.py:606
  97.3 3.6 %mix.1 = (f32[384,640]{1,0:T(8,128)}, bf16[384,640]{1,0:T(8,128)(2,1)}, bf16[4,160,384]{2,1,0:T(8,128)(2,1)}) custom-call(s32[1]{0:T(128)} %bitcast.layer, bf16[160,384]{1,0:T(8,128)(2,1)} %get-tuple-element.73.refs_0_, bf16[160,384]{1,0:T(8,128)(2,1)} %copy-done.22, bf16[160,384]{1,0:T(8,128)(2,1)} %copy-done.23, bf16[160,384]{1,0:T(8,128)(2,1)} %copy-done.24, ...), custom_call_target="tpu_custom_call" | custom-call | flops 1000000 | bytes 100000 | tf_op jit(solution)/shard_map/mix/pallas_call | solution.py:345
  103.9 12.6 %ffn.2 = (f32[384,640]{1,0:T(8,128)}, f32[384,640]{1,0:T(8,128)}, bf16[384,640]{1,0:T(8,128)(2,1)}, bf16[384,640]{1,0:T(8,128)(2,1)}, bf16[768,1280]{1,0:T(8,128)(2,1)}, /*index=5*/bf16[768,1280]{1,0:T(8,128)(2,1)}) custom-call(bf16[384,640]{1,0:T(8,128)(2,1)} %get-tuple-element.78.refs_0_, bf16[384,640]{1,0:T(8,128)(2,1)} %copy-done.9, ...), custom_call_target="tpu_custom_call" | custom-call | flops 1000000 | bytes 100000 | tf_op jit(solution)/shard_map/ffn/pallas_call | solution.py:409
  119.2 12.7 %ffn.3 = (f32[384,640]{1,0:T(8,128)}, f32[384,640]{1,0:T(8,128)}, bf16[384,640]{1,0:T(8,128)(2,1)}, bf16[384,640]{1,0:T(8,128)(2,1)}, bf16[768,1280]{1,0:T(8,128)(2,1)}, /*index=5*/bf16[768,1280]{1,0:T(8,128)(2,1)}) custom-call(bf16[384,640]{1,0:T(8,128)(2,1)} %copy-done.10, bf16[384,640]{1,0:T(8,128)(2,1)} %copy-done.12, bf16[384,640]{1,0:T(8,128)(2,1)} %copy-done.8, ...), custom_call_target="tpu_custom_call" | custom-call | flops 1000000 | bytes 100000 | tf_op jit(solution)/shard_map/ffn/pallas_call | solution.py:409
  138.4 12.4 %outer.1 = bf16[2,640,1280]{2,1,0:T(8,128)(2,1)} custom-call(s32[1]{0:T(128)} %bitcast.4._, bf16[384,640]{1,0:T(8,128)(2,1)} %get-tuple-element.78.refs_0_, bf16[384,640]{1,0:T(8,128)(2,1)} %copy-done.9, bf16[384,640]{1,0:T(8,128)(2,1)} %copy-done.10, bf16[384,640]{1,0:T(8,128)(2,1)} %copy-done.12, bf16[384,640]{1,0:T(8,128)(2,1)} %copy-done.3, ...), custom_call_target="tpu_custom_call" | custom-call | flops 1000000 | bytes 100000 | tf_op jit(solution)/shard_map/outer/pallas_call | solution.py:453
  151.9 5.6 %turn.1 = (f32[384,640]{1,0:T(8,128)}, bf16[640,640]{1,0:T(8,128)(2,1)}, f32[8,640]{1,0:T(8,128)}, bf16[160,384]{1,0:T(8,128)(2,1)}, bf16[160,384]{1,0:T(8,128)(...) custom-call(s32[1]{0:T(128)} %bitcast.layer, bf16[4,160,640]{2,1,0:T(8,128)(2,1)} %copy-done.4, ...), custom_call_target="tpu_custom_call" | custom-call | flops 1000000 | bytes 100000 | tf_op jit(solution)/shard_map/turn/pallas_call | solution.py:497
  157.5 4.6 %collective-permute-start.12 = (bf16[160,384]{1,0:T(8,128)(2,1)}, bf16[160,384]{1,0:T(8,128)(2,1)S(1)}, u32[]{:S(2)}, u32[]{:S(2)}) collective-permute-start(bf16[160,384]{1,0:T(8,128)(2,1)} %get-tuple-element.92), channel_id=1, source_target_pairs={{0,8},{8,0},{16,24},{24,16},{1,9},{9,1},{17,25},{25,17},{2,10},{10... | collective-permute-start | bytes 368648 | tf_op jit(solution)/shard_map/ppermute | solution.py:606
  162.2 2.4 collective-permute-start.14
  164.6 2.2 add_convert_fusion.1
  166.8 7.1 %collective-permute-done.13.refs_2_ = bf16[160,384]{1,0:T(8,128)(2,1)S(1)} collective-permute-done((bf16[160,384]{1,0:T(8,128)(2,1)}, bf16[160,384]{1,0:T(8,128)(2,1)S(1)}, u32[]{:S(2)}, u32[]{:S(2)}) %collective-permute-start.13) | collective-permute-done | bytes 122912 | tf_op jit(solution)/shard_map/ppermute | solution.py:606
  175.4 1.9 collective-permute-start.18
  177.3 34.8 %attend_back_0.1 = (bf16[480,384]{1,0:T(8,128)(2,1)}, bf16[480,384]{1,0:T(8,128)(2,1)}, bf16[480,384]{1,0:T(8,128)(2,1)}, bf16[480,384]{1,0:T(8,128)(2,1)}, bf16[480,1536]{1,0:T(8,128)(2,1)}) custom-call(s32[1]{0:T(128)} %bitcast.layer, s32[6,2]{1,0:T(8,128)} %get-tuple-element.67.bounds, s32[1536,128]{1,0:T(8,128)} %get-tuple-element.68.segc_ref, ...), custom_call_target="tpu_custom_call" | custom-call | flops 1000000 | bytes 100000 | tf_op jit(solution)/shard_map/attend_back_0/pallas_call | solution.py:307
  214.1 3.0 collective-permute-start.19
  217.1 2.4 collective-permute-start.21
  219.6 21.1 %collective-permute-done.19.refs_1_ = bf16[480,384]{1,0:T(8,128)(2,1)S(1)} collective-permute-done((bf16[480,384]{1,0:T(8,128)(2,1)S(1)}, bf16[480,384]{1,0:T(8,128)(2,1)S(1)}, u32[]{:S(2)}, u32[]{:S(2)}) %collective-permute-start.19) | collective-permute-done | bytes 368672 | tf_op jit(solution)/shard_map/ppermute | solution.py:606
  240.7 15.7 %collective-permute-done.20.refs_2_ = bf16[480,384]{1,0:T(8,128)(2,1)S(1)} collective-permute-done((bf16[480,384]{1,0:T(8,128)(2,1)S(1)}, bf16[480,384]{1,0:T(8,128)(2,1)S(1)}, u32[]{:S(2)}, u32[]{:S(2)}) %collective-permute-start.20) | collective-permute-done | bytes 368672 | tf_op jit(solution)/shard_map/ppermute | solution.py:606
  257.3 5.7 %finish.1 = bf16[384,640]{1,0:T(8,128)(2,1)} custom-call(s32[1]{0:T(128)} %bitcast.layer, bf16[480,384]{1,0:T(8,128)(2,1)} %get-tuple-element.111.refs_0_, bf16[480,384]{1,0:T(8,128)(2,1)} %copy-done.17, bf16[480,384]{1,0:T(8,128)(2,1)} %copy-done.18, bf16[480,384]{1,0:T(8,128)(2,1)} %copy-done.19, bf16[4,3,160,640]{3,2,1,0:T(8,128)(2,1)} %bitcast.21, ...), custom_call_target="tpu_custom_call" | custom-call | flops 1000000 | bytes 100000 | tf_op jit(solution)/shard_map/finish/pallas_call | solution.py:530
  263.1 5.1 %small.1 = bf16[640,1152]{1,0:T(8,128)(2,1)} custom-call(bf16[480,1536]{1,0:T(8,128)(2,1)} %get-tuple-element.118.flat_ref, bf16[1536,640]{1,0:T(8,128)(2,1)} %get-tuple-element.119.unit_ref, bf16[3,160,640]{2,1,0:T(8,128)(2,1)} %get-tuple-element.115.w_ref, bf16[2,640]{1,0:T(2,128)(2,1)} %gain_ref.3, bf16[2,640]{1,0:T(2,128)(2,1)} %shift_ref.3, ...), custom_call_target="tpu_custom_call" | custom-call | flops 1000000 | bytes 100000 | tf_op jit(solution)/shard_map/small/pallas_call | solution.py:565
  268.1 23.4 %all_to_all.15 = bf16[8,80,1152]{2,1,0:T(8,128)(2,1)S(1)} all-to-all(bf16[8,80,1152]{2,1,0:T(8,128)(2,1)} %bitcast.19), channel_id=1, replica_groups=mesh['narrow'=4,'far'=2,'near'=2,'core'=2] {'far','near','core'}, dimensions={0} | all-to-all | bytes 2949120 | tf_op jit(solution)/shard_map/all_to_all | solution.py:612
  292.8 20.3 %all-to-all-start.2 = ((bf16[4,80,164]{2,1,0:T(8,128)(2,1)}), bf16[4,80,164]{2,1,0:T(8,128)(2,1)S(1)}, u32[]{:S(2)}, u32[]{:S(2)}) async-start(bf16[4,80,164]{2,1,0:T(8,128)(2,1)} %pad_maximum_fusion.2), calls=%async_computation.2 | async-start | bytes 327680 | tf_op jit(solution)/shard_map/all_to_all | solution.py:612
  314.2 11.0 %all-to-all-done.2 = bf16[4,80,164]{2,1,0:T(8,128)(2,1)S(1)} async-done(((bf16[4,80,164]{2,1,0:T(8,128)(2,1)}), bf16[4,80,164]{2,1,0:T(8,128)(2,1)S(1)}, u32[]{:S(2)}, u32[]{:S(2)}) %all-to-all-start.2) | async-done | bytes 104992 | tf_op jit(solution)/shard_map/all_to_all | solution.py:612
  327.3 2.0 fusion
  329.3 3.1 copy.37
  (130 shorter events, 27.9 us)
Async XLA Ops:
  7.2 35.8 %copy-start = (bf16[1536,640]{1,0:T(8,128)(2,1)S(1)}, bf16[1536,640]{1,0:T(8,128)(2,1)}, u32[]{:S(2)}) copy-start(bf16[1536,640]{1,0:T(8,128)(2,1)} %param.10) | copy-start | bytes 5898244
  7.2 95.9 %all-gather.7.cloned.1.call-start = ((), (), s32[]{:S(2)}) async-start(), calls=%async_computation.4 | async-start | bytes 3686400 | tf_op jit(solution)/shard_map/all_gather | solution.py:639
  36.8 59.5 %all-to-all-start = ((bf16[4,160,640]{2,1,0:T(8,128)(2,1)}), bf16[4,160,640]{2,1,0:T(8,128)(2,1)S(1)}, u32[]{:S(2)}, u32[]{:S(2)}) async-start(bf16[4,160,640]{2,1,0:T(8,128)(2,1)} %get-tuple-element.66), calls=%async_computation | async-start | bytes 1638400 | tf_op jit(solution)/shard_map/all_to_all | solution.py:612
  42.0 177.5 %all-gather.13.cloned.1.call-start = ((), (), s32[]{:S(2)}) async-start(), calls=%async_computation.8 | async-start | bytes 3072000 | tf_op jit(solution)/shard_map/all_gather | solution.py:660
  42.7 284.5 %all-gather.9.cloned.1.call-start = ((), (), s32[]{:S(2)}) async-start(), calls=%async_computation.5 | async-start | bytes 2457600 | tf_op jit(solution)/shard_map/all_gather | solution.py:680
  43.1 29.6 %copy-start.3 = (bf16[384,640]{1,0:T(8,128)(2,1)}, bf16[384,640]{1,0:T(8,128)(2,1)S(1)}, u32[]{:S(2)}) copy-start(bf16[384,640]{1,0:T(8,128)(2,1)S(1)} %constant_dynamic-slice_fusion.refs_2_.refs_4_) | copy-start | bytes 1474564
  43.1 59.0 %collective-permute-start.5 = (bf16[384,640]{1,0:T(8,128)(2,1)S(1)}, bf16[384,640]{1,0:T(8,128)(2,1)S(1)}, u32[]{:S(2)}, u32[]{:S(2)}) collective-permute-start(bf16[384,640]{1,0:T(8,128)(2,1)S(1)} %constant_dynamic-slice_fusion.refs_2_.refs_4_), channel_id=1, source_target_pairs={{0,1},{1,0},{2,3},{3,2},{4,5},{5,4},{6,7},{7,6},{8,9},{9,8},{10,11... | collective-permute-start | bytes 1474568 | tf_op jit(solution)/shard_map/ppermute | solution.py:600
  43.2 58.7 %collective-permute-start.7 = (bf16[384,640]{1,0:T(8,128)(2,1)S(1)}, bf16[384,640]{1,0:T(8,128)(2,1)S(1)}, u32[]{:S(2)}, u32[]{:S(2)}) collective-permute-start(bf16[384,640]{1,0:T(8,128)(2,1)S(1)} %constant_dynamic-slice_fusion.refs_2_.refs_4_), channel_id=1, source_target_pairs={{0,2},{2,0},{1,3},{3,1},{4,6},{6,4},{5,7},{7,5},{8,10},{10,8},{9,1... | collective-permute-start | bytes 1474568 | tf_op jit(solution)/shard_map/ppermute | solution.py:600
  66.3 12.1 %collective-permute-start = (bf16[160,384]{1,0:T(8,128)(2,1)}, bf16[160,384]{1,0:T(8,128)(2,1)S(1)}, u32[]{:S(2)}, u32[]{:S(2)}) collective-permute-start(bf16[160,384]{1,0:T(8,128)(2,1)} %get-tuple-element.74), channel_id=1, source_target_pairs={{0,8},{8,0},{16,24},{24,16},{1,9},{9,1},{17,25},{25,17},{2,10},{10... | collective-permute-start | bytes 368648 | tf_op jit(solution)/shard_map/ppermute | solution.py:606
  68.3 28.0 %collective-permute-start.1 = (bf16[160,384]{1,0:T(8,128)(2,1)}, bf16[160,384]{1,0:T(8,128)(2,1)S(1)}, u32[]{:S(2)}, u32[]{:S(2)}) collective-permute-start(bf16[160,384]{1,0:T(8,128)(2,1)} %get-tuple-element.75), channel_id=1, source_target_pairs={{0,16},{8,24},{16,0},{24,8},{1,17},{9,25},{17,1},{25,9},{2,18},{10... | collective-permute-start | bytes 368648 | tf_op jit(solution)/shard_map/ppermute | solution.py:606
  70.7 25.7 %collective-permute-start.2 = (bf16[160,384]{1,0:T(8,128)(2,1)}, bf16[160,384]{1,0:T(8,128)(2,1)S(1)}, u32[]{:S(2)}, u32[]{:S(2)}) collective-permute-start(bf16[160,384]{1,0:T(8,128)(2,1)} %get-tuple-element.76), channel_id=1, source_target_pairs={{0,24},{8,16},{16,8},{24,0},{1,25},{9,17},{17,9},{25,1},{2,26},{10... | collective-permute-start | bytes 368648 | tf_op jit(solution)/shard_map/ppermute | solution.py:606
  78.4 18.0 %copy-start.22 = (bf16[160,384]{1,0:T(8,128)(2,1)}, bf16[160,384]{1,0:T(8,128)(2,1)S(1)}, u32[]{:S(2)}) copy-start(bf16[160,384]{1,0:T(8,128)(2,1)S(1)} %collective-permute-done.refs_1_) | copy-start | bytes 368644
  101.0 2.1 collective-permute-start.3
  101.0 15.5 %collective-permute-start.4 = (bf16[384,640]{1,0:T(8,128)(2,1)}, bf16[384,640]{1,0:T(8,128)(2,1)S(1)}, u32[]{:S(2)}, u32[]{:S(2)}) collective-permute-start(bf16[384,640]{1,0:T(8,128)(2,1)} %get-tuple-element.78.refs_0_), channel_id=1, source_target_pairs={{0,2},{2,0},{1,3},{3,1},{4,6},{6,4},{5,7},{7,5},{8,10},{10,8},{9,1... | collective-permute-start | bytes 1474568 | tf_op jit(solution)/shard_map/ppermute | solution.py:600
  101.9 14.8 %collective-permute-start.8 = (bf16[384,640]{1,0:T(8,128)(2,1)S(1)}, bf16[384,640]{1,0:T(8,128)(2,1)S(1)}, u32[]{:S(2)}, u32[]{:S(2)}) collective-permute-start(bf16[384,640]{1,0:T(8,128)(2,1)S(1)} %collective-permute-done.7.refs_2_.refs_6_), channel_id=1, source_target_pairs={{0,1},{1,0},{2,3},{3,2},{4,5},{5,4},{6,7},{7,6},{8,9},{9,8},{10,11... | collective-permute-start | bytes 1474568 | tf_op jit(solution)/shard_map/ppermute | solution.py:600
  116.5 1.9 collective-permute-start.6
  132.0 2.1 collective-permute-start.10
  132.1 4.2 %collective-permute-start.16 = (bf16[384,640]{1,0:T(8,128)(2,1)}, bf16[384,640]{1,0:T(8,128)(2,1)S(1)}, u32[]{:S(2)}, u32[]{:S(2)}) collective-permute-start(bf16[384,640]{1,0:T(8,128)(2,1)} %get-tuple-element.97), channel_id=1, source_target_pairs={{0,1},{1,0},{2,3},{3,2},{4,5},{5,4},{6,7},{7,6},{8,9},{9,8},{10,11... | collective-permute-start | bytes 1474568 | tf_op jit(solution)/shard_map/ppermute | solution.py:600
  132.5 32.1 %collective-permute-start.15 = (bf16[384,640]{1,0:T(8,128)(2,1)}, bf16[384,640]{1,0:T(8,128)(2,1)}, u32[]{:S(2)}, u32[]{:S(2)}) collective-permute-start(bf16[384,640]{1,0:T(8,128)(2,1)} %get-tuple-element.95), channel_id=1, source_target_pairs={{0,1},{1,0},{2,3},{3,2},{4,5},{5,4},{6,7},{7,6},{8,9},{9,8},{10,11... | collective-permute-start | bytes 1474568 | tf_op jit(solution)/shard_map/ppermute | solution.py:600
  132.7 18.2 %collective-permute-start.9 = (bf16[384,640]{1,0:T(8,128)(2,1)S(1)}, bf16[384,640]{1,0:T(8,128)(2,1)S(1)}, u32[]{:S(2)}, u32[]{:S(2)}) collective-permute-start(bf16[384,640]{1,0:T(8,128)(2,1)S(1)} %copy-done.25), channel_id=1, source_target_pairs={{0,1},{1,0},{2,3},{3,2},{4,5},{5,4},{6,7},{7,6},{8,9},{9,8},{10,11... | collective-permute-start | bytes 1474568 | tf_op jit(solution)/shard_map/ppermute | solution.py:600
  135.4 15.4 %collective-permute-start.11 = (bf16[384,640]{1,0:T(8,128)(2,1)S(1)}, bf16[384,640]{1,0:T(8,128)(2,1)S(1)}, u32[]{:S(2)}, u32[]{:S(2)}) collective-permute-start(bf16[384,640]{1,0:T(8,128)(2,1)S(1)} %add_convert_fusion.3), channel_id=1, source_target_pairs={{0,2},{2,0},{1,3},{3,1},{4,6},{6,4},{5,7},{7,5},{8,10},{10,8},{9,1... | collective-permute-start | bytes 1474568 | tf_op jit(solution)/shard_map/ppermute | solution.py:600
  137.2 27.3 %collective-permute-start.17 = (bf16[384,640]{1,0:T(8,128)(2,1)}, bf16[384,640]{1,0:T(8,128)(2,1)}, u32[]{:S(2)}, u32[]{:S(2)}) collective-permute-start(bf16[384,640]{1,0:T(8,128)(2,1)} %add_convert_fusion.2), channel_id=1, source_target_pairs={{0,2},{2,0},{1,3},{3,1},{4,6},{6,4},{5,7},{7,5},{8,10},{10,8},{9,1... | collective-permute-start | bytes 1474568 | tf_op jit(solution)/shard_map/ppermute | solution.py:600
  157.5 9.3 %collective-permute-start.12 = (bf16[160,384]{1,0:T(8,128)(2,1)}, bf16[160,384]{1,0:T(8,128)(2,1)S(1)}, u32[]{:S(2)}, u32[]{:S(2)}) collective-permute-start(bf16[160,384]{1,0:T(8,128)(2,1)} %get-tuple-element.92), channel_id=1, source_target_pairs={{0,8},{8,0},{16,24},{24,16},{1,9},{9,1},{17,25},{25,17},{2,10},{10... | collective-permute-start | bytes 368648 | tf_op jit(solution)/shard_map/ppermute | solution.py:606
  162.1 11.8 %collective-permute-start.13 = (bf16[160,384]{1,0:T(8,128)(2,1)}, bf16[160,384]{1,0:T(8,128)(2,1)S(1)}, u32[]{:S(2)}, u32[]{:S(2)}) collective-permute-start(bf16[160,384]{1,0:T(8,128)(2,1)} %get-tuple-element.93), channel_id=1, source_target_pairs={{0,16},{8,24},{16,0},{24,8},{1,17},{9,25},{17,1},{25,9},{2,18},{10... | collective-permute-start | bytes 368648 | tf_op jit(solution)/shard_map/ppermute | solution.py:606
  162.2 11.7 %collective-permute-start.14 = (bf16[160,384]{1,0:T(8,128)(2,1)}, bf16[160,384]{1,0:T(8,128)(2,1)}, u32[]{:S(2)}, u32[]{:S(2)}) collective-permute-start(bf16[160,384]{1,0:T(8,128)(2,1)} %get-tuple-element.94), channel_id=1, source_target_pairs={{0,24},{8,16},{16,8},{24,0},{1,25},{9,17},{17,9},{25,1},{2,26},{10... | collective-permute-start | bytes 368648 | tf_op jit(solution)/shard_map/ppermute | solution.py:606
  173.9 153.4 %reduce-scatter.2.cloned.1.call-start = ((), (), s32[]{:S(2)}) async-start(), calls=%async_computation.7 | async-start | bytes 2048000 | tf_op jit(solution)/shard_map/reduce_scatter | solution.py:691
  175.4 36.7 %collective-permute-start.18 = (bf16[640,1280]{1,0:T(8,128)(2,1)}, bf16[640,1280]{1,0:T(8,128)(2,1)S(1)}, u32[]{:S(2)}, u32[]{:S(2)}) collective-permute-start(bf16[640,1280]{1,0:T(8,128)(2,1)} %get-tuple-element.149), channel_id=1, source_target_pairs={{0,4},{4,0},{1,5},{5,1},{2,6},{6,2},{3,7},{7,3},{8,12},{12,8},{9,1... | collective-permute-start | bytes 4915208 | tf_op jit(solution)/shard_map/ppermute | solution.py:600
  213.8 115.5 %all-gather.11.cloned.1.call-start = ((), (), s32[]{:S(2)}) async-start(), calls=%async_computation.6 | async-start | bytes 2457600 | tf_op jit(solution)/shard_map/all_gather | solution.py:695
  214.1 26.6 %collective-permute-start.19 = (bf16[480,384]{1,0:T(8,128)(2,1)S(1)}, bf16[480,384]{1,0:T(8,128)(2,1)S(1)}, u32[]{:S(2)}, u32[]{:S(2)}) collective-permute-start(bf16[480,384]{1,0:T(8,128)(2,1)S(1)} %copy-done.28), channel_id=1, source_target_pairs={{0,8},{8,0},{16,24},{24,16},{1,9},{9,1},{17,25},{25,17},{2,10},{10... | collective-permute-start | bytes 1105928 | tf_op jit(solution)/shard_map/ppermute | solution.py:606
  217.1 39.3 %collective-permute-start.20 = (bf16[480,384]{1,0:T(8,128)(2,1)S(1)}, bf16[480,384]{1,0:T(8,128)(2,1)S(1)}, u32[]{:S(2)}, u32[]{:S(2)}) collective-permute-start(bf16[480,384]{1,0:T(8,128)(2,1)S(1)} %copy-done.27), channel_id=1, source_target_pairs={{0,16},{8,24},{16,0},{24,8},{1,17},{9,25},{17,1},{25,9},{2,18},{10... | collective-permute-start | bytes 1105928 | tf_op jit(solution)/shard_map/ppermute | solution.py:606
  217.1 39.3 %collective-permute-start.21 = (bf16[480,384]{1,0:T(8,128)(2,1)S(1)}, bf16[480,384]{1,0:T(8,128)(2,1)S(1)}, u32[]{:S(2)}, u32[]{:S(2)}) collective-permute-start(bf16[480,384]{1,0:T(8,128)(2,1)S(1)} %copy-done.26), channel_id=1, source_target_pairs={{0,24},{8,16},{16,8},{24,0},{1,25},{9,17},{17,9},{25,1},{2,26},{10... | collective-permute-start | bytes 1105928 | tf_op jit(solution)/shard_map/ppermute | solution.py:606
  292.8 32.3 %all-to-all-start.2 = ((bf16[4,80,164]{2,1,0:T(8,128)(2,1)}), bf16[4,80,164]{2,1,0:T(8,128)(2,1)S(1)}, u32[]{:S(2)}, u32[]{:S(2)}) async-start(bf16[4,80,164]{2,1,0:T(8,128)(2,1)} %pad_maximum_fusion.2), calls=%async_computation.2 | async-start | bytes 327680 | tf_op jit(solution)/shard_map/all_to_all | solution.py:612
  (26 other events, 131.8 us)
Sparse Core Ops, SparseCore 0:
  10.7 89.4 all-gather.6
  101.8 50.6 all-gather.12
  174.1 43.6 all-gather.8
  220.5 54.5 reduce-scatter.1
  276.5 49.8 all-gather.10

commit v3 on v2

--- a/solution.py
+++ b/solution.py
@@ -14,6 +14,7 @@
 BQ = 256
 BK = 256
 STEP = 256
+STEPS = 3
 BF16 = jnp.bfloat16
 F32 = jnp.float32
 VMEM_LIMIT = 56 * 1024 * 1024
@@ -49,7 +50,7 @@
 
 def project_kernel(
     lens, x_ref, gain_ref, shift_ref, w_ref,
-    unit_ref, q_ref, k_ref, qt_ref, kt_ref, vt_ref, segc_ref, segr_ref, bounds_ref, full_ref, out_ref,
+    q_ref, k_ref, qt_ref, kt_ref, vt_ref, seg_ref, bounds_ref, full_ref, out_ref,
 ):
     across, kinds, _, narrow = w_ref.shape
 
@@ -62,82 +63,78 @@
             for copy in range(out_ref.shape[0]):
                 out_ref[copy, :, spot] = w_ref[part, kinds - 1]
 
-    block = pl.program_id(0)
-    first = block * BQ
-    last = first + BQ - 1
-    heads = q_ref.shape[0]
+    size = x_ref.shape[0]
+    first = pl.program_id(0) * size
+    tiles = size // BQ
     end = jnp.int32(0)
-    low = jnp.int32(0)
-    high = jnp.int32(pl.num_programs(0) * BQ)
-    rows = first + lax.broadcasted_iota(jnp.int32, segc_ref.shape, 0)
-    cols = first + lax.broadcasted_iota(jnp.int32, segr_ref.shape, 1)
-    seg_rows = jnp.zeros(segc_ref.shape, jnp.int32)
-    seg_cols = jnp.zeros(segr_ref.shape, jnp.int32)
+    low = [jnp.int32(0)] * tiles
+    high = [jnp.int32(0) + pl.num_programs(0) * size] * tiles
+    cols = first + lax.broadcasted_iota(jnp.int32, seg_ref.shape, 1)
+    segment = jnp.zeros(seg_ref.shape, jnp.int32)
     for item in range(lens.shape[1]):
         end = end + lens[0, item]
-        low = jnp.where(end <= first, end, low)
-        high = jnp.where((end > last) & (end < high), end, high)
-        seg_rows = seg_rows + (rows >= end).astype(jnp.int32)
-        seg_cols = seg_cols + (cols >= end).astype(jnp.int32)
-    segc_ref[...] = seg_rows
-    segr_ref[...] = seg_cols
-    low = lax.div(low, jnp.int32(STEP))
-    high = lax.div(high + (STEP - 1), jnp.int32(STEP))
-    steps = lax.div((high - low) * STEP + (BK - 1), jnp.int32(BK))
-    room = pl.num_programs(0) * (BQ // STEP) - steps * (BK // STEP)
-    bounds_ref[block, 0] = jnp.minimum(low, room)
-    bounds_ref[block, 1] = steps
+        for tile in range(tiles):
+            start = first + tile * BQ
+            low[tile] = jnp.where(end <= start, end, low[tile])
+            later = (end > start + (BQ - 1)) & (end < high[tile])
+            high[tile] = jnp.where(later, end, high[tile])
+        segment = segment + (cols >= end).astype(jnp.int32)
+    seg_ref[...] = segment.astype(F32)
+    for tile in range(tiles):
+        lowest = lax.div(low[tile], jnp.int32(STEP))
+        highest = lax.div(high[tile] + (STEP - 1), jnp.int32(STEP))
+        steps = lax.div((highest - lowest) * STEP + (BK - 1), jnp.int32(BK))
+        room = pl.num_programs(0) * (size // STEP) - steps * (BK // STEP)
+        block = pl.program_id(0) * tiles + tile
+        bounds_ref[block, 0] = jnp.minimum(lowest, room)
+        bounds_ref[block, 1] = steps
     unit, _ = normalized(x_ref[...].astype(F32))
     xn = (unit * gain_ref[0:1, :].astype(F32) + shift_ref[0:1, :].astype(F32)).astype(BF16)
-    unit_ref[...] = unit.astype(BF16)
     for item, (rows_ref, cols_ref) in enumerate(((q_ref, qt_ref), (k_ref, kt_ref), (None, vt_ref))):
         cols_ref[...] = dot_nt(full_ref[item], xn).astype(BF16)
         if rows_ref is not None:
             full = dot_nt(xn, full_ref[item]).astype(BF16)
-            for head in range(heads):
+            for head in range(q_ref.shape[0]):
                 rows_ref[head] = full[:, head * HD : (head + 1) * HD]
 
 
 def project(lens, tokens, gains, shifts, weights, depth):
     count, dim = tokens.shape
     width = weights.shape[2]
+    blocks = count // BQ
+    size = count // STEPS
     heads = width // HD
-    blocks = count // BQ
-    per_head = pl.BlockSpec((heads, BQ, HD), lambda i: (0, i, 0))
-    turned = pl.BlockSpec((width, BQ), lambda i: (0, i))
+    per_head = pl.BlockSpec((heads, size, HD), lambda i: (0, i, 0))
+    turned = pl.BlockSpec((width, size), lambda i: (0, i))
     fixed2 = pl.BlockSpec((2, dim), lambda i: (0, 0))
     return pl.pallas_call(
         project_kernel,
-        grid=(blocks,),
+        grid=(STEPS,),
         in_specs=[
             pl.BlockSpec(memory_space=pltpu.SMEM),
-            pl.BlockSpec((BQ, dim), lambda i: (i, 0)),
+            pl.BlockSpec((size, dim), lambda i: (i, 0)),
             fixed2,
             fixed2,
             pl.BlockSpec(weights.shape, lambda i: (0, 0, 0, 0)),
         ],
         out_specs=[
-            pl.BlockSpec((BQ, dim), lambda i: (i, 0)),
             per_head,
             per_head,
             turned,
             turned,
             turned,
-            pl.BlockSpec((BQ, 128), lambda i: (i, 0)),
-            pl.BlockSpec((8, BQ), lambda i: (0, i)),
+            pl.BlockSpec((8, size), lambda i: (0, i)),
             pl.BlockSpec(memory_space=pltpu.SMEM),
             pl.BlockSpec((3, width, dim), lambda i: (0, 0, 0)),
             pl.BlockSpec((depth, width, dim), lambda i: (0, 0, 0)),
         ],
         out_shape=[
-            jax.ShapeDtypeStruct((count, dim), BF16),
             jax.ShapeDtypeStruct((heads, count, HD), BF16),
             jax.ShapeDtypeStruct((heads, count, HD), BF16),
             jax.ShapeDtypeStruct((width, count), BF16),
             jax.ShapeDtypeStruct((width, count), BF16),
             jax.ShapeDtypeStruct((width, count), BF16),
-            jax.ShapeDtypeStruct((count, 128), jnp.int32),
-            jax.ShapeDtypeStruct((8, count), jnp.int32),
+            jax.ShapeDtypeStruct((8, count), F32),
             jax.ShapeDtypeStruct((blocks, 2), jnp.int32),
             jax.ShapeDtypeStruct((3, width, dim), BF16),
             jax.ShapeDtypeStruct((depth, width, dim), BF16),
@@ -156,11 +153,18 @@
     return pl.ds(pl.multiple_of((layer[0] ^ item) * size, 128), size)
 
 
+def column_of(row_ref, column_ref):
+    for start in range(0, column_ref.shape[0], BK):
+        turned = row_ref[:, start : start + BK].T
+        column_ref[start : start + BK, :] = jnp.broadcast_to(turned[:, 0:1], (BK, 128))
+
+
 def attend_kernel(
-    first, heads, parts, layer, bounds, segc_ref, segr_ref, k_ref, qt_ref, vt_ref, *refs
+    first, heads, parts, layer, bounds, segr_ref, k_ref, qt_ref, vt_ref, *refs
 ):
-    part_refs, (ot_ref, lse_ref) = refs[:parts], refs[parts:]
+    part_refs, (ot_ref, lse_ref, segc_ref) = refs[:parts], refs[parts:]
     count = segc_ref.shape[0]
+    column_of(segr_ref, segc_ref)
     factor = SCALE * LOG2E
 
     def q_block(block, _):
@@ -198,42 +202,44 @@
         done = lax.fori_loop(0, bounds[block, 1], k_block, (empty,) * heads)
         for h in range(heads):
             top, total, acc = done[h]
-            ot_ref[h * HD : (h + 1) * HD, pl.ds(start, BQ)] = acc / total
+            ot_ref[h * HD : (h + 1) * HD, pl.ds(start, BQ)] = (acc / total).astype(BF16)
             lse_ref[h : h + 1, pl.ds(start, BQ)] = top * factor + jnp.log(total) * LOG2E
         return 0
 
     lax.fori_loop(0, count // BQ, q_block, 0)
     size = count // parts
     for part in range(parts):
-        part_refs[part][...] = ot_ref[:, spot_of(layer, part, size)].astype(BF16)
+        part_refs[part][...] = ot_ref[:, spot_of(layer, part, size)]
 
 
 def attend(first, heads, parts, layer, tables, k_rows, q_cols, v_cols):
-    segc, segr, bounds = tables
-    count = segc.shape[0]
+    segr, bounds = tables
+    count = segr.shape[1]
     out = pl.pallas_call(
         partial(attend_kernel, first, heads, parts),
-        in_specs=[pl.BlockSpec(memory_space=pltpu.SMEM)] * 2 + [vmem()] * 5,
+        in_specs=[pl.BlockSpec(memory_space=pltpu.SMEM)] * 2 + [vmem()] * 4,
         out_specs=[vmem()] * (parts + 2),
         out_shape=[jax.ShapeDtypeStruct((heads * HD, count // parts), BF16)] * parts
         + [
-            jax.ShapeDtypeStruct((heads * HD, count), F32),
+            jax.ShapeDtypeStruct((heads * HD, count), BF16),
             jax.ShapeDtypeStruct((8, count), F32),
         ],
+        scratch_shapes=[pltpu.VMEM((count, 128), F32)],
         compiler_params=pltpu.CompilerParams(vmem_limit_bytes=VMEM_LIMIT),
         cost_estimate=COST,
         name=f"attend_{first}",
-    )(layer, bounds, segc, segr, k_rows, q_cols, v_cols)
+    )(layer, bounds, segr, k_rows, q_cols, v_cols)
     return out[:parts], out[parts], out[parts + 1]
 
 
 def attend_back_kernel(
-    first, heads, parts, layer, bounds, segc_ref, segr_ref,
+    first, heads, parts, layer, bounds, segr_ref,
     q_ref, k_ref, qt_ref, kt_ref, vt_ref, ot_ref, lse_ref, *refs,
 ):
     part_refs, out_refs, refs = refs[:parts], refs[parts : 2 * parts], refs[2 * parts :]
-    flat_ref, dot_ref, do_ref, stat_ref, dq_ref, dqt_ref, dkt_ref, dvt_ref = refs
+    flat_ref, segc_ref, dot_ref, do_ref, stat_ref, dq_ref, dqt_ref, dkt_ref, dvt_ref = refs
     count = segc_ref.shape[0]
+    column_of(segr_ref, segc_ref)
     factor = SCALE * LOG2E
     size = count // parts
     for part in range(parts):
@@ -251,7 +257,11 @@
         for h in range(heads):
             lane = slice(h * HD, (h + 1) * HD)
             stats.append(
-                jnp.sum(dot_ref[lane, spot].astype(F32) * ot_ref[lane, spot], axis=0, keepdims=True)
+                jnp.sum(
+                    dot_ref[lane, spot].astype(F32) * ot_ref[lane, spot].astype(F32),
+                    axis=0,
+                    keepdims=True,
+                )
             )
         stats.append(jnp.zeros((8 - 2 * heads, BQ), F32)) if heads < 4 else None
         turned = jnp.concatenate(stats, axis=0).T
@@ -300,17 +310,18 @@
 
 
 def attend_back(first, heads, layer, tables, q_rows, k_rows, q_cols, k_cols, v_cols, out, lse, dout):
-    segc, segr, bounds = tables
-    count = segc.shape[0]
+    segr, bounds = tables
+    count = segr.shape[1]
     parts = len(dout)
     width = heads * HD
     result = pl.pallas_call(
         partial(attend_back_kernel, first, heads, parts),
-        in_specs=[pl.BlockSpec(memory_space=pltpu.SMEM)] * 2 + [vmem()] * (9 + parts),
+        in_specs=[pl.BlockSpec(memory_space=pltpu.SMEM)] * 2 + [vmem()] * (8 + parts),
         out_specs=[vmem()] * (parts + 1),
         out_shape=[jax.ShapeDtypeStruct((3 * width, count // parts), BF16)] * parts
         + [jax.ShapeDtypeStruct((3 * width, count), BF16)],
         scratch_shapes=[
+            pltpu.VMEM((count, 128), F32),
             pltpu.VMEM((width, count), BF16),
             pltpu.VMEM((heads, count, HD), BF16),
             pltpu.VMEM((2 * heads, BQ, 128), F32),
@@ -322,7 +333,7 @@
         compiler_params=pltpu.CompilerParams(vmem_limit_bytes=VMEM_LIMIT),
         cost_estimate=COST,
         name=f"attend_back_{first}",
-    )(layer, bounds, segc, segr, q_rows, k_rows, q_cols, k_cols, v_cols, out, lse, *dout)
+    )(layer, bounds, segr, q_rows, k_rows, q_cols, k_cols, v_cols, out, lse, *dout)
     return result[:parts], result[parts]
 
 
@@ -393,8 +404,8 @@
 
     @pl.when(item == pl.num_programs(0) - 1)
     def _():
-        y_out[...] = y_ref[:mine, :]
-        dx_out[...] = dx_ref[:mine, :]
+        y_out[...] = y_ref[:mine, :].astype(BF16)
+        dx_out[...] = dx_ref[:mine, :].astype(BF16)
         y_far[...] = y_ref[mine:, :].astype(BF16)
         dx_far[...] = dx_ref[mine:, :].astype(BF16)
 
@@ -411,8 +422,7 @@
         grid=(blocks,),
         in_specs=[whole] * 4 + [pl.BlockSpec((dim, 2 * hidden), lambda i: (i, 0))],
         out_specs=[whole] * 4 + [act] * 2,
-        out_shape=[jax.ShapeDtypeStruct((mine, dim), F32)] * 2
-        + [jax.ShapeDtypeStruct((mine, dim), BF16)] * 2
+        out_shape=[jax.ShapeDtypeStruct((mine, dim), BF16)] * 4
         + [jax.ShapeDtypeStruct((count, blocks * hidden), BF16)] * 2,
         scratch_shapes=[pltpu.VMEM((count, dim), F32)] * 2 + [pltpu.VMEM((count, dim), BF16)] * 2,
         compiler_params=pltpu.CompilerParams(vmem_limit_bytes=VMEM_LIMIT),
@@ -471,7 +481,7 @@
     dx2_ref, gout_ref, sums_ref = refs[7:10]
     dot_refs = refs[10:]
     middle = x2_ref[...]
-    grad = dx_ref[...] + core_ref[...].astype(F32) + near_ref[...].astype(F32)
+    grad = dx_ref[...].astype(F32) + core_ref[...].astype(F32) + near_ref[...].astype(F32)
     back, prod = norm_backward(middle, gain_ref[1:2, :].astype(F32), grad)
     dx2 = dy_ref[...].astype(F32) + back
     dx2_ref[...] = dx2
@@ -538,9 +548,10 @@
     )(layer, *parts, w_qkv, rows, dx2, gains)
 
 
-def small_kernel(flat_ref, unit_ref, w_ref, gain_ref, shift_ref, gout_ref, sums_ref, out_ref):
-    dim = unit_ref.shape[1]
-    inner = dot(flat_ref[...], unit_ref[...])
+def small_kernel(flat_ref, x_ref, w_ref, gain_ref, shift_ref, gout_ref, sums_ref, out_ref):
+    dim = x_ref.shape[1]
+    unit, _ = normalized(x_ref[...].astype(F32))
+    inner = dot(flat_ref[...], unit.astype(BF16))
     sums = jnp.sum(flat_ref[...].astype(F32), axis=1, keepdims=True)
     grad = inner * gain_ref[0:1, :].astype(F32) + sums * shift_ref[0:1, :].astype(F32)
     width = w_ref.shape[1]
@@ -559,8 +570,8 @@
     out_ref[:, dim + side :] = sums.T.astype(BF16)
 
 
-def small(flat, unit, w_qkv, gains, shifts, grad_out, sums):
-    side, dim = flat.shape[0], unit.shape[1]
+def small(flat, rows, w_qkv, gains, shifts, grad_out, sums):
+    side, dim = flat.shape[0], rows.shape[1]
     total = -(-(dim + side + 8) // 128) * 128
     return pl.pallas_call(
         small_kernel,
@@ -570,7 +581,7 @@
         compiler_params=pltpu.CompilerParams(vmem_limit_bytes=VMEM_LIMIT),
         cost_estimate=COST,
         name="small",
-    )(flat, unit, w_qkv, gains, shifts, grad_out, sums)
+    )(flat, rows, w_qkv, gains, shifts, grad_out, sums)
 
 
 def collect_kernel(layer, *refs):
@@ -591,6 +602,22 @@
         cost_estimate=COST,
         name="collect",
     )(layer, *parts)
+
+
+def keep_kernel(source_ref, out_ref):
+    out_ref[...] = source_ref[...]
+
+
+def keep(value):
+    return pl.pallas_call(
+        keep_kernel,
+        in_specs=[vmem()],
+        out_specs=vmem(),
+        out_shape=jax.ShapeDtypeStruct(value.shape, value.dtype),
+        compiler_params=pltpu.CompilerParams(vmem_limit_bytes=VMEM_LIMIT),
+        cost_estimate=COST,
+        name="keep",
+    )(value)
 
 
 WIDE = ("far", "near", "core")
@@ -649,7 +676,7 @@
     dy_own = (dy, swap(dy, "core"))
     dy_far = (dy_near, swap(dy_near, "core"))
 
-    unit, q_rows, k_rows, q_cols, k_cols, v_cols, *tables, w_proj, w_out = project(
+    q_rows, k_rows, q_cols, k_cols, v_cols, *tables, w_proj, w_out = project(
         seq_lens, tokens, norm_gains, norm_shifts, pieces, depth
     )
     w_out = exchange(w_out, "narrow")
@@ -675,7 +702,8 @@
     dout = spread(dout)
     y_core, y_far = (swap(part, "core") for part in (y_core, y_far))
     y_near = swap(add(y_b, y_far), "near")
-    out_mine = (x2 + y_a + y_core.astype(F32) + y_near.astype(F32)).astype(BF16)
+    out_mine = x2 + y_a.astype(F32) + y_core.astype(F32) + y_near.astype(F32)
+    out_mine = out_mine.astype(BF16)
     dout, out_mine = lax.optimization_barrier((dout, out_mine))
     layer_out = lax.all_gather(out_mine, "narrow", axis=0, tiled=True)
     back, flat_back = attend_back(
@@ -691,16 +719,15 @@
     total = lax.psum_scatter(total, "narrow", scatter_dimension=0, tiled=True).astype(F32)
 
     back = spread(back)
-    in_mine = finish(layers, back, w_proj_all, rows, dx2, norm_gains)
+    rest = small(flat_back, tokens, w_proj, norm_gains, norm_shifts, grad_out, norm_two)
+    in_mine = finish(layers, back, w_proj_all, rows, after(dx2, rest), norm_gains)
     input_grad = lax.all_gather(in_mine, "narrow", axis=0, tiled=True)
 
     side = 3 * width
     part = dim // across
-    rest = small(
-        after(flat_back, in_mine), unit, w_proj, norm_gains, norm_shifts, grad_out, norm_two
-    )
-    rest = exchange(rest.reshape(across, part, -1), WIDE)
+    rest = exchange(after(rest, in_mine).reshape(across, part, -1), WIDE)
     rest = jnp.sum(rest.astype(F32), axis=0)
+    layer_out = keep(after(layer_out, rest))
     gqkv = rest[:, dim : dim + side].reshape(part, 3, width).transpose(1, 0, 2)
     gout = rest[:, :dim].astype(BF16).reshape(part, depth, width).transpose(1, 0, 2)
     norms = rest[:, dim + side : dim + side + 4].astype(BF16)

time: 341 us -> 336 us (0.985)
  Pallas kernels: 126 us -> 116 us
  waiting for transfers between devices: 83.2 us -> 88.5 us
    ppermute x13, waiting for transfers between devices: 3.74 us -> 10.7 us  [swap(): return lax.ppermute(value, axis, [(0, 1), (1, 0)])]
    pallas_call x1, Pallas kernels: 34.8 us -> 28.1 us  [attend_back(): pl.pallas_call(partial(attend_back_kernel, first, heads, parts), in_specs...]
    pallas_call x1, Pallas kernels: 22.4 us -> 17.3 us  [attend(): pl.pallas_call(partial(attend_kernel, first, heads, parts), in_specs=[pl....]
    unnamed x65 -> x62, local copies, waits for them, and re-layouts: 12.9 us -> 11.5 us
    pallas_call x1 -> x2, Pallas kernels: 11.3 us -> 12.3 us  [the longest x1 9.29 us: project(): pl.pallas_call(project_kernel, grid=(STEPS,), in_specs=[pl.BlockSpec(memo...]
  transfers between devices with their start and end apart: 29 -> 29, of which waited for: 9 -> 11; matrix products, arithmetic and copies ran while one was open for 5% -> 5% of each run, Pallas kernels for 37% -> 34%
where the time goes in v3:
time: 336 us; the launch traced here: 335 us
  Pallas kernels  116 us (35%)
  waiting for transfers between devices  88.5 us (26%)
  starting transfers between devices  49.9 us (15%)
  blocking collectives  39.3 us (12%)
  local copies, waits for them, and re-layouts  17.3 us (5%)
  between operations  14.1 us (4%)
  other arithmetic  10.6 us (3%)
    ppermute x9, waiting for transfers between devices, spread(): lax.ppermute(parts[bit], 'narrow', [(i, i ^ bit) for i in range(size)])  65.8 us
    pallas_call x1, Pallas kernels, attend_back(): pl.pallas_call(partial(attend_back_kernel, first, heads, parts), in_specs...  28.1 us
    all_to_all x2, starting transfers between devices, exchange(): return lax.all_to_all(value, axis, 0, 0, tiled=True)  25.6 us
    all_to_all x1, blocking collectives, exchange(): return lax.all_to_all(value, axis, 0, 0, tiled=True)  24.8 us
    pallas_call x2, Pallas kernels, ffn(): pl.pallas_call(ffn_kernel, grid=(blocks,), in_specs=[whole] * 4 + [pl.Blo...  24.6 us
    pallas_call x1, Pallas kernels, attend(): pl.pallas_call(partial(attend_kernel, first, heads, parts), in_specs=[pl....  17.3 us
    ppermute x9, starting transfers between devices, spread(): lax.ppermute(parts[bit], 'narrow', [(i, i ^ bit) for i in range(size)])  17.3 us
    all_gather x1, blocking collectives, local(): lax.all_gather(jnp.concatenate([jnp.swapaxes(w_qkv, 1, 2), w_attn_out[Non...  14.4 us
  transfers between devices with their start and end apart: 29, of which 11 were waited for; matrix products, arithmetic and copies ran while one was open for 5% of the time, Pallas kernels for 34%

profile of v3, /device:TPU:0, one launch (start us, length us, event | category | flops | bytes accessed | tf_op | source)
XLA Modules:
  0.0 335.3 jit_solution(7116669849909588367)
XLA Ops:
  11.1 14.4 %all-gather = bf16[32,160,80]{2,1,0:T(8,128)(2,1)} all-gather(bf16[4,160,80]{2,1,0:T(8,128)(2,1)S(1)} %pad_maximum_fusion.1), channel_id=2, replica_groups=mesh['narrow'=4,'far'=2,'near'=2,'core'=2] {'far','near','core'}, dimensions={0}, use_global_device_ids=true | all-gather | bytes 921600 | tf_op jit(solution)/shard_map/all_gather | solution.py:663
  25.5 9.3 %project.1 = (bf16[5,1536,32]{2,1,0:T(8,128)(2,1)}, bf16[5,1536,32]{2,1,0:T(8,128)(2,1)}, bf16[160,1536]{1,0:T(8,128)(2,1)}, bf16[160,1536]{1,0:T(8,128)(2,1)}, ...) custom-call(s32[1,16]{1,0:T(1,128)} %lens.1, ...), custom_call_target="tpu_custom_call" | custom-call | flops 1000000 | bytes 100000 | tf_op jit(solution)/shard_map/project/pallas_call | solution.py:110
  34.8 5.3 %all-to-all-start = ((bf16[4,160,640]{2,1,0:T(8,128)(2,1)}), bf16[4,160,640]{2,1,0:T(8,128)(2,1)S(1)}, u32[]{:S(2)}, u32[]{:S(2)}) async-start(bf16[4,160,640]{2,1,0:T(8,128)(2,1)} %get-tuple-element.66), calls=%async_computation | async-start | bytes 1638400 | tf_op jit(solution)/shard_map/all_to_all | solution.py:639
  41.7 17.3 %attend_0.1 = (bf16[160,384]{1,0:T(8,128)(2,1)}, bf16[160,384]{1,0:T(8,128)(2,1)}, bf16[160,384]{1,0:T(8,128)(2,1)}, bf16[160,384]{1,0:T(8,128)(2,1)}, bf16[160,1536]{1,0:T(8,128)(2,1)}, /*index=5*/f32[8,1536]{1,0:T(8,128)}) custom-call(s32[1]{0:T(128)} %bitcast.layer, s32[6,2]{1,0:T(8,128)} %get-tuple-element.67.bounds, ...), custom_call_target="tpu_custom_call" | custom-call | flops 1000000 | bytes 100000 | tf_op jit(solution)/shard_map/attend_0/pallas_call | solution.py:218
  59.0 2.2 collective-permute-start
  61.2 2.3 collective-permute-start.1
  65.5 4.3 %collective-permute-done.refs_1_ = bf16[160,384]{1,0:T(8,128)(2,1)S(1)} collective-permute-done((bf16[160,384]{1,0:T(8,128)(2,1)}, bf16[160,384]{1,0:T(8,128)(2,1)S(1)}, u32[]{:S(2)}, u32[]{:S(2)}) %collective-permute-start) | collective-permute-done | bytes 122912 | tf_op jit(solution)/shard_map/ppermute | solution.py:633
  69.9 24.8 %collective-permute-done.1.refs_2_ = bf16[160,384]{1,0:T(8,128)(2,1)S(1)} collective-permute-done((bf16[160,384]{1,0:T(8,128)(2,1)}, bf16[160,384]{1,0:T(8,128)(2,1)S(1)}, u32[]{:S(2)}, u32[]{:S(2)}) %collective-permute-start.1) | collective-permute-done | bytes 122912 | tf_op jit(solution)/shard_map/ppermute | solution.py:633
  95.7 3.7 %mix.1 = (f32[384,640]{1,0:T(8,128)}, bf16[384,640]{1,0:T(8,128)(2,1)}, bf16[4,160,384]{2,1,0:T(8,128)(2,1)}) custom-call(s32[1]{0:T(128)} %bitcast.layer, bf16[160,384]{1,0:T(8,128)(2,1)} %get-tuple-element.72.refs_0_, bf16[160,384]{1,0:T(8,128)(2,1)} %copy-done.21, bf16[160,384]{1,0:T(8,128)(2,1)} %copy-done.22, bf16[160,384]{1,0:T(8,128)(2,1)} %copy-done.23, ...), custom_call_target="tpu_custom_call" | custom-call | flops 1000000 | bytes 100000 | tf_op jit(solution)/shard_map/mix/pallas_call | solution.py:356
  102.3 12.3 %ffn.2 = (bf16[384,640]{1,0:T(8,128)(2,1)}, bf16[384,640]{1,0:T(8,128)(2,1)}, bf16[384,640]{1,0:T(8,128)(2,1)}, bf16[384,640]{1,0:T(8,128)(2,1)}, bf16[768,1280]{1,0:T(8,128)(2,1)}, /*index=5*/bf16[768,1280]{1,0:T(8,128)(2,1)}) custom-call(bf16[384,640]{1,0:T(8,128)(2,1)} %get-tuple-element.77.refs_0_, bf16[384,640]{1,0:T(8,128)(2,1)} %copy-done.9, ...), custom_call_target="tpu_custom_call" | custom-call | flops 1000000 | bytes 100000 | tf_op jit(solution)/shard_map/ffn/pallas_call | solution.py:420
  117.3 12.3 %ffn.3 = (bf16[384,640]{1,0:T(8,128)(2,1)}, bf16[384,640]{1,0:T(8,128)(2,1)}, bf16[384,640]{1,0:T(8,128)(2,1)}, bf16[384,640]{1,0:T(8,128)(2,1)}, bf16[768,1280]{1,0:T(8,128)(2,1)}, /*index=5*/bf16[768,1280]{1,0:T(8,128)(2,1)}) custom-call(bf16[384,640]{1,0:T(8,128)(2,1)} %copy-done.10, bf16[384,640]{1,0:T(8,128)(2,1)} %copy-done.12, ...), custom_call_target="tpu_custom_call" | custom-call | flops 1000000 | bytes 100000 | tf_op jit(solution)/shard_map/ffn/pallas_call | solution.py:420
  137.0 12.3 %outer.1 = bf16[2,640,1280]{2,1,0:T(8,128)(2,1)} custom-call(s32[1]{0:T(128)} %bitcast.4._, bf16[384,640]{1,0:T(8,128)(2,1)} %get-tuple-element.77.refs_0_, bf16[384,640]{1,0:T(8,128)(2,1)} %copy-done.9, bf16[384,640]{1,0:T(8,128)(2,1)} %copy-done.10, bf16[384,640]{1,0:T(8,128)(2,1)} %copy-done.12, bf16[384,640]{1,0:T(8,128)(2,1)} %copy-done.3, ...), custom_call_target="tpu_custom_call" | custom-call | flops 1000000 | bytes 100000 | tf_op jit(solution)/shard_map/outer/pallas_call | solution.py:463
  150.3 5.5 %turn.1 = (f32[384,640]{1,0:T(8,128)}, bf16[640,640]{1,0:T(8,128)(2,1)}, f32[8,640]{1,0:T(8,128)}, bf16[160,384]{1,0:T(8,128)(2,1)}, bf16[160,384]{1,0:T(8,128)(...) custom-call(s32[1]{0:T(128)} %bitcast.layer, bf16[4,160,640]{2,1,0:T(8,128)(2,1)} %copy-done.4, ...), custom_call_target="tpu_custom_call" | custom-call | flops 1000000 | bytes 100000 | tf_op jit(solution)/shard_map/turn/pallas_call | solution.py:507
  155.8 4.4 %collective-permute-start.12 = (bf16[160,384]{1,0:T(8,128)(2,1)}, bf16[160,384]{1,0:T(8,128)(2,1)S(1)}, u32[]{:S(2)}, u32[]{:S(2)}) collective-permute-start(bf16[160,384]{1,0:T(8,128)(2,1)} %get-tuple-element.91), channel_id=1, source_target_pairs={{0,8},{8,0},{16,24},{24,16},{1,9},{9,1},{17,25},{25,17},{2,10},{10... | collective-permute-start | bytes 368648 | tf_op jit(solution)/shard_map/ppermute | solution.py:633
  160.2 2.4 collective-permute-start.14
  162.6 2.2 add_convert_fusion.1
  164.8 6.9 %collective-permute-done.13.refs_2_ = bf16[160,384]{1,0:T(8,128)(2,1)S(1)} collective-permute-done((bf16[160,384]{1,0:T(8,128)(2,1)}, bf16[160,384]{1,0:T(8,128)(2,1)S(1)}, u32[]{:S(2)}, u32[]{:S(2)}) %collective-permute-start.13) | collective-permute-done | bytes 122912 | tf_op jit(solution)/shard_map/ppermute | solution.py:633
  173.3 2.0 collective-permute-start.18
  175.3 28.1 %attend_back_0.1 = (bf16[480,384]{1,0:T(8,128)(2,1)}, bf16[480,384]{1,0:T(8,128)(2,1)}, bf16[480,384]{1,0:T(8,128)(2,1)}, bf16[480,384]{1,0:T(8,128)(2,1)}, bf16[480,1536]{1,0:T(8,128)(2,1)}) custom-call(s32[1]{0:T(128)} %bitcast.layer, s32[6,2]{1,0:T(8,128)} %get-tuple-element.67.bounds, f32[8,1536]{1,0:T(8,128)} %get-tuple-element.68.segr_ref, ...), custom_call_target="tpu_custom_call" | custom-call | flops 1000000 | bytes 100000 | tf_op jit(solution)/shard_map/attend_back_0/pallas_call | solution.py:317
  203.4 6.4 %collective-permute-done.18 = bf16[640,1280]{1,0:T(8,128)(2,1)S(1)} collective-permute-done((bf16[640,1280]{1,0:T(8,128)(2,1)}, bf16[640,1280]{1,0:T(8,128)(2,1)S(1)}, u32[]{:S(2)}, u32[]{:S(2)}) %collective-permute-start.18) | collective-permute-done | bytes 1638432 | tf_op jit(solution)/shard_map/ppermute | solution.py:627
  211.7 3.4 %collective-permute-start.19 = (bf16[480,384]{1,0:T(8,128)(2,1)S(1)}, bf16[480,384]{1,0:T(8,128)(2,1)S(1)}, u32[]{:S(2)}, u32[]{:S(2)}) collective-permute-start(bf16[480,384]{1,0:T(8,128)(2,1)S(1)} %copy-done.27), channel_id=1, source_target_pairs={{0,8},{8,0},{16,24},{24,16},{1,9},{9,1},{17,25},{25,17},{2,10},{10... | collective-permute-start | bytes 1105928 | tf_op jit(solution)/shard_map/ppermute | solution.py:633
  215.1 2.4 collective-permute-start.21
  217.5 5.9 %small.1 = bf16[640,1152]{1,0:T(8,128)(2,1)} custom-call(bf16[480,1536]{1,0:T(8,128)(2,1)} %get-tuple-element.106.flat_ref, bf16[1536,640]{1,0:T(8,128)(2,1)} %x_ref.3, bf16[3,160,640]{2,1,0:T(8,128)(2,1)} %get-tuple-element.107.w_ref, bf16[2,640]{1,0:T(2,128)(2,1)} %refs_7_.3, bf16[2,640]{1,0:T(2,128)(2,1)} %shift_ref.3, ...), custom_call_target="tpu_custom_call" | custom-call | flops 1000000 | bytes 100000 | tf_op jit(solution)/shard_map/small/pallas_call | solution.py:576
  223.4 6.0 %collective-permute-done.19.refs_1_ = bf16[480,384]{1,0:T(8,128)(2,1)S(1)} collective-permute-done((bf16[480,384]{1,0:T(8,128)(2,1)S(1)}, bf16[480,384]{1,0:T(8,128)(2,1)S(1)}, u32[]{:S(2)}, u32[]{:S(2)}) %collective-permute-start.19) | collective-permute-done | bytes 368672 | tf_op jit(solution)/shard_map/ppermute | solution.py:633
  229.4 23.7 %collective-permute-done.20.refs_2_ = bf16[480,384]{1,0:T(8,128)(2,1)S(1)} collective-permute-done((bf16[480,384]{1,0:T(8,128)(2,1)S(1)}, bf16[480,384]{1,0:T(8,128)(2,1)S(1)}, u32[]{:S(2)}, u32[]{:S(2)}) %collective-permute-start.20) | collective-permute-done | bytes 368672 | tf_op jit(solution)/shard_map/ppermute | solution.py:633
  254.0 5.8 %finish.1 = bf16[384,640]{1,0:T(8,128)(2,1)} custom-call(s32[1]{0:T(128)} %bitcast.layer, bf16[480,384]{1,0:T(8,128)(2,1)} %get-tuple-element.114.refs_0_, bf16[480,384]{1,0:T(8,128)(2,1)} %copy-done.16, bf16[480,384]{1,0:T(8,128)(2,1)} %copy-done.17, bf16[480,384]{1,0:T(8,128)(2,1)} %copy-done.18, bf16[4,3,160,640]{3,2,1,0:T(8,128)(2,1)} %bitcast.21, ...), custom_call_target="tpu_custom_call" | custom-call | flops 1000000 | bytes 100000 | tf_op jit(solution)/shard_map/finish/pallas_call | solution.py:540
  259.9 24.8 %all_to_all.15 = bf16[8,80,1152]{2,1,0:T(8,128)(2,1)S(1)} all-to-all(bf16[8,80,1152]{2,1,0:T(8,128)(2,1)S(1)} %bitcast.19), channel_id=1, replica_groups=mesh['narrow'=4,'far'=2,'near'=2,'core'=2] {'far','near','core'}, dimensions={0} | all-to-all | bytes 2949120 | tf_op jit(solution)/shard_map/all_to_all | solution.py:639
  286.0 20.3 %all-to-all-start.2 = ((bf16[4,80,164]{2,1,0:T(8,128)(2,1)}), bf16[4,80,164]{2,1,0:T(8,128)(2,1)S(1)}, u32[]{:S(2)}, u32[]{:S(2)}) async-start(bf16[4,80,164]{2,1,0:T(8,128)(2,1)} %pad_maximum_fusion.2), calls=%async_computation.2 | async-start | bytes 327680 | tf_op jit(solution)/shard_map/all_to_all | solution.py:639
  307.3 11.2 %all-to-all-done.2 = bf16[4,80,164]{2,1,0:T(8,128)(2,1)S(1)} async-done(((bf16[4,80,164]{2,1,0:T(8,128)(2,1)}), bf16[4,80,164]{2,1,0:T(8,128)(2,1)S(1)}, u32[]{:S(2)}, u32[]{:S(2)}) %all-to-all-start.2) | async-done | bytes 104992 | tf_op jit(solution)/shard_map/all_to_all | solution.py:639
  320.6 3.0 keep.1
  323.6 2.0 fusion
  325.6 3.1 copy.36
  (128 shorter events, 30.9 us)
Async XLA Ops:
  7.2 33.8 %copy-start = (bf16[1536,640]{1,0:T(8,128)(2,1)S(1)}, bf16[1536,640]{1,0:T(8,128)(2,1)}, u32[]{:S(2)}) copy-start(bf16[1536,640]{1,0:T(8,128)(2,1)} %param.10) | copy-start | bytes 5898244
  7.2 94.3 %all-gather.7.cloned.1.call-start = ((), (), s32[]{:S(2)}) async-start(), calls=%async_computation.4 | async-start | bytes 3686400 | tf_op jit(solution)/shard_map/all_gather | solution.py:666
  34.8 59.9 %all-to-all-start = ((bf16[4,160,640]{2,1,0:T(8,128)(2,1)}), bf16[4,160,640]{2,1,0:T(8,128)(2,1)S(1)}, u32[]{:S(2)}, u32[]{:S(2)}) async-start(bf16[4,160,640]{2,1,0:T(8,128)(2,1)} %get-tuple-element.66), calls=%async_computation | async-start | bytes 1638400 | tf_op jit(solution)/shard_map/all_to_all | solution.py:639
  40.1 183.3 %all-gather.13.cloned.1.call-start = ((), (), s32[]{:S(2)}) async-start(), calls=%async_computation.8 | async-start | bytes 3072000 | tf_op jit(solution)/shard_map/all_gather | solution.py:687
  40.9 279.8 %all-gather.9.cloned.1.call-start = ((), (), s32[]{:S(2)}) async-start(), calls=%async_computation.5 | async-start | bytes 2457600 | tf_op jit(solution)/shard_map/all_gather | solution.py:708
  41.0 24.5 %copy-start.3 = (bf16[384,640]{1,0:T(8,128)(2,1)}, bf16[384,640]{1,0:T(8,128)(2,1)S(1)}, u32[]{:S(2)}) copy-start(bf16[384,640]{1,0:T(8,128)(2,1)S(1)} %constant_dynamic-slice_fusion.refs_2_.refs_4_) | copy-start | bytes 1474564
  41.0 59.3 %collective-permute-start.5 = (bf16[384,640]{1,0:T(8,128)(2,1)S(1)}, bf16[384,640]{1,0:T(8,128)(2,1)S(1)}, u32[]{:S(2)}, u32[]{:S(2)}) collective-permute-start(bf16[384,640]{1,0:T(8,128)(2,1)S(1)} %constant_dynamic-slice_fusion.refs_2_.refs_4_), channel_id=1, source_target_pairs={{0,1},{1,0},{2,3},{3,2},{4,5},{5,4},{6,7},{7,6},{8,9},{9,8},{10,11... | collective-permute-start | bytes 1474568 | tf_op jit(solution)/shard_map/ppermute | solution.py:627
  41.1 58.9 %collective-permute-start.7 = (bf16[384,640]{1,0:T(8,128)(2,1)S(1)}, bf16[384,640]{1,0:T(8,128)(2,1)S(1)}, u32[]{:S(2)}, u32[]{:S(2)}) collective-permute-start(bf16[384,640]{1,0:T(8,128)(2,1)S(1)} %constant_dynamic-slice_fusion.refs_2_.refs_4_), channel_id=1, source_target_pairs={{0,2},{2,0},{1,3},{3,1},{4,6},{6,4},{5,7},{7,5},{8,10},{10,8},{9,1... | collective-permute-start | bytes 1474568 | tf_op jit(solution)/shard_map/ppermute | solution.py:627
  59.0 10.8 %collective-permute-start = (bf16[160,384]{1,0:T(8,128)(2,1)}, bf16[160,384]{1,0:T(8,128)(2,1)S(1)}, u32[]{:S(2)}, u32[]{:S(2)}) collective-permute-start(bf16[160,384]{1,0:T(8,128)(2,1)} %get-tuple-element.73), channel_id=1, source_target_pairs={{0,8},{8,0},{16,24},{24,16},{1,9},{9,1},{17,25},{25,17},{2,10},{10... | collective-permute-start | bytes 368648 | tf_op jit(solution)/shard_map/ppermute | solution.py:633
  61.2 33.5 %collective-permute-start.1 = (bf16[160,384]{1,0:T(8,128)(2,1)}, bf16[160,384]{1,0:T(8,128)(2,1)S(1)}, u32[]{:S(2)}, u32[]{:S(2)}) collective-permute-start(bf16[160,384]{1,0:T(8,128)(2,1)} %get-tuple-element.74), channel_id=1, source_target_pairs={{0,16},{8,24},{16,0},{24,8},{1,17},{9,25},{17,1},{25,9},{2,18},{10... | collective-permute-start | bytes 368648 | tf_op jit(solution)/shard_map/ppermute | solution.py:633
  63.5 31.2 %collective-permute-start.2 = (bf16[160,384]{1,0:T(8,128)(2,1)}, bf16[160,384]{1,0:T(8,128)(2,1)S(1)}, u32[]{:S(2)}, u32[]{:S(2)}) collective-permute-start(bf16[160,384]{1,0:T(8,128)(2,1)} %get-tuple-element.75), channel_id=1, source_target_pairs={{0,24},{8,16},{16,8},{24,0},{1,25},{9,17},{17,9},{25,1},{2,26},{10... | collective-permute-start | bytes 368648 | tf_op jit(solution)/shard_map/ppermute | solution.py:633
  69.9 24.9 %copy-start.21 = (bf16[160,384]{1,0:T(8,128)(2,1)}, bf16[160,384]{1,0:T(8,128)(2,1)S(1)}, u32[]{:S(2)}) copy-start(bf16[160,384]{1,0:T(8,128)(2,1)S(1)} %collective-permute-done.refs_1_) | copy-start | bytes 368644
  99.4 2.1 collective-permute-start.3
  99.4 15.1 %collective-permute-start.4 = (bf16[384,640]{1,0:T(8,128)(2,1)}, bf16[384,640]{1,0:T(8,128)(2,1)S(1)}, u32[]{:S(2)}, u32[]{:S(2)}) collective-permute-start(bf16[384,640]{1,0:T(8,128)(2,1)} %get-tuple-element.77.refs_0_), channel_id=1, source_target_pairs={{0,2},{2,0},{1,3},{3,1},{4,6},{6,4},{5,7},{7,5},{8,10},{10,8},{9,1... | collective-permute-start | bytes 1474568 | tf_op jit(solution)/shard_map/ppermute | solution.py:627
  100.0 14.8 %collective-permute-start.8 = (bf16[384,640]{1,0:T(8,128)(2,1)S(1)}, bf16[384,640]{1,0:T(8,128)(2,1)S(1)}, u32[]{:S(2)}, u32[]{:S(2)}) collective-permute-start(bf16[384,640]{1,0:T(8,128)(2,1)S(1)} %collective-permute-done.7.refs_2_.refs_6_), channel_id=1, source_target_pairs={{0,1},{1,0},{2,3},{3,2},{4,5},{5,4},{6,7},{7,6},{8,9},{9,8},{10,11... | collective-permute-start | bytes 1474568 | tf_op jit(solution)/shard_map/ppermute | solution.py:627
  114.6 1.9 collective-permute-start.6
  129.7 2.1 collective-permute-start.10
  129.9 4.0 %collective-permute-start.16 = (bf16[384,640]{1,0:T(8,128)(2,1)}, bf16[384,640]{1,0:T(8,128)(2,1)S(1)}, u32[]{:S(2)}, u32[]{:S(2)}) collective-permute-start(bf16[384,640]{1,0:T(8,128)(2,1)} %get-tuple-element.96), channel_id=1, source_target_pairs={{0,1},{1,0},{2,3},{3,2},{4,5},{5,4},{6,7},{7,6},{8,9},{9,8},{10,11... | collective-permute-start | bytes 1474568 | tf_op jit(solution)/shard_map/ppermute | solution.py:627
  130.2 32.4 %collective-permute-start.15 = (bf16[384,640]{1,0:T(8,128)(2,1)}, bf16[384,640]{1,0:T(8,128)(2,1)}, u32[]{:S(2)}, u32[]{:S(2)}) collective-permute-start(bf16[384,640]{1,0:T(8,128)(2,1)} %get-tuple-element.94), channel_id=1, source_target_pairs={{0,1},{1,0},{2,3},{3,2},{4,5},{5,4},{6,7},{7,6},{8,9},{9,8},{10,11... | collective-permute-start | bytes 1474568 | tf_op jit(solution)/shard_map/ppermute | solution.py:627
  130.4 18.9 %collective-permute-start.9 = (bf16[384,640]{1,0:T(8,128)(2,1)S(1)}, bf16[384,640]{1,0:T(8,128)(2,1)S(1)}, u32[]{:S(2)}, u32[]{:S(2)}) collective-permute-start(bf16[384,640]{1,0:T(8,128)(2,1)S(1)} %copy-done.24), channel_id=1, source_target_pairs={{0,1},{1,0},{2,3},{3,2},{4,5},{5,4},{6,7},{7,6},{8,9},{9,8},{10,11... | collective-permute-start | bytes 1474568 | tf_op jit(solution)/shard_map/ppermute | solution.py:627
  132.9 16.4 %collective-permute-start.11 = (bf16[384,640]{1,0:T(8,128)(2,1)S(1)}, bf16[384,640]{1,0:T(8,128)(2,1)S(1)}, u32[]{:S(2)}, u32[]{:S(2)}) collective-permute-start(bf16[384,640]{1,0:T(8,128)(2,1)S(1)} %add_convert_fusion.3), channel_id=1, source_target_pairs={{0,2},{2,0},{1,3},{3,1},{4,6},{6,4},{5,7},{7,5},{8,10},{10,8},{9,1... | collective-permute-start | bytes 1474568 | tf_op jit(solution)/shard_map/ppermute | solution.py:627
  135.8 26.8 %collective-permute-start.17 = (bf16[384,640]{1,0:T(8,128)(2,1)}, bf16[384,640]{1,0:T(8,128)(2,1)}, u32[]{:S(2)}, u32[]{:S(2)}) collective-permute-start(bf16[384,640]{1,0:T(8,128)(2,1)} %add_convert_fusion.2), channel_id=1, source_target_pairs={{0,2},{2,0},{1,3},{3,1},{4,6},{6,4},{5,7},{7,5},{8,10},{10,8},{9,1... | collective-permute-start | bytes 1474568 | tf_op jit(solution)/shard_map/ppermute | solution.py:627
  155.8 9.1 %collective-permute-start.12 = (bf16[160,384]{1,0:T(8,128)(2,1)}, bf16[160,384]{1,0:T(8,128)(2,1)S(1)}, u32[]{:S(2)}, u32[]{:S(2)}) collective-permute-start(bf16[160,384]{1,0:T(8,128)(2,1)} %get-tuple-element.91), channel_id=1, source_target_pairs={{0,8},{8,0},{16,24},{24,16},{1,9},{9,1},{17,25},{25,17},{2,10},{10... | collective-permute-start | bytes 368648 | tf_op jit(solution)/shard_map/ppermute | solution.py:633
  160.2 11.6 %collective-permute-start.13 = (bf16[160,384]{1,0:T(8,128)(2,1)}, bf16[160,384]{1,0:T(8,128)(2,1)S(1)}, u32[]{:S(2)}, u32[]{:S(2)}) collective-permute-start(bf16[160,384]{1,0:T(8,128)(2,1)} %get-tuple-element.92), channel_id=1, source_target_pairs={{0,16},{8,24},{16,0},{24,8},{1,17},{9,25},{17,1},{25,9},{2,18},{10... | collective-permute-start | bytes 368648 | tf_op jit(solution)/shard_map/ppermute | solution.py:633
  160.2 11.6 %collective-permute-start.14 = (bf16[160,384]{1,0:T(8,128)(2,1)}, bf16[160,384]{1,0:T(8,128)(2,1)}, u32[]{:S(2)}, u32[]{:S(2)}) collective-permute-start(bf16[160,384]{1,0:T(8,128)(2,1)} %get-tuple-element.93), channel_id=1, source_target_pairs={{0,24},{8,16},{16,8},{24,0},{1,25},{9,17},{17,9},{25,1},{2,26},{10... | collective-permute-start | bytes 368648 | tf_op jit(solution)/shard_map/ppermute | solution.py:633
  171.8 151.8 %reduce-scatter.2.cloned.1.call-start = ((), (), s32[]{:S(2)}) async-start(), calls=%async_computation.7 | async-start | bytes 2048000 | tf_op jit(solution)/shard_map/reduce_scatter | solution.py:719
  173.3 36.5 %collective-permute-start.18 = (bf16[640,1280]{1,0:T(8,128)(2,1)}, bf16[640,1280]{1,0:T(8,128)(2,1)S(1)}, u32[]{:S(2)}, u32[]{:S(2)}) collective-permute-start(bf16[640,1280]{1,0:T(8,128)(2,1)} %get-tuple-element.149), channel_id=1, source_target_pairs={{0,4},{4,0},{1,5},{5,1},{2,6},{6,2},{3,7},{7,3},{8,12},{12,8},{9,1... | collective-permute-start | bytes 4915208 | tf_op jit(solution)/shard_map/ppermute | solution.py:627
  211.4 114.2 %all-gather.11.cloned.1.call-start = ((), (), s32[]{:S(2)}) async-start(), calls=%async_computation.6 | async-start | bytes 2457600 | tf_op jit(solution)/shard_map/all_gather | solution.py:724
  211.7 17.7 %collective-permute-start.19 = (bf16[480,384]{1,0:T(8,128)(2,1)S(1)}, bf16[480,384]{1,0:T(8,128)(2,1)S(1)}, u32[]{:S(2)}, u32[]{:S(2)}) collective-permute-start(bf16[480,384]{1,0:T(8,128)(2,1)S(1)} %copy-done.27), channel_id=1, source_target_pairs={{0,8},{8,0},{16,24},{24,16},{1,9},{9,1},{17,25},{25,17},{2,10},{10... | collective-permute-start | bytes 1105928 | tf_op jit(solution)/shard_map/ppermute | solution.py:633
  215.1 38.1 %collective-permute-start.20 = (bf16[480,384]{1,0:T(8,128)(2,1)S(1)}, bf16[480,384]{1,0:T(8,128)(2,1)S(1)}, u32[]{:S(2)}, u32[]{:S(2)}) collective-permute-start(bf16[480,384]{1,0:T(8,128)(2,1)S(1)} %copy-done.26), channel_id=1, source_target_pairs={{0,16},{8,24},{16,0},{24,8},{1,17},{9,25},{17,1},{25,9},{2,18},{10... | collective-permute-start | bytes 1105928 | tf_op jit(solution)/shard_map/ppermute | solution.py:633
  215.1 38.1 %collective-permute-start.21 = (bf16[480,384]{1,0:T(8,128)(2,1)S(1)}, bf16[480,384]{1,0:T(8,128)(2,1)S(1)}, u32[]{:S(2)}, u32[]{:S(2)}) collective-permute-start(bf16[480,384]{1,0:T(8,128)(2,1)S(1)} %copy-done.25), channel_id=1, source_target_pairs={{0,24},{8,16},{16,8},{24,0},{1,25},{9,17},{17,9},{25,1},{2,26},{10... | collective-permute-start | bytes 1105928 | tf_op jit(solution)/shard_map/ppermute | solution.py:633
  286.0 32.6 %all-to-all-start.2 = ((bf16[4,80,164]{2,1,0:T(8,128)(2,1)}), bf16[4,80,164]{2,1,0:T(8,128)(2,1)S(1)}, u32[]{:S(2)}, u32[]{:S(2)}) async-start(bf16[4,80,164]{2,1,0:T(8,128)(2,1)} %pad_maximum_fusion.2), calls=%async_computation.2 | async-start | bytes 327680 | tf_op jit(solution)/shard_map/all_to_all | solution.py:639
  (25 other events, 140.4 us)
Sparse Core Ops, SparseCore 0:
  10.7 87.6 all-gather.6
  100.0 51.1 all-gather.12
  171.9 43.9 all-gather.8
  218.6 54.7 reduce-scatter.1
  274.9 50.1 all-gather.10

commit v4 on v3

--- a/solution.py
+++ b/solution.py
@@ -52,16 +52,19 @@
     lens, x_ref, gain_ref, shift_ref, w_ref,
     q_ref, k_ref, qt_ref, kt_ref, vt_ref, seg_ref, bounds_ref, full_ref, out_ref,
 ):
-    across, kinds, _, narrow = w_ref.shape
+    across = w_ref.shape[0]
+    kinds = full_ref.shape[0] + 1
+    narrow = w_ref.shape[2] // kinds
 
     @pl.when(pl.program_id(0) == 0)
     def _():
         for part in range(across):
             spot = slice(part * narrow, (part + 1) * narrow)
             for item in range(kinds - 1):
-                full_ref[item, :, spot] = w_ref[part, item]
+                full_ref[item, :, spot] = w_ref[part, :, item * narrow : (item + 1) * narrow]
+            last = w_ref[part, :, (kinds - 1) * narrow :]
             for copy in range(out_ref.shape[0]):
-                out_ref[copy, :, spot] = w_ref[part, kinds - 1]
+                out_ref[copy, :, spot] = last
 
     size = x_ref.shape[0]
     first = pl.program_id(0) * size
@@ -100,7 +103,7 @@
 
 def project(lens, tokens, gains, shifts, weights, depth):
     count, dim = tokens.shape
-    width = weights.shape[2]
+    width = weights.shape[1]
     blocks = count // BQ
     size = count // STEPS
     heads = width // HD
@@ -115,7 +118,7 @@
             pl.BlockSpec((size, dim), lambda i: (i, 0)),
             fixed2,
             fixed2,
-            pl.BlockSpec(weights.shape, lambda i: (0, 0, 0, 0)),
+            pl.BlockSpec(weights.shape, lambda i: (0, 0, 0)),
         ],
         out_specs=[
             per_head,
@@ -368,18 +371,15 @@
     )(layer, *ot, w_out, rows, gains, shifts)
 
 
-ROWS = 256
-
-
 def ffn_kernel(*refs):
     xn_parts, dy_parts, w_ref = refs[:2], refs[2:4], refs[4]
-    y_out, dx_out, y_far, dx_far, g_ref, du_ref = refs[5:11]
+    outs, (g_ref, du_ref) = refs[5:9], refs[9:11]
     y_ref, dx_ref, xn_ref, dy_ref = refs[11:]
-    item = pl.program_id(0)
-    mine = xn_parts[0].shape[0]
-    count, hidden = g_ref.shape
-
-    @pl.when(item == 0)
+    item, side = pl.program_id(0), pl.program_id(1)
+    mine, hidden = g_ref.shape
+    spot = pl.ds(pl.multiple_of(side * mine, mine), mine)
+
+    @pl.when((item == 0) & (side == 0))
     def _():
         for part in range(2):
             xn_ref[part * mine : (part + 1) * mine, :] = xn_parts[part][...]
@@ -389,25 +389,23 @@
 
     w_in = w_ref.at[:, :hidden]
     w_down = w_ref.at[:, hidden:]
-    for first in range(0, count, ROWS):
-        rows = slice(first, first + ROWS)
-        u = dot(xn_ref[rows, :], w_in[...])
-        dg = dot(dy_ref[rows, :], w_down[...])
-        half = 0.5 + 0.5 * lax.erf(u * 0.7071067811865476)
-        slope = half + u * (jnp.exp2(u * u * (-0.5 * LOG2E)) * 0.3989422804014327)
-        g = (u * half).astype(BF16)
-        du = (dg * slope).astype(BF16)
-        g_ref[rows, :] = g
-        du_ref[rows, :] = du
-        y_ref[rows, :] += dot_nt(g, w_down[...])
-        dx_ref[rows, :] += dot_nt(du, w_in[...])
-
-    @pl.when(item == pl.num_programs(0) - 1)
+    u = dot(xn_ref[spot, :], w_in[...])
+    dg = dot(dy_ref[spot, :], w_down[...])
+    half = 0.5 + 0.5 * lax.erf(u * 0.7071067811865476)
+    slope = half + u * (jnp.exp2(u * u * (-0.5 * LOG2E)) * 0.3989422804014327)
+    g = (u * half).astype(BF16)
+    du = (dg * slope).astype(BF16)
+    g_ref[...] = g
+    du_ref[...] = du
+    y_ref[spot, :] += dot_nt(g, w_down[...])
+    dx_ref[spot, :] += dot_nt(du, w_in[...])
+
+    @pl.when((item == pl.num_programs(0) - 1) & (side == 1))
     def _():
-        y_out[...] = y_ref[:mine, :].astype(BF16)
-        dx_out[...] = dx_ref[:mine, :].astype(BF16)
-        y_far[...] = y_ref[mine:, :].astype(BF16)
-        dx_far[...] = dx_ref[mine:, :].astype(BF16)
+        outs[0][...] = y_ref[:mine, :].astype(BF16)
+        outs[1][...] = dx_ref[:mine, :].astype(BF16)
+        outs[2][...] = y_ref[mine:, :].astype(BF16)
+        outs[3][...] = dx_ref[mine:, :].astype(BF16)
 
 
 def ffn(xn, dy, weights):
@@ -415,12 +413,12 @@
     count = 2 * mine
     blocks = weights.shape[0] // dim
     hidden = weights.shape[1] // 2
-    whole = pl.BlockSpec((mine, dim), lambda i: (0, 0))
-    act = pl.BlockSpec((count, hidden), lambda i: (0, i))
+    whole = pl.BlockSpec((mine, dim), lambda i, j: (0, 0))
+    act = pl.BlockSpec((mine, hidden), lambda i, j: (j, i))
     return pl.pallas_call(
         ffn_kernel,
-        grid=(blocks,),
-        in_specs=[whole] * 4 + [pl.BlockSpec((dim, 2 * hidden), lambda i: (i, 0))],
+        grid=(blocks, 2),
+        in_specs=[whole] * 4 + [pl.BlockSpec((dim, 2 * hidden), lambda i, j: (i, 0))],
         out_specs=[whole] * 4 + [act] * 2,
         out_shape=[jax.ShapeDtypeStruct((mine, dim), BF16)] * 4
         + [jax.ShapeDtypeStruct((count, blocks * hidden), BF16)] * 2,
@@ -661,7 +659,9 @@
     layers = layer.astype(jnp.int32).reshape(1)
 
     pieces = lax.all_gather(
-        jnp.concatenate([jnp.swapaxes(w_qkv, 1, 2), w_attn_out[None]], axis=0), WIDE, axis=0
+        jnp.concatenate([w_qkv.transpose(2, 0, 1).reshape(width, -1), w_attn_out], axis=1),
+        WIDE,
+        axis=0,
     )
     weights = lax.all_gather(
         jnp.concatenate([w_ffn_in, w_ffn_down], axis=1), ("far", "narrow"), axis=0, tiled=True

time: 336 us -> 334 us (level)
  Pallas kernels: 116 us -> 127 us
  waiting for transfers between devices: 88.5 us -> 77.6 us
  blocking collectives: 39.3 us -> 35.7 us
    pallas_call x1, Pallas kernels: 28.1 us -> 35.3 us  [attend_back(): pl.pallas_call(partial(attend_back_kernel, first, heads, parts), in_specs...]
    ppermute x13, waiting for transfers between devices: 10.7 us -> 3.97 us  [swap(): return lax.ppermute(value, axis, [(0, 1), (1, 0)])]
    pallas_call x1, Pallas kernels: 17.3 us -> 22.5 us  [attend(): pl.pallas_call(partial(attend_kernel, first, heads, parts), in_specs=[pl....]
    ppermute x9, waiting for transfers between devices: 65.8 us -> 61.9 us  [spread(): lax.ppermute(parts[bit], 'narrow', [(i, i ^ bit) for i in range(size)])]
    unnamed x62 -> x61, local copies, waits for them, and re-layouts: 11.5 us -> 10.4 us
  transfers between devices with their start and end apart: 29 -> 29, of which waited for: 11 -> 10; matrix products, arithmetic and copies ran while one was open for 5% -> 6% of each run, Pallas kernels for 34% -> 38%
where the time goes in v4:
time: 334 us; the launch traced here: 333 us
  Pallas kernels  127 us (38%)
  waiting for transfers between devices  77.6 us (23%)
  starting transfers between devices  50.7 us (15%)
  blocking collectives  35.7 us (11%)
  local copies, waits for them, and re-layouts  17.3 us (5%)
  between operations  14.1 us (4%)
  other arithmetic  10.7 us (3%)
    ppermute x9, waiting for transfers between devices, spread(): lax.ppermute(parts[bit], 'narrow', [(i, i ^ bit) for i in range(size)])  61.9 us
    pallas_call x1, Pallas kernels, attend_back(): pl.pallas_call(partial(attend_back_kernel, first, heads, parts), in_specs...  35.3 us
    pallas_call x2, Pallas kernels, ffn(): pl.pallas_call(ffn_kernel, grid=(blocks, 2), in_specs=[whole] * 4 + [pl.B...  24.7 us
    all_to_all x2, starting transfers between devices, exchange(): return lax.all_to_all(value, axis, 0, 0, tiled=True)  24.3 us
    pallas_call x1, Pallas kernels, attend(): pl.pallas_call(partial(attend_kernel, first, heads, parts), in_specs=[pl....  22.5 us
    all_to_all x1, blocking collectives, exchange(): return lax.all_to_all(value, axis, 0, 0, tiled=True)  22.3 us
    ppermute x9, starting transfers between devices, spread(): lax.ppermute(parts[bit], 'narrow', [(i, i ^ bit) for i in range(size)])  18.3 us
    all_gather x1, blocking collectives, local(): lax.all_gather(jnp.concatenate([w_qkv.transpose(2, 0, 1).reshape(width, -...  13.3 us
  transfers between devices with their start and end apart: 29, of which 10 were waited for; matrix products, arithmetic and copies ran while one was open for 6% of the time, Pallas kernels for 38%

profile of v4, /device:TPU:0, one launch (start us, length us, event | category | flops | bytes accessed | tf_op | source)
XLA Modules:
  0.0 333.4 jit_solution(10180876780901255692)
XLA Ops:
  7.2 1.9 pad_maximum_fusion
  11.1 13.3 %all-gather = bf16[1280,320]{1,0:T(8,128)(2,1)} all-gather(bf16[160,320]{1,0:T(8,128)(2,1)S(1)} %pad_maximum_fusion.2), channel_id=2, replica_groups=mesh['narrow'=4,'far'=2,'near'=2,'core'=2] {'far','near','core'}, dimensions={0}, use_global_device_ids=true | all-gather | bytes 921600 | tf_op jit(solution)/shard_map/all_gather | solution.py:661
  24.4 8.7 %project.1 = (bf16[5,1536,32]{2,1,0:T(8,128)(2,1)}, bf16[5,1536,32]{2,1,0:T(8,128)(2,1)}, bf16[160,1536]{1,0:T(8,128)(2,1)}, bf16[160,1536]{1,0:T(8,128)(2,1)}, ...) custom-call(s32[1,16]{1,0:T(1,128)} %lens.1, ...), custom_call_target="tpu_custom_call" | custom-call | flops 1000000 | bytes 100000 | tf_op jit(solution)/shard_map/project/pallas_call | solution.py:113
  33.1 4.9 %all-to-all-start = ((bf16[4,160,640]{2,1,0:T(8,128)(2,1)}), bf16[4,160,640]{2,1,0:T(8,128)(2,1)S(1)}, u32[]{:S(2)}, u32[]{:S(2)}) async-start(bf16[4,160,640]{2,1,0:T(8,128)(2,1)} %get-tuple-element.66), calls=%async_computation | async-start | bytes 1638400 | tf_op jit(solution)/shard_map/all_to_all | solution.py:637
  40.6 22.5 %attend_0.1 = (bf16[160,384]{1,0:T(8,128)(2,1)}, bf16[160,384]{1,0:T(8,128)(2,1)}, bf16[160,384]{1,0:T(8,128)(2,1)}, bf16[160,384]{1,0:T(8,128)(2,1)}, bf16[160,1536]{1,0:T(8,128)(2,1)}, /*index=5*/f32[8,1536]{1,0:T(8,128)}) custom-call(s32[1]{0:T(128)} %bitcast.layer, s32[6,2]{1,0:T(8,128)} %get-tuple-element.67.bounds, ...), custom_call_target="tpu_custom_call" | custom-call | flops 1000000 | bytes 100000 | tf_op jit(solution)/shard_map/attend_0/pallas_call | solution.py:221
  63.2 2.0 collective-permute-start
  65.2 2.4 collective-permute-start.1
  69.5 3.1 collective-permute-done.refs_1_
  72.6 19.0 %collective-permute-done.1.refs_2_ = bf16[160,384]{1,0:T(8,128)(2,1)S(1)} collective-permute-done((bf16[160,384]{1,0:T(8,128)(2,1)}, bf16[160,384]{1,0:T(8,128)(2,1)S(1)}, u32[]{:S(2)}, u32[]{:S(2)}) %collective-permute-start.1) | collective-permute-done | bytes 122912 | tf_op jit(solution)/shard_map/ppermute | solution.py:631
  92.5 3.7 %mix.1 = (f32[384,640]{1,0:T(8,128)}, bf16[384,640]{1,0:T(8,128)(2,1)}, bf16[4,160,384]{2,1,0:T(8,128)(2,1)}) custom-call(s32[1]{0:T(128)} %bitcast.layer, bf16[160,384]{1,0:T(8,128)(2,1)} %get-tuple-element.72.refs_0_, bf16[160,384]{1,0:T(8,128)(2,1)} %copy-done.21, bf16[160,384]{1,0:T(8,128)(2,1)} %copy-done.22, bf16[160,384]{1,0:T(8,128)(2,1)} %copy-done.23, ...), custom_call_target="tpu_custom_call" | custom-call | flops 1000000 | bytes 100000 | tf_op jit(solution)/shard_map/mix/pallas_call | solution.py:359
  99.1 12.4 %ffn.2 = (bf16[384,640]{1,0:T(8,128)(2,1)}, bf16[384,640]{1,0:T(8,128)(2,1)}, bf16[384,640]{1,0:T(8,128)(2,1)}, bf16[384,640]{1,0:T(8,128)(2,1)}, bf16[768,1280]{1,0:T(8,128)(2,1)}, /*index=5*/bf16[768,1280]{1,0:T(8,128)(2,1)}) custom-call(bf16[384,640]{1,0:T(8,128)(2,1)} %get-tuple-element.77.refs_0_, bf16[384,640]{1,0:T(8,128)(2,1)} %copy-done.9, ...), custom_call_target="tpu_custom_call" | custom-call | flops 1000000 | bytes 100000 | tf_op jit(solution)/shard_map/ffn/pallas_call | solution.py:418
  114.3 12.3 %ffn.3 = (bf16[384,640]{1,0:T(8,128)(2,1)}, bf16[384,640]{1,0:T(8,128)(2,1)}, bf16[384,640]{1,0:T(8,128)(2,1)}, bf16[384,640]{1,0:T(8,128)(2,1)}, bf16[768,1280]{1,0:T(8,128)(2,1)}, /*index=5*/bf16[768,1280]{1,0:T(8,128)(2,1)}) custom-call(bf16[384,640]{1,0:T(8,128)(2,1)} %copy-done.10, bf16[384,640]{1,0:T(8,128)(2,1)} %copy-done.12, ...), custom_call_target="tpu_custom_call" | custom-call | flops 1000000 | bytes 100000 | tf_op jit(solution)/shard_map/ffn/pallas_call | solution.py:418
  131.3 1.9 add_convert_fusion.2
  134.1 12.3 %outer.1 = bf16[2,640,1280]{2,1,0:T(8,128)(2,1)} custom-call(s32[1]{0:T(128)} %bitcast.4._, bf16[384,640]{1,0:T(8,128)(2,1)} %get-tuple-element.77.refs_0_, bf16[384,640]{1,0:T(8,128)(2,1)} %copy-done.9, bf16[384,640]{1,0:T(8,128)(2,1)} %copy-done.10, bf16[384,640]{1,0:T(8,128)(2,1)} %copy-done.12, bf16[384,640]{1,0:T(8,128)(2,1)} %copy-done.3, ...), custom_call_target="tpu_custom_call" | custom-call | flops 1000000 | bytes 100000 | tf_op jit(solution)/shard_map/outer/pallas_call | solution.py:461
  147.5 5.5 %turn.1 = (f32[384,640]{1,0:T(8,128)}, bf16[640,640]{1,0:T(8,128)(2,1)}, f32[8,640]{1,0:T(8,128)}, bf16[160,384]{1,0:T(8,128)(2,1)}, bf16[160,384]{1,0:T(8,128)(...) custom-call(s32[1]{0:T(128)} %bitcast.layer, bf16[4,160,640]{2,1,0:T(8,128)(2,1)} %copy-done.4, ...), custom_call_target="tpu_custom_call" | custom-call | flops 1000000 | bytes 100000 | tf_op jit(solution)/shard_map/turn/pallas_call | solution.py:505
  153.0 5.6 %collective-permute-start.12 = (bf16[160,384]{1,0:T(8,128)(2,1)}, bf16[160,384]{1,0:T(8,128)(2,1)S(1)}, u32[]{:S(2)}, u32[]{:S(2)}) collective-permute-start(bf16[160,384]{1,0:T(8,128)(2,1)} %get-tuple-element.91), channel_id=1, source_target_pairs={{0,8},{8,0},{16,24},{24,16},{1,9},{9,1},{17,25},{25,17},{2,10},{10... | collective-permute-start | bytes 368648 | tf_op jit(solution)/shard_map/ppermute | solution.py:631
  158.6 2.4 collective-permute-start.14
  161.0 2.2 add_convert_fusion.1
  163.2 6.9 %collective-permute-done.13.refs_2_ = bf16[160,384]{1,0:T(8,128)(2,1)S(1)} collective-permute-done((bf16[160,384]{1,0:T(8,128)(2,1)}, bf16[160,384]{1,0:T(8,128)(2,1)S(1)}, u32[]{:S(2)}, u32[]{:S(2)}) %collective-permute-start.13) | collective-permute-done | bytes 122912 | tf_op jit(solution)/shard_map/ppermute | solution.py:631
  172.6 35.3 %attend_back_0.1 = (bf16[480,384]{1,0:T(8,128)(2,1)}, bf16[480,384]{1,0:T(8,128)(2,1)}, bf16[480,384]{1,0:T(8,128)(2,1)}, bf16[480,384]{1,0:T(8,128)(2,1)}, bf16[480,1536]{1,0:T(8,128)(2,1)}) custom-call(s32[1]{0:T(128)} %bitcast.layer, s32[6,2]{1,0:T(8,128)} %get-tuple-element.67.bounds, f32[8,1536]{1,0:T(8,128)} %get-tuple-element.68.segr_ref, ...), custom_call_target="tpu_custom_call" | custom-call | flops 1000000 | bytes 100000 | tf_op jit(solution)/shard_map/attend_back_0/pallas_call | solution.py:320
  210.3 3.4 %collective-permute-start.19 = (bf16[480,384]{1,0:T(8,128)(2,1)S(1)}, bf16[480,384]{1,0:T(8,128)(2,1)S(1)}, u32[]{:S(2)}, u32[]{:S(2)}) collective-permute-start(bf16[480,384]{1,0:T(8,128)(2,1)S(1)} %copy-done.27), channel_id=1, source_target_pairs={{0,8},{8,0},{16,24},{24,16},{1,9},{9,1},{17,25},{25,17},{2,10},{10... | collective-permute-start | bytes 1105928 | tf_op jit(solution)/shard_map/ppermute | solution.py:631
  213.7 2.4 collective-permute-start.21
  216.1 5.9 %small.1 = bf16[640,1152]{1,0:T(8,128)(2,1)} custom-call(bf16[480,1536]{1,0:T(8,128)(2,1)} %get-tuple-element.106.flat_ref, bf16[1536,640]{1,0:T(8,128)(2,1)} %x_ref.3, bf16[3,160,640]{2,1,0:T(8,128)(2,1)} %get-tuple-element.107.w_ref, bf16[2,640]{1,0:T(2,128)(2,1)} %refs_7_.3, bf16[2,640]{1,0:T(2,128)(2,1)} %shift_ref.3, ...), custom_call_target="tpu_custom_call" | custom-call | flops 1000000 | bytes 100000 | tf_op jit(solution)/shard_map/small/pallas_call | solution.py:574
  222.0 15.2 %collective-permute-done.19.refs_1_ = bf16[480,384]{1,0:T(8,128)(2,1)S(1)} collective-permute-done((bf16[480,384]{1,0:T(8,128)(2,1)S(1)}, bf16[480,384]{1,0:T(8,128)(2,1)S(1)}, u32[]{:S(2)}, u32[]{:S(2)}) %collective-permute-start.19) | collective-permute-done | bytes 368672 | tf_op jit(solution)/shard_map/ppermute | solution.py:631
  237.2 17.8 %collective-permute-done.20.refs_2_ = bf16[480,384]{1,0:T(8,128)(2,1)S(1)} collective-permute-done((bf16[480,384]{1,0:T(8,128)(2,1)S(1)}, bf16[480,384]{1,0:T(8,128)(2,1)S(1)}, u32[]{:S(2)}, u32[]{:S(2)}) %collective-permute-start.20) | collective-permute-done | bytes 368672 | tf_op jit(solution)/shard_map/ppermute | solution.py:631
  255.9 5.8 %finish.1 = bf16[384,640]{1,0:T(8,128)(2,1)} custom-call(s32[1]{0:T(128)} %bitcast.layer, bf16[480,384]{1,0:T(8,128)(2,1)} %get-tuple-element.114.refs_0_, bf16[480,384]{1,0:T(8,128)(2,1)} %copy-done.16, bf16[480,384]{1,0:T(8,128)(2,1)} %copy-done.17, bf16[480,384]{1,0:T(8,128)(2,1)} %copy-done.18, bf16[4,3,160,640]{3,2,1,0:T(8,128)(2,1)} %bitcast.22, ...), custom_call_target="tpu_custom_call" | custom-call | flops 1000000 | bytes 100000 | tf_op jit(solution)/shard_map/finish/pallas_call | solution.py:538
  261.7 22.3 %all_to_all.15 = bf16[8,80,1152]{2,1,0:T(8,128)(2,1)S(1)} all-to-all(bf16[8,80,1152]{2,1,0:T(8,128)(2,1)S(1)} %bitcast.20), channel_id=1, replica_groups=mesh['narrow'=4,'far'=2,'near'=2,'core'=2] {'far','near','core'}, dimensions={0} | all-to-all | bytes 2949120 | tf_op jit(solution)/shard_map/all_to_all | solution.py:637
  285.4 19.4 %all-to-all-start.2 = ((bf16[4,80,164]{2,1,0:T(8,128)(2,1)}), bf16[4,80,164]{2,1,0:T(8,128)(2,1)S(1)}, u32[]{:S(2)}, u32[]{:S(2)}) async-start(bf16[4,80,164]{2,1,0:T(8,128)(2,1)} %pad_maximum_fusion.1), calls=%async_computation.2 | async-start | bytes 327680 | tf_op jit(solution)/shard_map/all_to_all | solution.py:637
  305.8 10.9 %all-to-all-done.2 = bf16[4,80,164]{2,1,0:T(8,128)(2,1)S(1)} async-done(((bf16[4,80,164]{2,1,0:T(8,128)(2,1)}), bf16[4,80,164]{2,1,0:T(8,128)(2,1)S(1)}, u32[]{:S(2)}, u32[]{:S(2)}) %all-to-all-start.2) | async-done | bytes 104992 | tf_op jit(solution)/shard_map/all_to_all | solution.py:637
  318.8 3.0 keep.1
  321.8 2.0 fusion
  323.7 3.1 copy.34
  (128 shorter events, 29.7 us)
Async XLA Ops:
  7.2 31.8 %copy-start = (bf16[1536,640]{1,0:T(8,128)(2,1)S(1)}, bf16[1536,640]{1,0:T(8,128)(2,1)}, u32[]{:S(2)}) copy-start(bf16[1536,640]{1,0:T(8,128)(2,1)} %param.10) | copy-start | bytes 5898244
  7.2 91.2 %all-gather.7.cloned.1.call-start = ((), (), s32[]{:S(2)}) async-start(), calls=%async_computation.4 | async-start | bytes 3686400 | tf_op jit(solution)/shard_map/all_gather | solution.py:666
  33.1 58.4 %all-to-all-start = ((bf16[4,160,640]{2,1,0:T(8,128)(2,1)}), bf16[4,160,640]{2,1,0:T(8,128)(2,1)S(1)}, u32[]{:S(2)}, u32[]{:S(2)}) async-start(bf16[4,160,640]{2,1,0:T(8,128)(2,1)} %get-tuple-element.66), calls=%async_computation | async-start | bytes 1638400 | tf_op jit(solution)/shard_map/all_to_all | solution.py:637
  38.0 184.0 %all-gather.13.cloned.1.call-start = ((), (), s32[]{:S(2)}) async-start(), calls=%async_computation.8 | async-start | bytes 3072000 | tf_op jit(solution)/shard_map/all_gather | solution.py:687
  38.8 280.0 %all-gather.9.cloned.1.call-start = ((), (), s32[]{:S(2)}) async-start(), calls=%async_computation.5 | async-start | bytes 2457600 | tf_op jit(solution)/shard_map/all_gather | solution.py:708
  39.1 30.4 %copy-start.3 = (bf16[384,640]{1,0:T(8,128)(2,1)}, bf16[384,640]{1,0:T(8,128)(2,1)S(1)}, u32[]{:S(2)}) copy-start(bf16[384,640]{1,0:T(8,128)(2,1)S(1)} %constant_dynamic-slice_fusion.refs_2_.refs_4_) | copy-start | bytes 1474564
  39.1 58.8 %collective-permute-start.5 = (bf16[384,640]{1,0:T(8,128)(2,1)S(1)}, bf16[384,640]{1,0:T(8,128)(2,1)S(1)}, u32[]{:S(2)}, u32[]{:S(2)}) collective-permute-start(bf16[384,640]{1,0:T(8,128)(2,1)S(1)} %constant_dynamic-slice_fusion.refs_2_.refs_4_), channel_id=1, source_target_pairs={{0,1},{1,0},{2,3},{3,2},{4,5},{5,4},{6,7},{7,6},{8,9},{9,8},{10,11... | collective-permute-start | bytes 1474568 | tf_op jit(solution)/shard_map/ppermute | solution.py:625
  39.2 58.5 %collective-permute-start.7 = (bf16[384,640]{1,0:T(8,128)(2,1)S(1)}, bf16[384,640]{1,0:T(8,128)(2,1)S(1)}, u32[]{:S(2)}, u32[]{:S(2)}) collective-permute-start(bf16[384,640]{1,0:T(8,128)(2,1)S(1)} %constant_dynamic-slice_fusion.refs_2_.refs_4_), channel_id=1, source_target_pairs={{0,2},{2,0},{1,3},{3,1},{4,6},{6,4},{5,7},{7,5},{8,10},{10,8},{9,1... | collective-permute-start | bytes 1474568 | tf_op jit(solution)/shard_map/ppermute | solution.py:625
  63.2 9.4 %collective-permute-start = (bf16[160,384]{1,0:T(8,128)(2,1)}, bf16[160,384]{1,0:T(8,128)(2,1)S(1)}, u32[]{:S(2)}, u32[]{:S(2)}) collective-permute-start(bf16[160,384]{1,0:T(8,128)(2,1)} %get-tuple-element.73), channel_id=1, source_target_pairs={{0,8},{8,0},{16,24},{24,16},{1,9},{9,1},{17,25},{25,17},{2,10},{10... | collective-permute-start | bytes 368648 | tf_op jit(solution)/shard_map/ppermute | solution.py:631
  65.2 26.3 %collective-permute-start.1 = (bf16[160,384]{1,0:T(8,128)(2,1)}, bf16[160,384]{1,0:T(8,128)(2,1)S(1)}, u32[]{:S(2)}, u32[]{:S(2)}) collective-permute-start(bf16[160,384]{1,0:T(8,128)(2,1)} %get-tuple-element.74), channel_id=1, source_target_pairs={{0,16},{8,24},{16,0},{24,8},{1,17},{9,25},{17,1},{25,9},{2,18},{10... | collective-permute-start | bytes 368648 | tf_op jit(solution)/shard_map/ppermute | solution.py:631
  67.6 24.0 %collective-permute-start.2 = (bf16[160,384]{1,0:T(8,128)(2,1)}, bf16[160,384]{1,0:T(8,128)(2,1)S(1)}, u32[]{:S(2)}, u32[]{:S(2)}) collective-permute-start(bf16[160,384]{1,0:T(8,128)(2,1)} %get-tuple-element.75), channel_id=1, source_target_pairs={{0,24},{8,16},{16,8},{24,0},{1,25},{9,17},{17,9},{25,1},{2,26},{10... | collective-permute-start | bytes 368648 | tf_op jit(solution)/shard_map/ppermute | solution.py:631
  72.6 19.0 %copy-start.21 = (bf16[160,384]{1,0:T(8,128)(2,1)}, bf16[160,384]{1,0:T(8,128)(2,1)S(1)}, u32[]{:S(2)}) copy-start(bf16[160,384]{1,0:T(8,128)(2,1)S(1)} %collective-permute-done.refs_1_) | copy-start | bytes 368644
  96.3 2.1 collective-permute-start.3
  96.3 15.3 %collective-permute-start.4 = (bf16[384,640]{1,0:T(8,128)(2,1)}, bf16[384,640]{1,0:T(8,128)(2,1)S(1)}, u32[]{:S(2)}, u32[]{:S(2)}) collective-permute-start(bf16[384,640]{1,0:T(8,128)(2,1)} %get-tuple-element.77.refs_0_), channel_id=1, source_target_pairs={{0,2},{2,0},{1,3},{3,1},{4,6},{6,4},{5,7},{7,5},{8,10},{10,8},{9,1... | collective-permute-start | bytes 1474568 | tf_op jit(solution)/shard_map/ppermute | solution.py:625
  97.7 14.1 %collective-permute-start.8 = (bf16[384,640]{1,0:T(8,128)(2,1)S(1)}, bf16[384,640]{1,0:T(8,128)(2,1)S(1)}, u32[]{:S(2)}, u32[]{:S(2)}) collective-permute-start(bf16[384,640]{1,0:T(8,128)(2,1)S(1)} %collective-permute-done.7.refs_2_.refs_6_), channel_id=1, source_target_pairs={{0,1},{1,0},{2,3},{3,2},{4,5},{5,4},{6,7},{7,6},{8,9},{9,8},{10,11... | collective-permute-start | bytes 1474568 | tf_op jit(solution)/shard_map/ppermute | solution.py:625
  111.6 1.9 collective-permute-start.6
  126.6 2.1 collective-permute-start.10
  126.8 4.5 %collective-permute-start.16 = (bf16[384,640]{1,0:T(8,128)(2,1)}, bf16[384,640]{1,0:T(8,128)(2,1)S(1)}, u32[]{:S(2)}, u32[]{:S(2)}) collective-permute-start(bf16[384,640]{1,0:T(8,128)(2,1)} %get-tuple-element.96), channel_id=1, source_target_pairs={{0,1},{1,0},{2,3},{3,2},{4,5},{5,4},{6,7},{7,6},{8,9},{9,8},{10,11... | collective-permute-start | bytes 1474568 | tf_op jit(solution)/shard_map/ppermute | solution.py:625
  127.1 33.9 %collective-permute-start.15 = (bf16[384,640]{1,0:T(8,128)(2,1)}, bf16[384,640]{1,0:T(8,128)(2,1)}, u32[]{:S(2)}, u32[]{:S(2)}) collective-permute-start(bf16[384,640]{1,0:T(8,128)(2,1)} %get-tuple-element.94), channel_id=1, source_target_pairs={{0,1},{1,0},{2,3},{3,2},{4,5},{5,4},{6,7},{7,6},{8,9},{9,8},{10,11... | collective-permute-start | bytes 1474568 | tf_op jit(solution)/shard_map/ppermute | solution.py:625
  127.3 19.1 %collective-permute-start.9 = (bf16[384,640]{1,0:T(8,128)(2,1)S(1)}, bf16[384,640]{1,0:T(8,128)(2,1)S(1)}, u32[]{:S(2)}, u32[]{:S(2)}) collective-permute-start(bf16[384,640]{1,0:T(8,128)(2,1)S(1)} %copy-done.24), channel_id=1, source_target_pairs={{0,1},{1,0},{2,3},{3,2},{4,5},{5,4},{6,7},{7,6},{8,9},{9,8},{10,11... | collective-permute-start | bytes 1474568 | tf_op jit(solution)/shard_map/ppermute | solution.py:625
  129.8 16.6 %collective-permute-start.11 = (bf16[384,640]{1,0:T(8,128)(2,1)S(1)}, bf16[384,640]{1,0:T(8,128)(2,1)S(1)}, u32[]{:S(2)}, u32[]{:S(2)}) collective-permute-start(bf16[384,640]{1,0:T(8,128)(2,1)S(1)} %add_convert_fusion.3), channel_id=1, source_target_pairs={{0,2},{2,0},{1,3},{3,1},{4,6},{6,4},{5,7},{7,5},{8,10},{10,8},{9,1... | collective-permute-start | bytes 1474568 | tf_op jit(solution)/shard_map/ppermute | solution.py:625
  133.3 27.7 %collective-permute-start.17 = (bf16[384,640]{1,0:T(8,128)(2,1)}, bf16[384,640]{1,0:T(8,128)(2,1)}, u32[]{:S(2)}, u32[]{:S(2)}) collective-permute-start(bf16[384,640]{1,0:T(8,128)(2,1)} %add_convert_fusion.2), channel_id=1, source_target_pairs={{0,2},{2,0},{1,3},{3,1},{4,6},{6,4},{5,7},{7,5},{8,10},{10,8},{9,1... | collective-permute-start | bytes 1474568 | tf_op jit(solution)/shard_map/ppermute | solution.py:625
  153.0 10.3 %collective-permute-start.12 = (bf16[160,384]{1,0:T(8,128)(2,1)}, bf16[160,384]{1,0:T(8,128)(2,1)S(1)}, u32[]{:S(2)}, u32[]{:S(2)}) collective-permute-start(bf16[160,384]{1,0:T(8,128)(2,1)} %get-tuple-element.91), channel_id=1, source_target_pairs={{0,8},{8,0},{16,24},{24,16},{1,9},{9,1},{17,25},{25,17},{2,10},{10... | collective-permute-start | bytes 368648 | tf_op jit(solution)/shard_map/ppermute | solution.py:631
  158.5 11.6 %collective-permute-start.13 = (bf16[160,384]{1,0:T(8,128)(2,1)}, bf16[160,384]{1,0:T(8,128)(2,1)S(1)}, u32[]{:S(2)}, u32[]{:S(2)}) collective-permute-start(bf16[160,384]{1,0:T(8,128)(2,1)} %get-tuple-element.92), channel_id=1, source_target_pairs={{0,16},{8,24},{16,0},{24,8},{1,17},{9,25},{17,1},{25,9},{2,18},{10... | collective-permute-start | bytes 368648 | tf_op jit(solution)/shard_map/ppermute | solution.py:631
  158.6 11.6 %collective-permute-start.14 = (bf16[160,384]{1,0:T(8,128)(2,1)}, bf16[160,384]{1,0:T(8,128)(2,1)}, u32[]{:S(2)}, u32[]{:S(2)}) collective-permute-start(bf16[160,384]{1,0:T(8,128)(2,1)} %get-tuple-element.93), channel_id=1, source_target_pairs={{0,24},{8,16},{16,8},{24,0},{1,25},{9,17},{17,9},{25,1},{2,26},{10... | collective-permute-start | bytes 368648 | tf_op jit(solution)/shard_map/ppermute | solution.py:631
  170.2 151.6 %reduce-scatter.2.cloned.1.call-start = ((), (), s32[]{:S(2)}) async-start(), calls=%async_computation.7 | async-start | bytes 2048000 | tf_op jit(solution)/shard_map/reduce_scatter | solution.py:719
  171.7 37.0 %collective-permute-start.18 = (bf16[640,1280]{1,0:T(8,128)(2,1)}, bf16[640,1280]{1,0:T(8,128)(2,1)S(1)}, u32[]{:S(2)}, u32[]{:S(2)}) collective-permute-start(bf16[640,1280]{1,0:T(8,128)(2,1)} %get-tuple-element.149), channel_id=1, source_target_pairs={{0,4},{4,0},{1,5},{5,1},{2,6},{6,2},{3,7},{7,3},{8,12},{12,8},{9,1... | collective-permute-start | bytes 4915208 | tf_op jit(solution)/shard_map/ppermute | solution.py:625
  210.3 113.5 %all-gather.11.cloned.1.call-start = ((), (), s32[]{:S(2)}) async-start(), calls=%async_computation.6 | async-start | bytes 2457600 | tf_op jit(solution)/shard_map/all_gather | solution.py:724
  210.3 26.9 %collective-permute-start.19 = (bf16[480,384]{1,0:T(8,128)(2,1)S(1)}, bf16[480,384]{1,0:T(8,128)(2,1)S(1)}, u32[]{:S(2)}, u32[]{:S(2)}) collective-permute-start(bf16[480,384]{1,0:T(8,128)(2,1)S(1)} %copy-done.27), channel_id=1, source_target_pairs={{0,8},{8,0},{16,24},{24,16},{1,9},{9,1},{17,25},{25,17},{2,10},{10... | collective-permute-start | bytes 1105928 | tf_op jit(solution)/shard_map/ppermute | solution.py:631
  213.7 41.3 %collective-permute-start.20 = (bf16[480,384]{1,0:T(8,128)(2,1)S(1)}, bf16[480,384]{1,0:T(8,128)(2,1)S(1)}, u32[]{:S(2)}, u32[]{:S(2)}) collective-permute-start(bf16[480,384]{1,0:T(8,128)(2,1)S(1)} %copy-done.26), channel_id=1, source_target_pairs={{0,16},{8,24},{16,0},{24,8},{1,17},{9,25},{17,1},{25,9},{2,18},{10... | collective-permute-start | bytes 1105928 | tf_op jit(solution)/shard_map/ppermute | solution.py:631
  213.7 41.3 %collective-permute-start.21 = (bf16[480,384]{1,0:T(8,128)(2,1)S(1)}, bf16[480,384]{1,0:T(8,128)(2,1)S(1)}, u32[]{:S(2)}, u32[]{:S(2)}) collective-permute-start(bf16[480,384]{1,0:T(8,128)(2,1)S(1)} %copy-done.25), channel_id=1, source_target_pairs={{0,24},{8,16},{16,8},{24,0},{1,25},{9,17},{17,9},{25,1},{2,26},{10... | collective-permute-start | bytes 1105928 | tf_op jit(solution)/shard_map/ppermute | solution.py:631
  285.4 31.3 %all-to-all-start.2 = ((bf16[4,80,164]{2,1,0:T(8,128)(2,1)}), bf16[4,80,164]{2,1,0:T(8,128)(2,1)S(1)}, u32[]{:S(2)}, u32[]{:S(2)}) async-start(bf16[4,80,164]{2,1,0:T(8,128)(2,1)} %pad_maximum_fusion.1), calls=%async_computation.2 | async-start | bytes 327680 | tf_op jit(solution)/shard_map/all_to_all | solution.py:637
  (25 other events, 136.1 us)
Sparse Core Ops, SparseCore 0:
  10.7 85.6 all-gather.6
  97.9 50.6 all-gather.12
  170.3 43.0 all-gather.8
  216.1 55.3 reduce-scatter.1
  272.9 49.9 all-gather.10

commit v5 on v4

--- a/solution.py
+++ b/solution.py
@@ -387,18 +387,17 @@
         y_ref[...] = jnp.zeros_like(y_ref)
         dx_ref[...] = jnp.zeros_like(dx_ref)
 
-    w_in = w_ref.at[:, :hidden]
-    w_down = w_ref.at[:, hidden:]
-    u = dot(xn_ref[spot, :], w_in[...])
-    dg = dot(dy_ref[spot, :], w_down[...])
+    w_in, w_down = (w_ref[:, part].reshape(xn_ref.shape[1], hidden) for part in range(2))
+    u = dot(xn_ref[spot, :], w_in)
+    dg = dot(dy_ref[spot, :], w_down)
     half = 0.5 + 0.5 * lax.erf(u * 0.7071067811865476)
     slope = half + u * (jnp.exp2(u * u * (-0.5 * LOG2E)) * 0.3989422804014327)
     g = (u * half).astype(BF16)
     du = (dg * slope).astype(BF16)
     g_ref[...] = g
     du_ref[...] = du
-    y_ref[spot, :] += dot_nt(g, w_down[...])
-    dx_ref[spot, :] += dot_nt(du, w_in[...])
+    y_ref[spot, :] += dot_nt(g, w_down)
+    dx_ref[spot, :] += dot_nt(du, w_in)
 
     @pl.when((item == pl.num_programs(0) - 1) & (side == 1))
     def _():
@@ -411,14 +410,15 @@
 def ffn(xn, dy, weights):
     mine, dim = xn[0].shape
     count = 2 * mine
-    blocks = weights.shape[0] // dim
-    hidden = weights.shape[1] // 2
+    _, _, tall, hidden = weights.shape
+    depth = dim // tall
+    blocks = weights.shape[0] // depth
     whole = pl.BlockSpec((mine, dim), lambda i, j: (0, 0))
     act = pl.BlockSpec((mine, hidden), lambda i, j: (j, i))
     return pl.pallas_call(
         ffn_kernel,
         grid=(blocks, 2),
-        in_specs=[whole] * 4 + [pl.BlockSpec((dim, 2 * hidden), lambda i, j: (i, 0))],
+        in_specs=[whole] * 4 + [pl.BlockSpec((depth, 2, tall, hidden), lambda i, j: (i, 0, 0, 0))],
         out_specs=[whole] * 4 + [act] * 2,
         out_shape=[jax.ShapeDtypeStruct((mine, dim), BF16)] * 4
         + [jax.ShapeDtypeStruct((count, blocks * hidden), BF16)] * 2,
@@ -663,13 +663,11 @@
         WIDE,
         axis=0,
     )
-    weights = lax.all_gather(
-        jnp.concatenate([w_ffn_in, w_ffn_down], axis=1), ("far", "narrow"), axis=0, tiled=True
-    )
+    weights = lax.all_gather(jnp.stack([w_ffn_in, w_ffn_down]), ("far", "narrow"), axis=0)
     group = max(1, dim // cols)
-    shape = (-1, group, dim, 2, cols)
     if group > 1:
-        weights = weights.reshape(shape).transpose(0, 2, 3, 1, 4).reshape(-1, 2 * group * cols)
+        weights = weights.reshape((-1, group, depth) + weights.shape[1:])
+        weights = weights.transpose(0, 2, 3, 4, 1, 5).reshape(-1, 2, dim // depth, group * cols)
     rows = lax.dynamic_slice_in_dim(tokens, layer * mine, mine, 0)
     dy = lax.dynamic_slice_in_dim(cotangent, layer * mine, mine, 0)
     dy_near = swap(dy, "near")

time: 334 us -> 334 us (level)
  no operation moved by 1% of the time
where the time goes in v5:
time: 334 us; the launch traced here: 333 us
  Pallas kernels  127 us (38%)
  waiting for transfers between devices  77.5 us (23%)
  starting transfers between devices  50.7 us (15%)
  blocking collectives  35.7 us (11%)
  local copies, waits for them, and re-layouts  17.3 us (5%)
  between operations  14.1 us (4%)
  other arithmetic  10.7 us (3%)
    ppermute x9, waiting for transfers between devices, spread(): lax.ppermute(parts[bit], 'narrow', [(i, i ^ bit) for i in range(size)])  61.9 us
    pallas_call x1, Pallas kernels, attend_back(): pl.pallas_call(partial(attend_back_kernel, first, heads, parts), in_specs...  35.3 us
    pallas_call x2, Pallas kernels, ffn(): pl.pallas_call(ffn_kernel, grid=(blocks, 2), in_specs=[whole] * 4 + [pl.B...  24.7 us
    all_to_all x2, starting transfers between devices, exchange(): return lax.all_to_all(value, axis, 0, 0, tiled=True)  24.3 us
    pallas_call x1, Pallas kernels, attend(): pl.pallas_call(partial(attend_kernel, first, heads, parts), in_specs=[pl....  22.6 us
    all_to_all x1, blocking collectives, exchange(): return lax.all_to_all(value, axis, 0, 0, tiled=True)  22.3 us
    ppermute x9, starting transfers between devices, spread(): lax.ppermute(parts[bit], 'narrow', [(i, i ^ bit) for i in range(size)])  18.2 us
    all_gather x1, blocking collectives, local(): lax.all_gather(jnp.concatenate([w_qkv.transpose(2, 0, 1).reshape(width, -...  13.3 us
  transfers between devices with their start and end apart: 29, of which 10 were waited for; matrix products, arithmetic and copies ran while one was open for 6% of the time, Pallas kernels for 38%

profile of v5, /device:TPU:0, one launch (start us, length us, event | category | flops | bytes accessed | tf_op | source)
XLA Modules:
  0.0 333.4 jit_solution(10528351717382824076)
XLA Ops:
  7.2 2.0 pad_maximum_fusion
  11.1 13.3 %all-gather = bf16[1280,320]{1,0:T(8,128)(2,1)} all-gather(bf16[160,320]{1,0:T(8,128)(2,1)S(1)} %pad_maximum_fusion.2), channel_id=2, replica_groups=mesh['narrow'=4,'far'=2,'near'=2,'core'=2] {'far','near','core'}, dimensions={0}, use_global_device_ids=true | all-gather | bytes 921600 | tf_op jit(solution)/shard_map/all_gather | solution.py:661
  24.4 8.7 %project.1 = (bf16[5,1536,32]{2,1,0:T(8,128)(2,1)}, bf16[5,1536,32]{2,1,0:T(8,128)(2,1)}, bf16[160,1536]{1,0:T(8,128)(2,1)}, bf16[160,1536]{1,0:T(8,128)(2,1)}, ...) custom-call(s32[1,16]{1,0:T(1,128)} %lens.1, ...), custom_call_target="tpu_custom_call" | custom-call | flops 1000000 | bytes 100000 | tf_op jit(solution)/shard_map/project/pallas_call | solution.py:113
  33.2 4.9 %all-to-all-start = ((bf16[4,160,640]{2,1,0:T(8,128)(2,1)}), bf16[4,160,640]{2,1,0:T(8,128)(2,1)S(1)}, u32[]{:S(2)}, u32[]{:S(2)}) async-start(bf16[4,160,640]{2,1,0:T(8,128)(2,1)} %get-tuple-element.66), calls=%async_computation | async-start | bytes 1638400 | tf_op jit(solution)/shard_map/all_to_all | solution.py:637
  40.7 22.6 %attend_0.1 = (bf16[160,384]{1,0:T(8,128)(2,1)}, bf16[160,384]{1,0:T(8,128)(2,1)}, bf16[160,384]{1,0:T(8,128)(2,1)}, bf16[160,384]{1,0:T(8,128)(2,1)}, bf16[160,1536]{1,0:T(8,128)(2,1)}, /*index=5*/f32[8,1536]{1,0:T(8,128)}) custom-call(s32[1]{0:T(128)} %bitcast.layer, s32[6,2]{1,0:T(8,128)} %get-tuple-element.67.bounds, ...), custom_call_target="tpu_custom_call" | custom-call | flops 1000000 | bytes 100000 | tf_op jit(solution)/shard_map/attend_0/pallas_call | solution.py:221
  63.2 2.0 collective-permute-start
  65.2 2.4 collective-permute-start.1
  69.5 7.1 %collective-permute-done.refs_1_ = bf16[160,384]{1,0:T(8,128)(2,1)S(1)} collective-permute-done((bf16[160,384]{1,0:T(8,128)(2,1)}, bf16[160,384]{1,0:T(8,128)(2,1)S(1)}, u32[]{:S(2)}, u32[]{:S(2)}) %collective-permute-start) | collective-permute-done | bytes 122912 | tf_op jit(solution)/shard_map/ppermute | solution.py:631
  76.6 14.9 %collective-permute-done.1.refs_2_ = bf16[160,384]{1,0:T(8,128)(2,1)S(1)} collective-permute-done((bf16[160,384]{1,0:T(8,128)(2,1)}, bf16[160,384]{1,0:T(8,128)(2,1)S(1)}, u32[]{:S(2)}, u32[]{:S(2)}) %collective-permute-start.1) | collective-permute-done | bytes 122912 | tf_op jit(solution)/shard_map/ppermute | solution.py:631
  92.6 3.7 %mix.1 = (f32[384,640]{1,0:T(8,128)}, bf16[384,640]{1,0:T(8,128)(2,1)}, bf16[4,160,384]{2,1,0:T(8,128)(2,1)}) custom-call(s32[1]{0:T(128)} %bitcast.layer, bf16[160,384]{1,0:T(8,128)(2,1)} %get-tuple-element.72.refs_0_, bf16[160,384]{1,0:T(8,128)(2,1)} %copy-done.21, bf16[160,384]{1,0:T(8,128)(2,1)} %copy-done.22, bf16[160,384]{1,0:T(8,128)(2,1)} %copy-done.23, ...), custom_call_target="tpu_custom_call" | custom-call | flops 1000000 | bytes 100000 | tf_op jit(solution)/shard_map/mix/pallas_call | solution.py:359
  99.1 12.4 %ffn.2 = (bf16[384,640]{1,0:T(8,128)(2,1)}, bf16[384,640]{1,0:T(8,128)(2,1)}, bf16[384,640]{1,0:T(8,128)(2,1)}, bf16[384,640]{1,0:T(8,128)(2,1)}, bf16[768,1280]{1,0:T(8,128)(2,1)}, /*index=5*/bf16[768,1280]{1,0:T(8,128)(2,1)}) custom-call(bf16[384,640]{1,0:T(8,128)(2,1)} %get-tuple-element.77.refs_0_, bf16[384,640]{1,0:T(8,128)(2,1)} %copy-done.9, ...), custom_call_target="tpu_custom_call" | custom-call | flops 1000000 | bytes 100000 | tf_op jit(solution)/shard_map/ffn/pallas_call | solution.py:418
  114.3 12.3 %ffn.3 = (bf16[384,640]{1,0:T(8,128)(2,1)}, bf16[384,640]{1,0:T(8,128)(2,1)}, bf16[384,640]{1,0:T(8,128)(2,1)}, bf16[384,640]{1,0:T(8,128)(2,1)}, bf16[768,1280]{1,0:T(8,128)(2,1)}, /*index=5*/bf16[768,1280]{1,0:T(8,128)(2,1)}) custom-call(bf16[384,640]{1,0:T(8,128)(2,1)} %copy-done.10, bf16[384,640]{1,0:T(8,128)(2,1)} %copy-done.12, ...), custom_call_target="tpu_custom_call" | custom-call | flops 1000000 | bytes 100000 | tf_op jit(solution)/shard_map/ffn/pallas_call | solution.py:418
  131.3 1.9 add_convert_fusion.2
  134.2 12.3 %outer.1 = bf16[2,640,1280]{2,1,0:T(8,128)(2,1)} custom-call(s32[1]{0:T(128)} %bitcast.4._, bf16[384,640]{1,0:T(8,128)(2,1)} %get-tuple-element.77.refs_0_, bf16[384,640]{1,0:T(8,128)(2,1)} %copy-done.9, bf16[384,640]{1,0:T(8,128)(2,1)} %copy-done.10, bf16[384,640]{1,0:T(8,128)(2,1)} %copy-done.12, bf16[384,640]{1,0:T(8,128)(2,1)} %copy-done.3, ...), custom_call_target="tpu_custom_call" | custom-call | flops 1000000 | bytes 100000 | tf_op jit(solution)/shard_map/outer/pallas_call | solution.py:461
  147.5 5.5 %turn.1 = (f32[384,640]{1,0:T(8,128)}, bf16[640,640]{1,0:T(8,128)(2,1)}, f32[8,640]{1,0:T(8,128)}, bf16[160,384]{1,0:T(8,128)(2,1)}, bf16[160,384]{1,0:T(8,128)(...) custom-call(s32[1]{0:T(128)} %bitcast.layer, bf16[4,160,640]{2,1,0:T(8,128)(2,1)} %copy-done.4, ...), custom_call_target="tpu_custom_call" | custom-call | flops 1000000 | bytes 100000 | tf_op jit(solution)/shard_map/turn/pallas_call | solution.py:505
  153.0 5.6 %collective-permute-start.12 = (bf16[160,384]{1,0:T(8,128)(2,1)}, bf16[160,384]{1,0:T(8,128)(2,1)S(1)}, u32[]{:S(2)}, u32[]{:S(2)}) collective-permute-start(bf16[160,384]{1,0:T(8,128)(2,1)} %get-tuple-element.91), channel_id=1, source_target_pairs={{0,8},{8,0},{16,24},{24,16},{1,9},{9,1},{17,25},{25,17},{2,10},{10... | collective-permute-start | bytes 368648 | tf_op jit(solution)/shard_map/ppermute | solution.py:631
  158.5 2.4 collective-permute-start.14
  161.0 2.2 add_convert_fusion.1
  163.2 6.9 %collective-permute-done.13.refs_2_ = bf16[160,384]{1,0:T(8,128)(2,1)S(1)} collective-permute-done((bf16[160,384]{1,0:T(8,128)(2,1)}, bf16[160,384]{1,0:T(8,128)(2,1)S(1)}, u32[]{:S(2)}, u32[]{:S(2)}) %collective-permute-start.13) | collective-permute-done | bytes 122912 | tf_op jit(solution)/shard_map/ppermute | solution.py:631
  172.6 35.3 %attend_back_0.1 = (bf16[480,384]{1,0:T(8,128)(2,1)}, bf16[480,384]{1,0:T(8,128)(2,1)}, bf16[480,384]{1,0:T(8,128)(2,1)}, bf16[480,384]{1,0:T(8,128)(2,1)}, bf16[480,1536]{1,0:T(8,128)(2,1)}) custom-call(s32[1]{0:T(128)} %bitcast.layer, s32[6,2]{1,0:T(8,128)} %get-tuple-element.67.bounds, f32[8,1536]{1,0:T(8,128)} %get-tuple-element.68.segr_ref, ...), custom_call_target="tpu_custom_call" | custom-call | flops 1000000 | bytes 100000 | tf_op jit(solution)/shard_map/attend_back_0/pallas_call | solution.py:320
  210.3 3.4 %collective-permute-start.19 = (bf16[480,384]{1,0:T(8,128)(2,1)S(1)}, bf16[480,384]{1,0:T(8,128)(2,1)S(1)}, u32[]{:S(2)}, u32[]{:S(2)}) collective-permute-start(bf16[480,384]{1,0:T(8,128)(2,1)S(1)} %copy-done.27), channel_id=1, source_target_pairs={{0,8},{8,0},{16,24},{24,16},{1,9},{9,1},{17,25},{25,17},{2,10},{10... | collective-permute-start | bytes 1105928 | tf_op jit(solution)/shard_map/ppermute | solution.py:631
  213.7 2.4 collective-permute-start.21
  216.1 5.9 %small.1 = bf16[640,1152]{1,0:T(8,128)(2,1)} custom-call(bf16[480,1536]{1,0:T(8,128)(2,1)} %get-tuple-element.106.flat_ref, bf16[1536,640]{1,0:T(8,128)(2,1)} %x_ref.3, bf16[3,160,640]{2,1,0:T(8,128)(2,1)} %get-tuple-element.107.w_ref, bf16[2,640]{1,0:T(2,128)(2,1)} %refs_7_.3, bf16[2,640]{1,0:T(2,128)(2,1)} %shift_ref.3, ...), custom_call_target="tpu_custom_call" | custom-call | flops 1000000 | bytes 100000 | tf_op jit(solution)/shard_map/small/pallas_call | solution.py:574
  222.0 15.2 %collective-permute-done.19.refs_1_ = bf16[480,384]{1,0:T(8,128)(2,1)S(1)} collective-permute-done((bf16[480,384]{1,0:T(8,128)(2,1)S(1)}, bf16[480,384]{1,0:T(8,128)(2,1)S(1)}, u32[]{:S(2)}, u32[]{:S(2)}) %collective-permute-start.19) | collective-permute-done | bytes 368672 | tf_op jit(solution)/shard_map/ppermute | solution.py:631
  237.2 17.8 %collective-permute-done.20.refs_2_ = bf16[480,384]{1,0:T(8,128)(2,1)S(1)} collective-permute-done((bf16[480,384]{1,0:T(8,128)(2,1)S(1)}, bf16[480,384]{1,0:T(8,128)(2,1)S(1)}, u32[]{:S(2)}, u32[]{:S(2)}) %collective-permute-start.20) | collective-permute-done | bytes 368672 | tf_op jit(solution)/shard_map/ppermute | solution.py:631
  255.8 5.8 %finish.1 = bf16[384,640]{1,0:T(8,128)(2,1)} custom-call(s32[1]{0:T(128)} %bitcast.layer, bf16[480,384]{1,0:T(8,128)(2,1)} %get-tuple-element.114.refs_0_, bf16[480,384]{1,0:T(8,128)(2,1)} %copy-done.16, bf16[480,384]{1,0:T(8,128)(2,1)} %copy-done.17, bf16[480,384]{1,0:T(8,128)(2,1)} %copy-done.18, bf16[4,3,160,640]{3,2,1,0:T(8,128)(2,1)} %bitcast.27, ...), custom_call_target="tpu_custom_call" | custom-call | flops 1000000 | bytes 100000 | tf_op jit(solution)/shard_map/finish/pallas_call | solution.py:538
  261.7 22.3 %all_to_all.15 = bf16[8,80,1152]{2,1,0:T(8,128)(2,1)S(1)} all-to-all(bf16[8,80,1152]{2,1,0:T(8,128)(2,1)S(1)} %bitcast.25), channel_id=1, replica_groups=mesh['narrow'=4,'far'=2,'near'=2,'core'=2] {'far','near','core'}, dimensions={0} | all-to-all | bytes 2949120 | tf_op jit(solution)/shard_map/all_to_all | solution.py:637
  285.3 19.4 %all-to-all-start.2 = ((bf16[4,80,164]{2,1,0:T(8,128)(2,1)}), bf16[4,80,164]{2,1,0:T(8,128)(2,1)S(1)}, u32[]{:S(2)}, u32[]{:S(2)}) async-start(bf16[4,80,164]{2,1,0:T(8,128)(2,1)} %pad_maximum_fusion.1), calls=%async_computation.2 | async-start | bytes 327680 | tf_op jit(solution)/shard_map/all_to_all | solution.py:637
  305.8 10.9 %all-to-all-done.2 = bf16[4,80,164]{2,1,0:T(8,128)(2,1)S(1)} async-done(((bf16[4,80,164]{2,1,0:T(8,128)(2,1)}), bf16[4,80,164]{2,1,0:T(8,128)(2,1)S(1)}, u32[]{:S(2)}, u32[]{:S(2)}) %all-to-all-start.2) | async-done | bytes 104992 | tf_op jit(solution)/shard_map/all_to_all | solution.py:637
  318.8 3.0 keep.1
  321.8 2.0 fusion
  323.7 3.1 copy.34
  (128 shorter events, 29.7 us)
Async XLA Ops:
  7.2 31.9 %copy-start = (bf16[1536,640]{1,0:T(8,128)(2,1)S(1)}, bf16[1536,640]{1,0:T(8,128)(2,1)}, u32[]{:S(2)}) copy-start(bf16[1536,640]{1,0:T(8,128)(2,1)} %param.10) | copy-start | bytes 5898244
  7.2 91.2 %all-gather.12.cloned.1.call-start = ((), (), s32[]{:S(2)}) async-start(), calls=%async_computation.7 | async-start | bytes 3686400 | tf_op jit(solution)/shard_map/all_gather | solution.py:666
  33.2 58.4 %all-to-all-start = ((bf16[4,160,640]{2,1,0:T(8,128)(2,1)}), bf16[4,160,640]{2,1,0:T(8,128)(2,1)S(1)}, u32[]{:S(2)}, u32[]{:S(2)}) async-start(bf16[4,160,640]{2,1,0:T(8,128)(2,1)} %get-tuple-element.66), calls=%async_computation | async-start | bytes 1638400 | tf_op jit(solution)/shard_map/all_to_all | solution.py:637
  38.1 184.0 %all-gather.14.cloned.1.call-start = ((), (), s32[]{:S(2)}) async-start(), calls=%async_computation.8 | async-start | bytes 3072000 | tf_op jit(solution)/shard_map/all_gather | solution.py:685
  38.8 280.0 %all-gather.8.cloned.1.call-start = ((), (), s32[]{:S(2)}) async-start(), calls=%async_computation.4 | async-start | bytes 2457600 | tf_op jit(solution)/shard_map/all_gather | solution.py:706
  39.1 30.4 %copy-start.3 = (bf16[384,640]{1,0:T(8,128)(2,1)}, bf16[384,640]{1,0:T(8,128)(2,1)S(1)}, u32[]{:S(2)}) copy-start(bf16[384,640]{1,0:T(8,128)(2,1)S(1)} %constant_dynamic-slice_fusion.refs_2_.refs_4_) | copy-start | bytes 1474564
  39.1 58.9 %collective-permute-start.5 = (bf16[384,640]{1,0:T(8,128)(2,1)S(1)}, bf16[384,640]{1,0:T(8,128)(2,1)S(1)}, u32[]{:S(2)}, u32[]{:S(2)}) collective-permute-start(bf16[384,640]{1,0:T(8,128)(2,1)S(1)} %constant_dynamic-slice_fusion.refs_2_.refs_4_), channel_id=1, source_target_pairs={{0,1},{1,0},{2,3},{3,2},{4,5},{5,4},{6,7},{7,6},{8,9},{9,8},{10,11... | collective-permute-start | bytes 1474568 | tf_op jit(solution)/shard_map/ppermute | solution.py:625
  39.2 58.5 %collective-permute-start.7 = (bf16[384,640]{1,0:T(8,128)(2,1)S(1)}, bf16[384,640]{1,0:T(8,128)(2,1)S(1)}, u32[]{:S(2)}, u32[]{:S(2)}) collective-permute-start(bf16[384,640]{1,0:T(8,128)(2,1)S(1)} %constant_dynamic-slice_fusion.refs_2_.refs_4_), channel_id=1, source_target_pairs={{0,2},{2,0},{1,3},{3,1},{4,6},{6,4},{5,7},{7,5},{8,10},{10,8},{9,1... | collective-permute-start | bytes 1474568 | tf_op jit(solution)/shard_map/ppermute | solution.py:625
  63.2 13.4 %collective-permute-start = (bf16[160,384]{1,0:T(8,128)(2,1)}, bf16[160,384]{1,0:T(8,128)(2,1)S(1)}, u32[]{:S(2)}, u32[]{:S(2)}) collective-permute-start(bf16[160,384]{1,0:T(8,128)(2,1)} %get-tuple-element.73), channel_id=1, source_target_pairs={{0,8},{8,0},{16,24},{24,16},{1,9},{9,1},{17,25},{25,17},{2,10},{10... | collective-permute-start | bytes 368648 | tf_op jit(solution)/shard_map/ppermute | solution.py:631
  65.2 26.3 %collective-permute-start.1 = (bf16[160,384]{1,0:T(8,128)(2,1)}, bf16[160,384]{1,0:T(8,128)(2,1)S(1)}, u32[]{:S(2)}, u32[]{:S(2)}) collective-permute-start(bf16[160,384]{1,0:T(8,128)(2,1)} %get-tuple-element.74), channel_id=1, source_target_pairs={{0,16},{8,24},{16,0},{24,8},{1,17},{9,25},{17,1},{25,9},{2,18},{10... | collective-permute-start | bytes 368648 | tf_op jit(solution)/shard_map/ppermute | solution.py:631
  67.6 23.9 %collective-permute-start.2 = (bf16[160,384]{1,0:T(8,128)(2,1)}, bf16[160,384]{1,0:T(8,128)(2,1)S(1)}, u32[]{:S(2)}, u32[]{:S(2)}) collective-permute-start(bf16[160,384]{1,0:T(8,128)(2,1)} %get-tuple-element.75), channel_id=1, source_target_pairs={{0,24},{8,16},{16,8},{24,0},{1,25},{9,17},{17,9},{25,1},{2,26},{10... | collective-permute-start | bytes 368648 | tf_op jit(solution)/shard_map/ppermute | solution.py:631
  96.3 2.1 collective-permute-start.3
  96.3 15.3 %collective-permute-start.4 = (bf16[384,640]{1,0:T(8,128)(2,1)}, bf16[384,640]{1,0:T(8,128)(2,1)S(1)}, u32[]{:S(2)}, u32[]{:S(2)}) collective-permute-start(bf16[384,640]{1,0:T(8,128)(2,1)} %get-tuple-element.77.refs_0_), channel_id=1, source_target_pairs={{0,2},{2,0},{1,3},{3,1},{4,6},{6,4},{5,7},{7,5},{8,10},{10,8},{9,1... | collective-permute-start | bytes 1474568 | tf_op jit(solution)/shard_map/ppermute | solution.py:625
  97.8 14.0 %collective-permute-start.8 = (bf16[384,640]{1,0:T(8,128)(2,1)S(1)}, bf16[384,640]{1,0:T(8,128)(2,1)S(1)}, u32[]{:S(2)}, u32[]{:S(2)}) collective-permute-start(bf16[384,640]{1,0:T(8,128)(2,1)S(1)} %collective-permute-done.7.refs_2_.refs_6_), channel_id=1, source_target_pairs={{0,1},{1,0},{2,3},{3,2},{4,5},{5,4},{6,7},{7,6},{8,9},{9,8},{10,11... | collective-permute-start | bytes 1474568 | tf_op jit(solution)/shard_map/ppermute | solution.py:625
  111.6 1.9 collective-permute-start.6
  126.6 2.1 collective-permute-start.10
  126.8 4.6 %collective-permute-start.16 = (bf16[384,640]{1,0:T(8,128)(2,1)}, bf16[384,640]{1,0:T(8,128)(2,1)S(1)}, u32[]{:S(2)}, u32[]{:S(2)}) collective-permute-start(bf16[384,640]{1,0:T(8,128)(2,1)} %get-tuple-element.96), channel_id=1, source_target_pairs={{0,1},{1,0},{2,3},{3,2},{4,5},{5,4},{6,7},{7,6},{8,9},{9,8},{10,11... | collective-permute-start | bytes 1474568 | tf_op jit(solution)/shard_map/ppermute | solution.py:625
  127.1 33.9 %collective-permute-start.15 = (bf16[384,640]{1,0:T(8,128)(2,1)}, bf16[384,640]{1,0:T(8,128)(2,1)}, u32[]{:S(2)}, u32[]{:S(2)}) collective-permute-start(bf16[384,640]{1,0:T(8,128)(2,1)} %get-tuple-element.94), channel_id=1, source_target_pairs={{0,1},{1,0},{2,3},{3,2},{4,5},{5,4},{6,7},{7,6},{8,9},{9,8},{10,11... | collective-permute-start | bytes 1474568 | tf_op jit(solution)/shard_map/ppermute | solution.py:625
  127.3 19.2 %collective-permute-start.9 = (bf16[384,640]{1,0:T(8,128)(2,1)S(1)}, bf16[384,640]{1,0:T(8,128)(2,1)S(1)}, u32[]{:S(2)}, u32[]{:S(2)}) collective-permute-start(bf16[384,640]{1,0:T(8,128)(2,1)S(1)} %copy-done.24), channel_id=1, source_target_pairs={{0,1},{1,0},{2,3},{3,2},{4,5},{5,4},{6,7},{7,6},{8,9},{9,8},{10,11... | collective-permute-start | bytes 1474568 | tf_op jit(solution)/shard_map/ppermute | solution.py:625
  129.8 16.7 %collective-permute-start.11 = (bf16[384,640]{1,0:T(8,128)(2,1)S(1)}, bf16[384,640]{1,0:T(8,128)(2,1)S(1)}, u32[]{:S(2)}, u32[]{:S(2)}) collective-permute-start(bf16[384,640]{1,0:T(8,128)(2,1)S(1)} %add_convert_fusion.3), channel_id=1, source_target_pairs={{0,2},{2,0},{1,3},{3,1},{4,6},{6,4},{5,7},{7,5},{8,10},{10,8},{9,1... | collective-permute-start | bytes 1474568 | tf_op jit(solution)/shard_map/ppermute | solution.py:625
  133.3 27.7 %collective-permute-start.17 = (bf16[384,640]{1,0:T(8,128)(2,1)}, bf16[384,640]{1,0:T(8,128)(2,1)}, u32[]{:S(2)}, u32[]{:S(2)}) collective-permute-start(bf16[384,640]{1,0:T(8,128)(2,1)} %add_convert_fusion.2), channel_id=1, source_target_pairs={{0,2},{2,0},{1,3},{3,1},{4,6},{6,4},{5,7},{7,5},{8,10},{10,8},{9,1... | collective-permute-start | bytes 1474568 | tf_op jit(solution)/shard_map/ppermute | solution.py:625
  153.0 10.2 %collective-permute-start.12 = (bf16[160,384]{1,0:T(8,128)(2,1)}, bf16[160,384]{1,0:T(8,128)(2,1)S(1)}, u32[]{:S(2)}, u32[]{:S(2)}) collective-permute-start(bf16[160,384]{1,0:T(8,128)(2,1)} %get-tuple-element.91), channel_id=1, source_target_pairs={{0,8},{8,0},{16,24},{24,16},{1,9},{9,1},{17,25},{25,17},{2,10},{10... | collective-permute-start | bytes 368648 | tf_op jit(solution)/shard_map/ppermute | solution.py:631
  158.5 11.6 %collective-permute-start.13 = (bf16[160,384]{1,0:T(8,128)(2,1)}, bf16[160,384]{1,0:T(8,128)(2,1)S(1)}, u32[]{:S(2)}, u32[]{:S(2)}) collective-permute-start(bf16[160,384]{1,0:T(8,128)(2,1)} %get-tuple-element.92), channel_id=1, source_target_pairs={{0,16},{8,24},{16,0},{24,8},{1,17},{9,25},{17,1},{25,9},{2,18},{10... | collective-permute-start | bytes 368648 | tf_op jit(solution)/shard_map/ppermute | solution.py:631
  158.5 11.6 %collective-permute-start.14 = (bf16[160,384]{1,0:T(8,128)(2,1)}, bf16[160,384]{1,0:T(8,128)(2,1)}, u32[]{:S(2)}, u32[]{:S(2)}) collective-permute-start(bf16[160,384]{1,0:T(8,128)(2,1)} %get-tuple-element.93), channel_id=1, source_target_pairs={{0,24},{8,16},{16,8},{24,0},{1,25},{9,17},{17,9},{25,1},{2,26},{10... | collective-permute-start | bytes 368648 | tf_op jit(solution)/shard_map/ppermute | solution.py:631
  170.2 151.6 %reduce-scatter.2.cloned.1.call-start = ((), (), s32[]{:S(2)}) async-start(), calls=%async_computation.6 | async-start | bytes 2048000 | tf_op jit(solution)/shard_map/reduce_scatter | solution.py:717
  171.7 37.0 %collective-permute-start.18 = (bf16[640,1280]{1,0:T(8,128)(2,1)}, bf16[640,1280]{1,0:T(8,128)(2,1)S(1)}, u32[]{:S(2)}, u32[]{:S(2)}) collective-permute-start(bf16[640,1280]{1,0:T(8,128)(2,1)} %get-tuple-element.149), channel_id=1, source_target_pairs={{0,4},{4,0},{1,5},{5,1},{2,6},{6,2},{3,7},{7,3},{8,12},{12,8},{9,1... | collective-permute-start | bytes 4915208 | tf_op jit(solution)/shard_map/ppermute | solution.py:625
  210.2 113.5 %all-gather.10.cloned.1.call-start = ((), (), s32[]{:S(2)}) async-start(), calls=%async_computation.5 | async-start | bytes 2457600 | tf_op jit(solution)/shard_map/all_gather | solution.py:722
  210.3 26.9 %collective-permute-start.19 = (bf16[480,384]{1,0:T(8,128)(2,1)S(1)}, bf16[480,384]{1,0:T(8,128)(2,1)S(1)}, u32[]{:S(2)}, u32[]{:S(2)}) collective-permute-start(bf16[480,384]{1,0:T(8,128)(2,1)S(1)} %copy-done.27), channel_id=1, source_target_pairs={{0,8},{8,0},{16,24},{24,16},{1,9},{9,1},{17,25},{25,17},{2,10},{10... | collective-permute-start | bytes 1105928 | tf_op jit(solution)/shard_map/ppermute | solution.py:631
  213.7 41.3 %collective-permute-start.20 = (bf16[480,384]{1,0:T(8,128)(2,1)S(1)}, bf16[480,384]{1,0:T(8,128)(2,1)S(1)}, u32[]{:S(2)}, u32[]{:S(2)}) collective-permute-start(bf16[480,384]{1,0:T(8,128)(2,1)S(1)} %copy-done.26), channel_id=1, source_target_pairs={{0,16},{8,24},{16,0},{24,8},{1,17},{9,25},{17,1},{25,9},{2,18},{10... | collective-permute-start | bytes 1105928 | tf_op jit(solution)/shard_map/ppermute | solution.py:631
  213.7 41.3 %collective-permute-start.21 = (bf16[480,384]{1,0:T(8,128)(2,1)S(1)}, bf16[480,384]{1,0:T(8,128)(2,1)S(1)}, u32[]{:S(2)}, u32[]{:S(2)}) collective-permute-start(bf16[480,384]{1,0:T(8,128)(2,1)S(1)} %copy-done.25), channel_id=1, source_target_pairs={{0,24},{8,16},{16,8},{24,0},{1,25},{9,17},{17,9},{25,1},{2,26},{10... | collective-permute-start | bytes 1105928 | tf_op jit(solution)/shard_map/ppermute | solution.py:631
  237.2 17.8 %copy-start.16 = (bf16[480,384]{1,0:T(8,128)(2,1)}, bf16[480,384]{1,0:T(8,128)(2,1)S(1)}, u32[]{:S(2)}) copy-start(bf16[480,384]{1,0:T(8,128)(2,1)S(1)} %collective-permute-done.19.refs_1_) | copy-start | bytes 1105924
  285.3 31.3 %all-to-all-start.2 = ((bf16[4,80,164]{2,1,0:T(8,128)(2,1)}), bf16[4,80,164]{2,1,0:T(8,128)(2,1)S(1)}, u32[]{:S(2)}, u32[]{:S(2)}) async-start(bf16[4,80,164]{2,1,0:T(8,128)(2,1)} %pad_maximum_fusion.1), calls=%async_computation.2 | async-start | bytes 327680 | tf_op jit(solution)/shard_map/all_to_all | solution.py:637
  (25 other events, 133.1 us)
Sparse Core Ops, SparseCore 0:
  10.7 85.6 all-gather.11
  97.9 50.6 all-gather.13
  170.3 43.0 all-gather.7
  216.1 55.3 reduce-scatter.1
  272.9 49.9 all-gather.9
